TPU v7x, 32 devices: a whole 2x2x4 slice. The times are simulated.
32 devices in a mesh: groups: 2 (over x), expert: 16 (over z, y, core).
Axes of the slice: x: 2, y: 2, z: 4, core: 2. Of those that a mesh axis runs over, the one named last changes fastest.
Arguments:
- out_grad: bfloat16 [4096, 2560], P(('groups', 'expert')), parts along dimension 0, may hold values from -6 to 6
- saved_hidden: bfloat16 [4096, 6, 768], P(('groups', 'expert')), parts along dimension 0, may hold values from -0.21875 to 0.21875
- expert_ids: int32 [4096, 6], P(('groups', 'expert')), parts along dimension 0, may hold values from 0 to 15, as said below
- gate_weights: bfloat16 [4096, 6], P(('groups', 'expert')), parts along dimension 0, may hold values from 0.049804688 to 0.5
- trained: int32 [32], P(('groups', 'expert')), parts along dimension 0, may hold values 0 or 1
- down_weight: bfloat16 [16, 768, 2560], P('expert'), may hold values from -0.125 to 0.125
Outputs:
- hidden_grad: bfloat16 [4096, 6, 768], P(('groups', 'expert')), parts along dimension 0
- gate_grad: bfloat16 [4096, 6], P(('groups', 'expert')), parts along dimension 0
- weight_grad: bfloat16 [32, 768, 2560], P(('groups', 'expert')), parts along dimension 0
There are 2 independent parts, one for each index of `groups`. A program takes and returns all parts, laid end to end along the dimension named above; an argument that names none is the same for every part. Nothing has to cross between parts.
Inputs may be any that keep to these rules, and one draw needn't show every extreme that they name: `expert_ids`: each row names 6 different experts. The rows of one device name any one expert at most 72 times, and some expert is named exactly 72 times by the rows of every device.
All inputs are finite; a program needn't handle non-finite values. No bound on the sum of `trained` on one device may be relied on, other than what follows from the above.
Results may differ from a plain program's by a relative error of at most 0.0085.
Values may be sent and summed in bfloat16 or wider, within the bound.
No kernel may reach another device: no remote copies, remote signals or barrier semaphores. Data moves between devices by JAX's collectives and lax.ppermute only.
A program may use at most 128 MiB of HBM per device.

v0:
```python
import jax
import jax.numpy as jnp
from jax import lax
from jax.sharding import PartitionSpec as P


def local(out_grad, saved_hidden, expert_ids, gate_weights, trained, down_weight):
    experts = lax.axis_size("expert")
    tok_rows, model_width = out_grad.shape
    top_count = expert_ids.shape[1]
    hidden_units = saved_hidden.shape[2]
    capacity = min(tok_rows, 3 * tok_rows * top_count // (2 * experts))
    slot_count = tok_rows * top_count
    flat_ids = expert_ids.reshape(slot_count)
    onehot = (flat_ids[:, None] == jnp.arange(experts, dtype=jnp.int32)[None, :]).astype(jnp.int32)
    slot_rank = jnp.sum(jnp.cumsum(onehot, axis=0) * onehot, axis=1) - 1
    places = flat_ids * capacity + slot_rank
    owner_rows = jnp.arange(slot_count, dtype=jnp.int32) // top_count
    flat_hidden = saved_hidden.reshape(slot_count, hidden_units)
    flat_gates = gate_weights.reshape(slot_count)
    send_grad = (
        jnp.zeros((experts * capacity, model_width), jnp.bfloat16)
        .at[places]
        .set(out_grad[owner_rows])
    )
    send_hidden = (
        jnp.zeros((experts * capacity, hidden_units), jnp.bfloat16).at[places].set(flat_hidden)
    )
    send_gate = jnp.zeros((experts * capacity,), jnp.bfloat16).at[places].set(flat_gates)
    recv_grad, recv_hidden, recv_gate = (
        lax.all_to_all(
            send_grad.reshape(experts, capacity, model_width),
            "expert",
            split_axis=0,
            concat_axis=0,
            tiled=True,
        ),
        lax.all_to_all(
            send_hidden.reshape(experts, capacity, hidden_units),
            "expert",
            split_axis=0,
            concat_axis=0,
            tiled=True,
        ),
        lax.all_to_all(
            send_gate.reshape(experts, capacity), "expert", split_axis=0, concat_axis=0, tiled=True
        ),
    )
    rows_grad = recv_grad.reshape(experts * capacity, model_width)
    rows_hidden = recv_hidden.reshape(experts * capacity, hidden_units)
    gate_col = recv_gate.reshape(experts * capacity, 1).astype(jnp.float32)
    weight = down_weight[0]
    upstream = lax.dot_general(
        rows_grad, weight, (((1,), (1,)), ((), ())), preferred_element_type=jnp.float32
    ).astype(jnp.bfloat16)
    upstream_wide = upstream.astype(jnp.float32)
    hidden_part = (gate_col * upstream_wide).astype(jnp.bfloat16)
    gate_part = jnp.sum(rows_hidden.astype(jnp.float32) * upstream_wide, axis=1).astype(
        jnp.bfloat16
    )
    back_hidden, back_gate = (
        lax.all_to_all(
            hidden_part.reshape(experts, capacity, hidden_units),
            "expert",
            split_axis=0,
            concat_axis=0,
            tiled=True,
        ),
        lax.all_to_all(
            gate_part.reshape(experts, capacity), "expert", split_axis=0, concat_axis=0, tiled=True
        ),
    )
    hidden_grad = back_hidden.reshape(experts * capacity, hidden_units)[places].reshape(
        tok_rows, top_count, hidden_units
    )
    gate_grad = back_gate.reshape(experts * capacity)[places].reshape(tok_rows, top_count)
    scaled = (gate_col * rows_grad.astype(jnp.float32)).astype(jnp.bfloat16)
    weight_sum = lax.dot_general(
        rows_hidden, scaled, (((0,), (0,)), ((), ())), preferred_element_type=jnp.float32
    )
    weight_grad = (weight_sum * trained[0].astype(jnp.float32)).astype(jnp.bfloat16)
    return (hidden_grad, gate_grad, weight_grad[None])


def solution(mesh):
    placed = (
        P(("groups", "expert"), None),
        P(("groups", "expert"), None, None),
        P(("groups", "expert"), None),
        P(("groups", "expert"), None),
        P(("groups", "expert")),
        P("expert", None, None),
    )
    return jax.shard_map(
        local,
        mesh=mesh,
        in_specs=placed,
        out_specs=(
            P(("groups", "expert"), None, None),
            P(("groups", "expert"), None),
            P(("groups", "expert"), None, None),
        ),
        check_vma=False,
    )
```

profile of v0, /device:TPU:13, one launch (start us, length us, event | category | flops | bytes accessed | tf_op | source)
XLA Modules:
  0.0 283.6 jit_solution(11119569849924000101)
XLA Ops:
  0.6 0.0 copy-start
  0.6 0.9 copy.28
  1.5 0.1 eq.29
  1.6 0.1 eq.25
  1.8 0.7 broadcast_multiply_fusion
  2.5 1.7 reduce-window.6
  4.2 0.3 slice_reduce_fusion
  4.5 0.1 fusion.17
  4.6 0.1 copy.27
  4.7 0.1 mul.47
  4.8 0.8 copy.31
  5.7 0.1 reshape.216
  5.8 8.6 %scatter_custom_fusion = bf16[1152]{0:T(1024)(128)(2,1)S(1)} fusion(s32[768]{0:T(1024)S(1)} %fusion.19, bf16[768]{0:T(1024)(128)(2,1)S(1)} %reshape.216, bf16[]{:T(256)} %constant.9.clone.1), kind=kCustom, calls=%fused_computation.44 | custom fusion | bytes 2306 | tf_op jit(solution)/shard_map/scatter | solution.py:29
  14.5 0.7 all_to_all.25
  15.2 6.6 %all-to-all-start = ((bf16[16,1,72]{2,1,0:T(2,128)(2,1)}), bf16[16,1,72]{2,1,0:T(2,128)(2,1)S(1)}, u32[]{:S(2)}, u32[]{:S(2)}) async-start(bf16[16,1,72]{2,1,0:T(2,128)(2,1)} %all_to_all.25), calls=%async_computation | async-start | bytes 16384 | tf_op jit(solution)/shard_map/all_to_all | solution.py:45
  21.7 1.9 copy.33
  23.7 0.4 reshape.232
  24.1 7.0 %scatter_custom_fusion.2 = bf16[1152,768]{1,0:T(8,128)(2,1)} fusion(s32[768]{0:T(1024)S(1)} %fusion.19, bf16[768,768]{1,0:T(8,128)(2,1)S(1)} %reshape.232, bf16[]{:T(256)} %constant.9.clone.1), kind=kCustom, calls=%fused_computation.22 | custom fusion | bytes 1769474 | tf_op jit(solution)/shard_map/scatter | solution.py:27
  31.1 0.0 all-to-all-done
  31.1 6.0 %all-to-all-start.3 = ((bf16[16,72,768]{2,1,0:T(8,128)(2,1)}), bf16[16,72,768]{2,1,0:T(8,128)(2,1)S(1)}, u32[]{:S(2)}, u32[]{:S(2)}) async-start(bf16[16,72,768]{2,1,0:T(8,128)(2,1)} %bitcast.6), calls=%async_computation.3 | async-start | bytes 3538944 | tf_op jit(solution)/shard_map/all_to_all | solution.py:38
  37.2 0.0 copy-done
  37.2 28.2 %scatter_custom_fusion.1 = bf16[1152,2560]{1,0:T(8,128)(2,1)} fusion(s32[768]{0:T(1024)S(1)} %fusion.19, bf16[128,2560]{1,0:T(8,128)(2,1)S(1)} %copy-done, s32[1024]{0:T(1024)S(1)} %pad_clamp_fusion.1, bf16[]{:T(256)} %constant.9.clone.1), kind=kCustom, calls=%fused_computation.16 | custom fusion | bytes 5898242 | tf_op jit(solution)/shard_map/scatter | solution.py:24
  65.4 12.2 %all-to-all-done.3 = bf16[16,72,768]{2,1,0:T(8,128)(2,1)S(1)} async-done(((bf16[16,72,768]{2,1,0:T(8,128)(2,1)}), bf16[16,72,768]{2,1,0:T(8,128)(2,1)S(1)}, u32[]{:S(2)}, u32[]{:S(2)}) %all-to-all-start.3) | async-done | bytes 1769504 | tf_op jit(solution)/shard_map/all_to_all | solution.py:38
  77.5 0.0 copy-start.1
  77.5 4.9 %all-to-all-start.1 = ((bf16[16,72,2560]{2,1,0:T(8,128)(2,1)}), bf16[16,72,2560]{2,1,0:T(8,128)(2,1)}, u32[]{:S(2)}, u32[]{:S(2)}) async-start(bf16[16,72,2560]{2,1,0:T(8,128)(2,1)} %bitcast.44), calls=%async_computation.1 | async-start | bytes 11796480 | tf_op jit(solution)/shard_map/all_to_all | solution.py:31
  82.5 0.1 reshape.185
  82.6 128.9 %all-to-all-done.1 = bf16[16,72,2560]{2,1,0:T(8,128)(2,1)} async-done(((bf16[16,72,2560]{2,1,0:T(8,128)(2,1)}), bf16[16,72,2560]{2,1,0:T(8,128)(2,1)}, u32[]{:S(2)}, u32[]{:S(2)}) %all-to-all-start.1) | async-done | bytes 5898272 | tf_op jit(solution)/shard_map/all_to_all | solution.py:31
  211.4 0.0 copy-done.1
  211.4 10.0 %fusion.9 = (bf16[1152]{0:T(1024)(128)(2,1)S(1)}, bf16[1152,768]{1,0:T(8,128)(2,1)}) fusion(bf16[16,72,768]{2,1,0:T(8,128)(2,1)S(1)} %all-to-all-done.3, f32[1152]{0:T(1024)S(1)} %reshape.185, bf16[1152,2560]{1,0:T(8,128)(2,1)} %bitcast.2, bf16[1,768,2560]{2,1,0:T(8,128)(2,1)} %param.11), kind=kOutput, calls=%fused_computation.19 | convolution fusion | flops 4536040448 | bytes 13376256 | tf_op jit(solution)/shard_map/dot_general | solution.py:53
  221.4 0.1 convert_element_type.88
  221.5 8.5 %all_to_all.31 = bf16[16,1,72]{2,1,0:T(2,128)(2,1)S(1)} all-to-all(bf16[16,1,72]{2,1,0:T(2,128)(2,1)S(1)} %convert_element_type.88), channel_id=1, replica_groups=mesh['groups'=2,'expert'=16] {'expert'}, dimensions={0} | all-to-all | bytes 4608 | tf_op jit(solution)/shard_map/all_to_all | solution.py:69
  230.0 6.2 %all-to-all-start.2 = ((bf16[16,72,768]{2,1,0:T(8,128)(2,1)}), bf16[16,72,768]{2,1,0:T(8,128)(2,1)S(1)}, u32[]{:S(2)}, u32[]{:S(2)}) async-start(bf16[16,72,768]{2,1,0:T(8,128)(2,1)} %bitcast.45), calls=%async_computation.2 | async-start | bytes 3538944 | tf_op jit(solution)/shard_map/all_to_all | solution.py:62
  237.0 9.4 %fusion.3 = bf16[1,768,2560]{2,1,0:T(8,128)(2,1)} fusion(bf16[16,72,768]{2,1,0:T(8,128)(2,1)} %copy-done.1, bf16[16,72,2560]{2,1,0:T(8,128)(2,1)} %all-to-all-done.1, f32[16,72]{1,0:T(8,128)S(1)} %bitcast.47, f32[]{:T(128)} %bitcast.10), kind=kOutput, calls=%fused_computation.11 | convolution fusion | flops 4542627840 | bytes 11604484 | tf_op jit(solution)/shard_map/dot_general | solution.py:78
  246.4 0.1 reshape.183
  246.5 5.0 %gather_fusion.1 = bf16[768]{0:T(1024)(128)(2,1)S(1)} fusion(bf16[1152]{0:T(1024)(128)(2,1)S(1)} %reshape.183, s32[1024]{0:T(1024)S(1)} %pad_clamp_fusion), kind=kCustom, calls=%fused_computation.2 | custom fusion | bytes 6144 | tf_op jit(solution)/shard_map/gather | solution.py:76
  251.5 0.1 reshape.184
  251.7 0.7 copy.36
  252.3 24.3 %all-to-all-done.2 = bf16[16,72,768]{2,1,0:T(8,128)(2,1)S(1)} async-done(((bf16[16,72,768]{2,1,0:T(8,128)(2,1)}), bf16[16,72,768]{2,1,0:T(8,128)(2,1)S(1)}, u32[]{:S(2)}, u32[]{:S(2)}) %all-to-all-start.2) | async-done | bytes 1769504 | tf_op jit(solution)/shard_map/all_to_all | solution.py:62
  276.7 3.4 %gather_fusion = bf16[768,768]{1,0:T(8,128)(2,1)} fusion(bf16[1152,768]{1,0:T(8,128)(2,1)S(1)} %bitcast.43, s32[1024]{0:T(1024)S(1)} %pad_clamp_fusion), kind=kCustom, calls=%fused_computation.1 | custom fusion | bytes 2362368 | tf_op jit(solution)/shard_map/gather | solution.py:73
  280.1 2.2 reshape.180
  282.4 1.2 copy.35
  (10 shorter events, 0.2 us)
Async XLA Ops:
  0.6 36.5 %copy-start = (bf16[128,2560]{1,0:T(8,128)(2,1)S(1)}, bf16[128,2560]{1,0:T(8,128)(2,1)}, u32[]{:S(2)}) copy-start(bf16[128,2560]{1,0:T(8,128)(2,1)} %param.6) | copy-start | bytes 1966084
  15.2 15.9 %all-to-all-start = ((bf16[16,1,72]{2,1,0:T(2,128)(2,1)}), bf16[16,1,72]{2,1,0:T(2,128)(2,1)S(1)}, u32[]{:S(2)}, u32[]{:S(2)}) async-start(bf16[16,1,72]{2,1,0:T(2,128)(2,1)} %all_to_all.25), calls=%async_computation | async-start | bytes 16384 | tf_op jit(solution)/shard_map/all_to_all | solution.py:45
  31.1 46.4 %all-to-all-start.3 = ((bf16[16,72,768]{2,1,0:T(8,128)(2,1)}), bf16[16,72,768]{2,1,0:T(8,128)(2,1)S(1)}, u32[]{:S(2)}, u32[]{:S(2)}) async-start(bf16[16,72,768]{2,1,0:T(8,128)(2,1)} %bitcast.6), calls=%async_computation.3 | async-start | bytes 3538944 | tf_op jit(solution)/shard_map/all_to_all | solution.py:38
  77.5 133.9 %copy-start.1 = (bf16[16,72,768]{2,1,0:T(8,128)(2,1)}, bf16[16,72,768]{2,1,0:T(8,128)(2,1)S(1)}, u32[]{:S(2)}) copy-start(bf16[16,72,768]{2,1,0:T(8,128)(2,1)S(1)} %all-to-all-done.3) | copy-start | bytes 5308420
  77.5 133.9 %all-to-all-start.1 = ((bf16[16,72,2560]{2,1,0:T(8,128)(2,1)}), bf16[16,72,2560]{2,1,0:T(8,128)(2,1)}, u32[]{:S(2)}, u32[]{:S(2)}) async-start(bf16[16,72,2560]{2,1,0:T(8,128)(2,1)} %bitcast.44), calls=%async_computation.1 | async-start | bytes 11796480 | tf_op jit(solution)/shard_map/all_to_all | solution.py:31
  230.0 46.7 %all-to-all-start.2 = ((bf16[16,72,768]{2,1,0:T(8,128)(2,1)}), bf16[16,72,768]{2,1,0:T(8,128)(2,1)S(1)}, u32[]{:S(2)}, u32[]{:S(2)}) async-start(bf16[16,72,768]{2,1,0:T(8,128)(2,1)} %bitcast.45), calls=%async_computation.2 | async-start | bytes 3538944 | tf_op jit(solution)/shard_map/all_to_all | solution.py:62
where the time goes:
time: 284 us
  waiting for transfers between devices  165 us (58%)
  local copies, waits for them, and re-layouts  62.5 us (22%)
  starting transfers between devices  23.7 us (8%)
  matrix products  19.4 us (7%)
  blocking collectives  8.5 us (3%)
    all_to_all x1, waiting for transfers between devices, local(): lax.all_to_all(send_grad.reshape(experts, capacity, model_width), 'expert...  129 us
    scatter x1, local copies, waits for them, and re-layouts, local(): send_grad = jnp.zeros((experts * capacity, model_width), jnp.bfloat16).at...  28.2 us
    all_to_all x1, waiting for transfers between devices, local(): lax.all_to_all(hidden_part.reshape(experts, capacity, hidden_units), 'exp...  24.3 us
    all_to_all x1, waiting for transfers between devices, local(): lax.all_to_all(send_hidden.reshape(experts, capacity, hidden_units), 'exp...  12.2 us
    dot_general x1, matrix products, local(): lax.dot_general(rows_grad, weight, (((1,), (1,)), ((), ())), preferred_el...  10 us
    dot_general x1, matrix products, local(): lax.dot_general(rows_hidden, scaled, (((0,), (0,)), ((), ())), preferred_...  9.43 us
    scatter x1, local copies, waits for them, and re-layouts, local(): jnp.zeros((experts * capacity,), jnp.bfloat16).at[places].set(flat_gates)  8.62 us
    all_to_all x1, blocking collectives, local(): lax.all_to_all(gate_part.reshape(experts, capacity), 'expert', split_axis...  8.5 us
  transfers between devices with their start and end apart: 4, of which 3 were waited for; matrix products, arithmetic and copies ran while one was open for 19% of the time, Pallas kernels for 0%

commit v1 on v0

v1 whole, which is shorter than its diff:
```python
import functools

import jax
import jax.numpy as jnp
from jax import lax
from jax.experimental import pallas as pl
from jax.experimental.pallas import tpu as pltpu
from jax.sharding import PartitionSpec as P

F32, BF16, I32 = jnp.float32, jnp.bfloat16, jnp.int32
VMEM_LIMIT = 48 * 1024 * 1024


def whole(memory_space=pltpu.VMEM):
    return pl.BlockSpec(memory_space=memory_space)


def earlier(tokens):
    row = lax.broadcasted_iota(I32, (tokens, tokens), 0)
    column = lax.broadcasted_iota(I32, (tokens, tokens), 1)
    return (row < column).astype(F32).astype(BF16)


def pack_kernel(experts, capacity, ids_ref, gates_ref, hidden_ref, out_ref, place_ref, table, select):
    top_count, tokens = ids_ref.shape
    expert = lax.broadcasted_iota(I32, (experts, tokens), 0)
    named = jnp.zeros((experts, tokens), F32)
    for k in range(top_count):
        named = named + (ids_ref[k : k + 1, :] == expert).astype(F32)
    rank = jnp.dot(named.astype(BF16), earlier(tokens), preferred_element_type=F32).astype(I32)
    target = expert * capacity + rank
    for k in range(top_count):
        place_ref[k : k + 1, :] = jnp.sum(
            jnp.where(ids_ref[k : k + 1, :] == expert, target, 0), axis=0, keepdims=True
        )
        table[k * tokens : (k + 1) * tokens, :] = hidden_ref[:, k, :]
    rows = out_ref.shape[0]
    step = 128
    for first in range(0, rows, step):
        row = lax.broadcasted_iota(I32, (step, tokens), 0) + first
        for k in range(top_count):
            select[:, k * tokens : (k + 1) * tokens] = jnp.where(
                place_ref[k : k + 1, :] == row, gates_ref[k : k + 1, :].astype(F32), 0.0
            ).astype(BF16)
        out_ref[first : first + step, :] = jnp.dot(
            select[...], table[...], preferred_element_type=F32
        ).astype(BF16)


def pack(ids_t, gates_t, saved_hidden, experts, capacity):
    tokens, top_count, hidden_units = saved_hidden.shape
    return pl.pallas_call(
        functools.partial(pack_kernel, experts, capacity),
        out_shape=(
            jax.ShapeDtypeStruct((experts * capacity, hidden_units), BF16),
            jax.ShapeDtypeStruct((top_count, tokens), I32),
        ),
        in_specs=[whole()] * 3,
        out_specs=(whole(), whole()),
        scratch_shapes=[
            pltpu.VMEM((top_count * tokens, hidden_units), BF16),
            pltpu.VMEM((128, top_count * tokens), BF16),
        ],
        compiler_params=pltpu.CompilerParams(vmem_limit_bytes=VMEM_LIMIT),
        name="pack",
    )(ids_t, gates_t, saved_hidden)


def source_rank(ids, expert, tokens):
    named = jnp.max((ids == expert).astype(F32), axis=0, keepdims=True)
    rank = jnp.dot(named.astype(BF16), earlier(tokens), preferred_element_type=F32)
    return jnp.where(named > 0.5, rank.astype(I32), -1)


def upstream_kernel(capacity, expert_ref, ids_ref, grad_ref, weight_ref, out_ref):
    tokens = grad_ref.shape[0]
    dense = lax.dot_general(
        grad_ref[...], weight_ref[...], (((1,), (1,)), ((), ())), preferred_element_type=F32
    ).astype(BF16)
    rank = source_rank(ids_ref[0], expert_ref[0], tokens)
    choose = (rank == lax.broadcasted_iota(I32, (capacity, tokens), 0)).astype(F32).astype(BF16)
    out_ref[0] = jnp.dot(choose, dense, preferred_element_type=F32).astype(BF16)


def upstream(expert, ids_all, grads, weight, capacity):
    sources, top_count, tokens = ids_all.shape
    hidden_units, width = weight.shape
    return pl.pallas_call(
        functools.partial(upstream_kernel, capacity),
        out_shape=jax.ShapeDtypeStruct((sources, capacity, hidden_units), BF16),
        grid_spec=pltpu.PrefetchScalarGridSpec(
            num_scalar_prefetch=1,
            grid=(sources,),
            in_specs=[
                pl.BlockSpec((1, top_count, tokens), lambda j, e: (j, 0, 0)),
                pl.BlockSpec((tokens, width), lambda j, e: (j, 0)),
                pl.BlockSpec((hidden_units, width), lambda j, e: (0, 0)),
            ],
            out_specs=pl.BlockSpec((1, capacity, hidden_units), lambda j, e: (j, 0, 0)),
        ),
        compiler_params=pltpu.CompilerParams(vmem_limit_bytes=VMEM_LIMIT),
        name="upstream",
    )(expert, ids_all, grads, weight)


def weight_kernel(scalar_ref, ids_ref, hidden_ref, grad_ref, out_ref, dense):
    sources, top_count, tokens = ids_ref.shape
    capacity = hidden_ref.shape[1]

    @pl.when(pl.program_id(0) == 0)
    def _():
        for j in range(sources):
            rank = source_rank(ids_ref[j], scalar_ref[0], tokens)
            choose = (rank == lax.broadcasted_iota(I32, (capacity, tokens), 0)).astype(F32).astype(BF16)
            dense[:, j * tokens : (j + 1) * tokens] = lax.dot_general(
                hidden_ref[j], choose, (((0,), (0,)), ((), ())), preferred_element_type=F32
            ).astype(BF16)

    total = jnp.dot(dense[...], grad_ref[...], preferred_element_type=F32)
    out_ref[...] = (total * scalar_ref[1].astype(F32)).astype(BF16)


def weight_sum(scalars, ids_all, recv_hidden, grads):
    sources, capacity, hidden_units = recv_hidden.shape
    _, top_count, tokens = ids_all.shape
    rows, width = grads.shape
    step = 256
    return pl.pallas_call(
        weight_kernel,
        out_shape=jax.ShapeDtypeStruct((hidden_units, width), BF16),
        grid_spec=pltpu.PrefetchScalarGridSpec(
            num_scalar_prefetch=1,
            grid=(width // step,),
            in_specs=[
                pl.BlockSpec((sources, top_count, tokens), lambda n, e: (0, 0, 0)),
                pl.BlockSpec((sources, capacity, hidden_units), lambda n, e: (0, 0, 0)),
                pl.BlockSpec((rows, step), lambda n, e: (0, n)),
            ],
            out_specs=pl.BlockSpec((hidden_units, step), lambda n, e: (0, n)),
            scratch_shapes=[pltpu.VMEM((hidden_units, rows), BF16)],
        ),
        compiler_params=pltpu.CompilerParams(vmem_limit_bytes=VMEM_LIMIT),
        name="weight_sum",
    )(scalars, ids_all, recv_hidden, grads)


def unpack_kernel(place_ref, gates_ref, hidden_ref, back_ref, grad_ref, gate_ref, select):
    tokens, top_count = place_ref.shape
    rows = back_ref.shape[0]
    for k in range(top_count):
        lane = lax.broadcasted_iota(I32, (tokens, rows), 1)
        select[...] = (place_ref[:, k : k + 1] == lane).astype(F32).astype(BF16)
        up = jnp.dot(select[...], back_ref[...], preferred_element_type=F32)
        grad_ref[:, k, :] = (gates_ref[:, k : k + 1].astype(F32) * up).astype(BF16)
        gate_ref[:, k : k + 1] = jnp.sum(
            hidden_ref[:, k, :].astype(F32) * up, axis=1, keepdims=True
        ).astype(BF16)


def unpack(place, gates, saved_hidden, back):
    tokens, top_count, hidden_units = saved_hidden.shape
    return pl.pallas_call(
        unpack_kernel,
        out_shape=(
            jax.ShapeDtypeStruct((tokens, top_count, hidden_units), BF16),
            jax.ShapeDtypeStruct((tokens, top_count), BF16),
        ),
        in_specs=[whole()] * 4,
        out_specs=(whole(), whole()),
        scratch_shapes=[pltpu.VMEM((tokens, back.shape[0]), BF16)],
        compiler_params=pltpu.CompilerParams(vmem_limit_bytes=VMEM_LIMIT),
        name="unpack",
    )(place, gates, saved_hidden, back)


def local(out_grad, saved_hidden, expert_ids, gate_weights, trained, down_weight):
    experts = lax.axis_size("expert")
    tokens, top_count, hidden_units = saved_hidden.shape
    capacity = min(tokens, 3 * tokens * top_count // (2 * experts))
    ids_t = expert_ids.T
    me = lax.axis_index("expert").astype(I32)
    ids_all = lax.all_gather(ids_t, "expert", axis=0)
    grads = lax.all_gather(out_grad, "expert", axis=0, tiled=True)
    packed, place_t = pack(ids_t, gate_weights.T, saved_hidden, experts, capacity)
    recv_hidden = lax.all_to_all(
        packed.reshape(experts, capacity, hidden_units), "expert", 0, 0, tiled=True
    )
    up = upstream(me[None], ids_all, grads, down_weight[0], capacity)
    back = lax.all_to_all(up, "expert", 0, 0, tiled=True)
    weight_grad = weight_sum(jnp.stack([me, trained[0]]), ids_all, recv_hidden, grads)
    hidden_grad, gate_grad = unpack(
        place_t.T, gate_weights, saved_hidden, back.reshape(experts * capacity, hidden_units)
    )
    return hidden_grad, gate_grad, weight_grad[None]


def solution(mesh):
    placed = (
        P(("groups", "expert"), None),
        P(("groups", "expert"), None, None),
        P(("groups", "expert"), None),
        P(("groups", "expert"), None),
        P(("groups", "expert")),
        P("expert", None, None),
    )
    return jax.shard_map(
        local,
        mesh=mesh,
        in_specs=placed,
        out_specs=(
            P(("groups", "expert"), None, None),
            P(("groups", "expert"), None),
            P(("groups", "expert"), None, None),
        ),
        check_vma=False,
    )
```

time: 284 us -> 221 us (0.78)
  waiting for transfers between devices: 165 us -> 58.1 us
  blocking collectives: 8.5 us -> 73 us
  local copies, waits for them, and re-layouts: 62.5 us -> 8.68 us
  Pallas kernels: 0 us -> 52.2 us
  matrix products: 19.4 us -> 0 us
  between operations: 1.43 us -> 14.8 us
  starting transfers between devices: 23.7 us -> 13.2 us
    all_to_all x4 -> x2, waiting for transfers between devices: 165 us -> 23.2 us  [the longest x1 23.2 us: local(): back = lax.all_to_all(up, 'expert', 0, 0, tiled=True)]
    all_gather x0 -> x1, blocking collectives: none -> 73 us  [local(): ids_all = lax.all_gather(ids_t, 'expert', axis=0)]
    pallas_call x0 -> x4, Pallas kernels: none -> 52.2 us  [the longest x1 26.8 us: upstream(): pl.pallas_call(functools.partial(upstream_kernel, capacity), out_shape=ja...]
    scatter x3 -> x0, local copies, waits for them, and re-layouts: 43.8 us -> none  [the longest x1 28.2 us: local(): send_grad = jnp.zeros((experts * capacity, model_width), jnp.bfloat16).at...]
    all_gather x0 -> x1, waiting for transfers between devices: none -> 34.2 us  [local(): grads = lax.all_gather(out_grad, 'expert', axis=0, tiled=True)]
    dot_general x2 -> x0, matrix products: 19.4 us -> none  [the longest x1 10 us: local(): lax.dot_general(rows_grad, weight, (((1,), (1,)), ((), ())), preferred_el...]
    all_to_all x4 -> x2, starting transfers between devices: 23.7 us -> 13.2 us  [the longest x1 6.63 us: local(): back = lax.all_to_all(up, 'expert', 0, 0, tiled=True)]
    all_to_all x1 -> x0, blocking collectives: 8.5 us -> none  [local(): lax.all_to_all(gate_part.reshape(experts, capacity), 'expert', split_axis...]
  transfers between devices with their start and end apart: 4 -> 3, of which waited for: 3 -> 2; matrix products, arithmetic and copies ran while one was open for 19% -> 1% of each run, Pallas kernels for 0% -> 21%
where the time goes in v1:
time: 221 us; the launch traced here: 220 us
  blocking collectives  73 us (33%)
  waiting for transfers between devices  58.1 us (26%)
  Pallas kernels  52.2 us (24%)
  between operations  14.8 us (7%)
  starting transfers between devices  13.2 us (6%)
  local copies, waits for them, and re-layouts  8.68 us (4%)
    all_gather x1, blocking collectives, local(): ids_all = lax.all_gather(ids_t, 'expert', axis=0)  73 us
    all_gather x1, waiting for transfers between devices, local(): grads = lax.all_gather(out_grad, 'expert', axis=0, tiled=True)  34.2 us
    pallas_call x1, Pallas kernels, upstream(): pl.pallas_call(functools.partial(upstream_kernel, capacity), out_shape=ja...  26.8 us
    all_to_all x1, waiting for transfers between devices, local(): back = lax.all_to_all(up, 'expert', 0, 0, tiled=True)  23.2 us
    pallas_call x1, Pallas kernels, weight_sum(): pl.pallas_call(weight_kernel, out_shape=jax.ShapeDtypeStruct((hidden_unit...  16.4 us
    unnamed x14, local copies, waits for them, and re-layouts  8.57 us
    all_to_all x1, starting transfers between devices, local(): back = lax.all_to_all(up, 'expert', 0, 0, tiled=True)  6.63 us
    all_to_all x1, starting transfers between devices, local(): lax.all_to_all(packed.reshape(experts, capacity, hidden_units), 'expert',...  6.55 us
  transfers between devices with their start and end apart: 3, of which 2 were waited for; matrix products, arithmetic and copies ran while one was open for 1% of the time, Pallas kernels for 21%

profile of v1, /device:TPU:13, one launch (start us, length us, event | category | flops | bytes accessed | tf_op | source)
XLA Modules:
  0.0 220.0 jit_solution(17530572760968582667)
XLA Ops:
  7.2 0.0 copy-start.3
  7.2 0.0 copy-start.4
  7.2 0.0 all-gather.4.cloned.1.call-start
  7.2 0.7 all-gather.4.cloned.1.call-update
  7.9 1.9 copy.15.hidden_ref
  9.9 0.0 copy-done.3
  9.9 0.0 copy-done.4
  9.9 3.4 %pack.1 = (bf16[1152,768]{1,0:T(8,128)(2,1)S(1)}, s32[6,128]{1,0:T(8,128)S(1)}) custom-call(s32[6,128]{1,0:T(8,128)S(1)} %bitcast.13, bf16[6,128]{1,0:T(8,128)(2,1)S(1)} %bitcast.15, bf16[128,6,768]{2,1,0:T(8,128)(2,1)S(1)} %copy.15.hidden_ref), custom_call_target="tpu_custom_call" | custom-call | tf_op jit(solution)/shard_map/pack/pallas_call | solution.py:52
  13.3 0.0 copy-start.2
  13.3 1.2 copy-done.2
  14.5 6.6 %all-to-all-start.1 = ((bf16[16,72,768]{2,1,0:T(8,128)(2,1)}), bf16[16,72,768]{2,1,0:T(8,128)(2,1)S(1)}, u32[]{:S(2)}, u32[]{:S(2)}) async-start(bf16[16,72,768]{2,1,0:T(8,128)(2,1)} %bitcast.11), calls=%async_computation.1 | async-start | bytes 3538944 | tf_op jit(solution)/shard_map/all_to_all | solution.py:185
  21.0 73.0 %all-gather.1.ids_ref = s32[16,6,128]{2,1,0:T(8,128)S(1)} all-gather(s32[1,6,128]{2,1,0:T(8,128)S(1)} %bitcast.14), channel_id=2, replica_groups=mesh['groups'=2,'expert'=16] {'expert'}, dimensions={0}, use_global_device_ids=true | all-gather | bytes 52224 | tf_op jit(solution)/shard_map/all_gather | solution.py:182
  94.0 34.2 %all-gather.4.cloned.1.call-done.grad_ref = bf16[2048,2560]{1,0:T(8,128)(2,1)} async-done(((bf16[128,2560]{1,0:T(8,128)(2,1)}), bf16[2048,2560]{1,0:T(8,128)(2,1)}) %all-gather.4.cloned.1.call-update) | async-done | bytes 10485776 | tf_op jit(solution)/shard_map/all_gather | solution.py:183
  128.2 0.0 copy-start.1
  128.2 2.1 copy-done.1
  130.3 26.8 %upstream.1 = bf16[16,72,768]{2,1,0:T(8,128)(2,1)S(1)} custom-call(s32[1]{0:T(128)} %bitcast.3.expert_ref, s32[16,6,128]{2,1,0:T(8,128)S(1)} %all-gather.1.ids_ref, bf16[2048,2560]{1,0:T(8,128)(2,1)} %all-gather.4.cloned.1.call-done.grad_ref, bf16[768,2560]{1,0:T(8,128)(2,1)S(1)} %bitcast.10), custom_call_target="tpu_custom_call" | custom-call | tf_op jit(solution)/shard_map/upstream/pallas_call | solution.py:88
  157.1 0.0 copy-start
  157.1 1.3 copy-done
  158.3 0.0 all-to-all-done.1.hidden_ref
  158.3 6.6 %all-to-all-start = ((bf16[16,72,768]{2,1,0:T(8,128)(2,1)}), bf16[16,72,768]{2,1,0:T(8,128)(2,1)}, u32[]{:S(2)}, u32[]{:S(2)}) async-start(bf16[16,72,768]{2,1,0:T(8,128)(2,1)} %copy-done), calls=%async_computation | async-start | bytes 3538944 | tf_op jit(solution)/shard_map/all_to_all | solution.py:189
  165.0 0.1 copy.17.gates_ref
  165.1 0.1 copy.16
  165.9 0.1 pad_add_fusion.scalar_ref
  166.0 16.4 %weight_sum.1 = bf16[768,2560]{1,0:T(8,128)(2,1)} custom-call(s32[2]{0:T(128)S(1)} %pad_add_fusion.scalar_ref, s32[16,6,128]{2,1,0:T(8,128)S(1)} %all-gather.1.ids_ref, bf16[16,72,768]{2,1,0:T(8,128)(2,1)S(1)} %all-to-all-done.1.hidden_ref, bf16[2048,2560]{1,0:T(8,128)(2,1)} %all-gather.4.cloned.1.call-done.grad_ref), custom_call_target="tpu_custom_call" | custom-call | tf_op jit(solution)/shard_map/weight_sum/pallas_call | solution.py:128
  182.3 23.2 %all-to-all-done = bf16[16,72,768]{2,1,0:T(8,128)(2,1)} async-done(((bf16[16,72,768]{2,1,0:T(8,128)(2,1)}), bf16[16,72,768]{2,1,0:T(8,128)(2,1)}, u32[]{:S(2)}, u32[]{:S(2)}) %all-to-all-start) | async-done | bytes 1769504 | tf_op jit(solution)/shard_map/all_to_all | solution.py:189
  205.5 5.7 %unpack.1 = (bf16[128,6,768]{2,1,0:T(8,128)(2,1)S(1)}, bf16[128,6]{1,0:T(8,128)(2,1)S(1)}) custom-call(s32[128,6]{1,0:T(8,128)S(1)} %bitcast.12, bf16[128,6]{1,0:T(8,128)(2,1)S(1)} %copy.17.gates_ref, bf16[128,6,768]{2,1,0:T(8,128)(2,1)S(1)} %copy.15.hidden_ref, bf16[1152,768]{1,0:T(8,128)(2,1)} %bitcast.6.back_ref), custom_call_target="tpu_custom_call" | custom-call | tf_op jit(solution)/shard_map/unpack/pallas_call | solution.py:162
  211.2 1.2 copy.19
  212.5 0.7 copy.20
Async XLA Ops:
  7.2 2.7 %copy-start.3 = (s32[128,6]{0,1:T(8,128)S(1)}, s32[128,6]{0,1:T(8,128)}, u32[]{:S(2)}) copy-start(s32[128,6]{0,1:T(8,128)} %param.8) | copy-start | bytes 9220
  7.2 2.7 %copy-start.4 = (bf16[128,6]{0,1:T(8,128)(2,1)S(1)}, bf16[128,6]{0,1:T(8,128)(2,1)}, u32[]{:S(2)}) copy-start(bf16[128,6]{0,1:T(8,128)(2,1)} %param.9) | copy-start | bytes 4612
  7.2 121.0 %all-gather.4.cloned.1.call-start = ((), (), s32[]{:S(2)}) async-start(), calls=%async_computation.2 | async-start | bytes 11141120 | tf_op jit(solution)/shard_map/all_gather | solution.py:183
  13.3 1.2 copy-start.2
  14.5 143.9 %all-to-all-start.1 = ((bf16[16,72,768]{2,1,0:T(8,128)(2,1)}), bf16[16,72,768]{2,1,0:T(8,128)(2,1)S(1)}, u32[]{:S(2)}, u32[]{:S(2)}) async-start(bf16[16,72,768]{2,1,0:T(8,128)(2,1)} %bitcast.11), calls=%async_computation.1 | async-start | bytes 3538944 | tf_op jit(solution)/shard_map/all_to_all | solution.py:185
  128.2 2.1 copy-start.1
  157.1 1.3 copy-start
  158.3 47.2 %all-to-all-start = ((bf16[16,72,768]{2,1,0:T(8,128)(2,1)}), bf16[16,72,768]{2,1,0:T(8,128)(2,1)}, u32[]{:S(2)}, u32[]{:S(2)}) async-start(bf16[16,72,768]{2,1,0:T(8,128)(2,1)} %copy-done), calls=%async_computation | async-start | bytes 3538944 | tf_op jit(solution)/shard_map/all_to_all | solution.py:189
Sparse Core Ops, SparseCore 0:
  10.3 117.8 all-gather.3

commit v2 on v1

--- a/solution.py
+++ b/solution.py
@@ -33,7 +33,7 @@
         place_ref[k : k + 1, :] = jnp.sum(
             jnp.where(ids_ref[k : k + 1, :] == expert, target, 0), axis=0, keepdims=True
         )
-        table[k * tokens : (k + 1) * tokens, :] = hidden_ref[:, k, :]
+        table[k * tokens : (k + 1) * tokens, :] = hidden_ref[k]
     rows = out_ref.shape[0]
     step = 128
     for first in range(0, rows, step):
@@ -47,8 +47,8 @@
         ).astype(BF16)
 
 
-def pack(ids_t, gates_t, saved_hidden, experts, capacity):
-    tokens, top_count, hidden_units = saved_hidden.shape
+def pack(ids_t, gates_t, hidden_t, experts, capacity):
+    top_count, tokens, hidden_units = hidden_t.shape
     return pl.pallas_call(
         functools.partial(pack_kernel, experts, capacity),
         out_shape=(
@@ -63,7 +63,7 @@
         ],
         compiler_params=pltpu.CompilerParams(vmem_limit_bytes=VMEM_LIMIT),
         name="pack",
-    )(ids_t, gates_t, saved_hidden)
+    )(ids_t, gates_t, hidden_t)
 
 
 def source_rank(ids, expert, tokens):
@@ -144,33 +144,209 @@
     )(scalars, ids_all, recv_hidden, grads)
 
 
-def unpack_kernel(place_ref, gates_ref, hidden_ref, back_ref, grad_ref, gate_ref, select):
+RING_STEPS = 4
+
+
+def ring_device(position, core):
+    z, y = (position, 0) if position < 4 else (7 - position, 1)
+    return (z * 2 + y) * 2 + core
+
+
+def ring_shift(step):
+    return [
+        (ring_device(p, core), ring_device((p + step) % 8, core)) for p in range(8) for core in range(2)
+    ]
+
+
+def ring_gather(block, ids_t, packed):
+    half = block.shape[0] // 2
+    ids_all = lax.all_to_all(jnp.broadcast_to(ids_t[None], (16, *ids_t.shape)), "expert", 0, 0, tiled=True)
+    ahead = behind = block
+    pieces = [block]
+    for step in range(RING_STEPS - 1):
+        ahead = lax.ppermute(ahead, "expert", ring_shift(1))
+        behind = lax.ppermute(behind, "expert", ring_shift(-1))
+        if step == 1:
+            ahead, behind, ids_all, packed = lax.optimization_barrier((ahead, behind, ids_all, packed))
+        pieces += [ahead, behind]
+    pieces += [
+        lax.ppermute(ahead[:half], "expert", ring_shift(1)),
+        lax.ppermute(behind[half:], "expert", ring_shift(-1)),
+    ]
+    pieces[7], pieces[8], packed = lax.optimization_barrier((pieces[7], pieces[8], packed))
+    swap = [(i, i ^ 1) for i in range(16)]
+    return ids_all, packed, pieces + [lax.ppermute(piece, "expert", swap) for piece in pieces]
+
+
+OFFSETS = (0, -1, 1, -2, 2, -3, 3, 4)
+
+
+def slot_source(me, slot):
+    chip, core = me // 2, me % 2
+    z, y = chip // 2, chip % 2
+    position = jnp.where(y == 0, z, 7 - z)
+    other = (position + OFFSETS[slot // 2] + 8) % 8
+    oz = jnp.where(other < 4, other, 7 - other)
+    oy = jnp.where(other < 4, 0, 1)
+    return (oz * 2 + oy) * 2 + (core + slot % 2) % 2
+
+
+def fetches(piece_refs, grads, sems, tokens):
+    per_core = len(piece_refs) // 2
+    copies = []
+    for slot in range(16):
+        refs = piece_refs[(slot % 2) * per_core :]
+        i = slot // 2
+        parts = [refs[i]] if i < 7 else [refs[7], refs[8]]
+        at = slot * tokens
+        mine = []
+        for n, part in enumerate(parts):
+            mine.append(
+                pltpu.make_async_copy(part, grads.at[pl.ds(at, part.shape[0])], sems.at[slot, n])
+            )
+            at += part.shape[0]
+        copies.append(mine)
+    return copies
+
+
+def ring_upstream_kernel(capacity, me_ref, ids_ref, weight_ref, *rest):
+    pieces, (out_ref, grads, sems) = rest[:18], rest[18:]
+    tokens = ids_ref.shape[2]
+    copies = fetches(pieces, grads, sems, tokens)
+    for mine in copies:
+        for copy in mine:
+            copy.start()
+    group = 4
+    for first in range(0, 16, group):
+        for mine in copies[first : first + group]:
+            for copy in mine:
+                copy.wait()
+        dense = lax.dot_general(
+            grads[first * tokens : (first + group) * tokens, :],
+            weight_ref[...],
+            (((1,), (1,)), ((), ())),
+            preferred_element_type=F32,
+        ).astype(BF16)
+        for slot in range(first, first + group):
+            source = slot_source(me_ref[0], slot)
+            rank = source_rank(ids_ref[source], me_ref[0], tokens)
+            row = lax.broadcasted_iota(I32, (capacity, tokens), 0)
+            choose = (rank == row).astype(F32).astype(BF16)
+            at = (slot - first) * tokens
+            out_ref[source] = jnp.dot(
+                choose, dense[at : at + tokens, :], preferred_element_type=F32
+            ).astype(BF16)
+
+
+def ring_upstream(me, ids_all, pieces, weight, capacity):
+    sources, top_count, tokens = ids_all.shape
+    hidden_units, width = weight.shape
+    return pl.pallas_call(
+        functools.partial(ring_upstream_kernel, capacity),
+        out_shape=jax.ShapeDtypeStruct((sources, capacity, hidden_units), BF16),
+        in_specs=[whole(pltpu.SMEM), whole(), whole()] + [whole(pl.ANY)] * 18,
+        out_specs=whole(),
+        scratch_shapes=[
+            pltpu.VMEM((sources * tokens, width), BF16),
+            pltpu.SemaphoreType.DMA((16, 2)),
+        ],
+        compiler_params=pltpu.CompilerParams(vmem_limit_bytes=VMEM_LIMIT),
+        cost_estimate=pl.CostEstimate(
+            flops=2 * sources * tokens * hidden_units * width,
+            bytes_accessed=2 * (sources * tokens + hidden_units) * width,
+            transcendentals=0,
+        ),
+        name="upstream",
+    )(me, ids_all, weight, *pieces)
+
+
+def ring_weight_kernel(scalar_ref, ids_ref, hidden_ref, *rest):
+    pieces, (out_ref, grads, sems, dense) = rest[:18], rest[18:]
+    tokens = ids_ref.shape[2]
+    capacity = hidden_ref.shape[1]
+    copies = fetches(pieces, grads, sems, tokens)
+    for mine in copies:
+        for copy in mine:
+            copy.start()
+    for slot in range(16):
+        source = slot_source(scalar_ref[0], slot)
+        rank = source_rank(ids_ref[source], scalar_ref[0], tokens)
+        row = lax.broadcasted_iota(I32, (capacity, tokens), 0)
+        choose = (rank == row).astype(F32).astype(BF16)
+        dense[:, slot * tokens : (slot + 1) * tokens] = lax.dot_general(
+            hidden_ref[source], choose, (((0,), (0,)), ((), ())), preferred_element_type=F32
+        ).astype(BF16)
+    for mine in copies:
+        for copy in mine:
+            copy.wait()
+    width = grads.shape[1]
+    step = 256
+
+    @pl.loop(0, width // step)
+    def _(n):
+        at = pl.ds(pl.multiple_of(n * step, step), step)
+        total = jnp.dot(dense[...], grads[:, at], preferred_element_type=F32)
+        out_ref[:, at] = (total * scalar_ref[1].astype(F32)).astype(BF16)
+
+
+def ring_weight_sum(scalars, ids_all, recv_hidden, pieces):
+    sources, capacity, hidden_units = recv_hidden.shape
+    _, top_count, tokens = ids_all.shape
+    width = pieces[0].shape[1]
+    return pl.pallas_call(
+        ring_weight_kernel,
+        out_shape=jax.ShapeDtypeStruct((hidden_units, width), BF16),
+        in_specs=[whole(pltpu.SMEM), whole(), whole()] + [whole(pl.ANY)] * 18,
+        out_specs=whole(),
+        scratch_shapes=[
+            pltpu.VMEM((sources * tokens, width), BF16),
+            pltpu.SemaphoreType.DMA((16, 2)),
+            pltpu.VMEM((hidden_units, sources * tokens), BF16),
+        ],
+        compiler_params=pltpu.CompilerParams(vmem_limit_bytes=VMEM_LIMIT),
+        cost_estimate=pl.CostEstimate(
+            flops=2 * sources * tokens * hidden_units * width,
+            bytes_accessed=2 * (sources * tokens + hidden_units) * width,
+            transcendentals=0,
+        ),
+        name="weight_sum",
+    )(scalars, ids_all, recv_hidden, *pieces)
+
+
+def unpack_kernel(place_ref, gates_ref, hidden_ref, back_ref, grad_ref, gate_ref, select, sums):
     tokens, top_count = place_ref.shape
     rows = back_ref.shape[0]
+    lane = lax.broadcasted_iota(I32, (tokens, rows), 1)
     for k in range(top_count):
-        lane = lax.broadcasted_iota(I32, (tokens, rows), 1)
-        select[...] = (place_ref[:, k : k + 1] == lane).astype(F32).astype(BF16)
-        up = jnp.dot(select[...], back_ref[...], preferred_element_type=F32)
-        grad_ref[:, k, :] = (gates_ref[:, k : k + 1].astype(F32) * up).astype(BF16)
-        gate_ref[:, k : k + 1] = jnp.sum(
-            hidden_ref[:, k, :].astype(F32) * up, axis=1, keepdims=True
-        ).astype(BF16)
-
-
-def unpack(place, gates, saved_hidden, back):
-    tokens, top_count, hidden_units = saved_hidden.shape
+        select[k * tokens : (k + 1) * tokens, :] = (
+            (place_ref[:, k : k + 1] == lane).astype(F32).astype(BF16)
+        )
+    sums[...] = jnp.zeros_like(sums)
+    up = jnp.dot(select[...], back_ref[...], preferred_element_type=F32)
+    for k in range(top_count):
+        mine = up[k * tokens : (k + 1) * tokens, :]
+        grad_ref[k] = (gates_ref[:, k : k + 1].astype(F32) * mine).astype(BF16)
+        sums[:, k : k + 1] = jnp.sum(hidden_ref[k].astype(F32) * mine, axis=1, keepdims=True)
+    gate_ref[...] = sums[...].T[:top_count, :].astype(BF16)
+
+
+def unpack(place, gates, hidden_t, back):
+    top_count, tokens, hidden_units = hidden_t.shape
     return pl.pallas_call(
         unpack_kernel,
         out_shape=(
-            jax.ShapeDtypeStruct((tokens, top_count, hidden_units), BF16),
-            jax.ShapeDtypeStruct((tokens, top_count), BF16),
+            jax.ShapeDtypeStruct((top_count, tokens, hidden_units), BF16),
+            jax.ShapeDtypeStruct((top_count, tokens), BF16),
         ),
         in_specs=[whole()] * 4,
         out_specs=(whole(), whole()),
-        scratch_shapes=[pltpu.VMEM((tokens, back.shape[0]), BF16)],
+        scratch_shapes=[
+            pltpu.VMEM((top_count * tokens, back.shape[0]), BF16),
+            pltpu.VMEM((tokens, 128), F32),
+        ],
         compiler_params=pltpu.CompilerParams(vmem_limit_bytes=VMEM_LIMIT),
         name="unpack",
-    )(place, gates, saved_hidden, back)
+    )(place, gates, hidden_t, back)
 
 
 def local(out_grad, saved_hidden, expert_ids, gate_weights, trained, down_weight):
@@ -178,20 +354,27 @@
     tokens, top_count, hidden_units = saved_hidden.shape
     capacity = min(tokens, 3 * tokens * top_count // (2 * experts))
     ids_t = expert_ids.T
+    hidden_t = saved_hidden.transpose(1, 0, 2)
     me = lax.axis_index("expert").astype(I32)
-    ids_all = lax.all_gather(ids_t, "expert", axis=0)
-    grads = lax.all_gather(out_grad, "expert", axis=0, tiled=True)
-    packed, place_t = pack(ids_t, gate_weights.T, saved_hidden, experts, capacity)
+    scalars = jnp.stack([me, trained[0]])
+    packed, place_t = pack(ids_t, gate_weights.T, hidden_t, experts, capacity)
+    if experts == 16:
+        ids_all, packed, grads = ring_gather(out_grad, ids_t, packed)
+        make_upstream, make_weight = ring_upstream, ring_weight_sum
+    else:
+        ids_all = lax.all_gather(ids_t, "expert", axis=0)
+        grads = lax.all_gather(out_grad, "expert", axis=0, tiled=True)
+        make_upstream, make_weight = upstream, weight_sum
     recv_hidden = lax.all_to_all(
         packed.reshape(experts, capacity, hidden_units), "expert", 0, 0, tiled=True
     )
-    up = upstream(me[None], ids_all, grads, down_weight[0], capacity)
+    up = make_upstream(me[None], ids_all, grads, down_weight[0], capacity)
     back = lax.all_to_all(up, "expert", 0, 0, tiled=True)
-    weight_grad = weight_sum(jnp.stack([me, trained[0]]), ids_all, recv_hidden, grads)
+    weight_grad = make_weight(scalars, ids_all, recv_hidden, grads)
     hidden_grad, gate_grad = unpack(
-        place_t.T, gate_weights, saved_hidden, back.reshape(experts * capacity, hidden_units)
+        place_t.T, gate_weights, hidden_t, back.reshape(experts * capacity, hidden_units)
     )
-    return hidden_grad, gate_grad, weight_grad[None]
+    return hidden_grad.transpose(1, 0, 2), gate_grad.T, weight_grad[None]
 
 
 def solution(mesh):

time: 221 us -> 158 us (0.71)
  blocking collectives: 73 us -> 0 us
  starting transfers between devices: 13.2 us -> 28.8 us
  between operations: 14.8 us -> 1.41 us
  waiting for transfers between devices: 58.1 us -> 70.4 us
  Pallas kernels: 52.2 us -> 43.6 us
  local copies, waits for them, and re-layouts: 8.68 us -> 12.9 us
    all_gather x1 -> x0, blocking collectives: 73 us -> none  [local(): ids_all = lax.all_gather(ids_t, 'expert', axis=0)]
    ppermute x0 -> x17, waiting for transfers between devices: none -> 42 us  [the longest x3 28.8 us: ring_gather(): ahead = lax.ppermute(ahead, 'expert', ring_shift(1))]
    all_gather x1 -> x0, waiting for transfers between devices: 34.2 us -> none  [local(): grads = lax.all_gather(out_grad, 'expert', axis=0, tiled=True)]
    all_to_all x1, waiting for transfers between devices: 0.01 us -> 10.6 us  [local(): lax.all_to_all(packed.reshape(experts, capacity, hidden_units), 'expert',...]
    ppermute x0 -> x17, starting transfers between devices: none -> 8.96 us  [the longest x3 2.96 us: ring_gather(): behind = lax.ppermute(behind, 'expert', ring_shift(-1))]
    all_to_all x1, waiting for transfers between devices: 23.2 us -> 14.7 us  [local(): back = lax.all_to_all(up, 'expert', 0, 0, tiled=True)]
    pallas_call x3, Pallas kernels: 48.9 us -> 40.4 us  [the longest x1 19.1 us: ring_upstream(): pl.pallas_call(functools.partial(ring_upstream_kernel, capacity), out_sha...]
    all_to_all x0 -> x1, starting transfers between devices: none -> 7.99 us  [ring_gather(): lax.all_to_all(jnp.broadcast_to(ids_t[None], (16, *ids_t.shape)), 'expert...]
  transfers between devices with their start and end apart: 3 -> 20, of which waited for: 2 -> 12; matrix products, arithmetic and copies ran while one was open for 1% -> 1% of each run, Pallas kernels for 21% -> 26%
where the time goes in v2:
time: 158 us; the launch traced here: 157 us
  waiting for transfers between devices  70.4 us (45%)
  Pallas kernels  43.6 us (28%)
  starting transfers between devices  28.8 us (18%)
  local copies, waits for them, and re-layouts  12.9 us (8%)
    ppermute x3, waiting for transfers between devices, ring_gather(): ahead = lax.ppermute(ahead, 'expert', ring_shift(1))  28.8 us
    pallas_call x1, Pallas kernels, ring_upstream(): pl.pallas_call(functools.partial(ring_upstream_kernel, capacity), out_sha...  19.1 us
    pallas_call x1, Pallas kernels, ring_weight_sum(): pl.pallas_call(ring_weight_kernel, out_shape=jax.ShapeDtypeStruct((hidden...  18.1 us
    all_to_all x1, waiting for transfers between devices, local(): back = lax.all_to_all(up, 'expert', 0, 0, tiled=True)  14.7 us
    unnamed x45, local copies, waits for them, and re-layouts  11.4 us
    all_to_all x1, waiting for transfers between devices, local(): lax.all_to_all(packed.reshape(experts, capacity, hidden_units), 'expert',...  10.6 us
    all_to_all x1, starting transfers between devices, ring_gather(): lax.all_to_all(jnp.broadcast_to(ids_t[None], (16, *ids_t.shape)), 'expert...  7.99 us
    all_to_all x1, starting transfers between devices, local(): lax.all_to_all(packed.reshape(experts, capacity, hidden_units), 'expert',...  6.99 us
  transfers between devices with their start and end apart: 20, of which 12 were waited for; matrix products, arithmetic and copies ran while one was open for 1% of the time, Pallas kernels for 26%

profile of v2, /device:TPU:13, one launch (start us, length us, event | category | flops | bytes accessed | tf_op | source)
XLA Modules:
  0.0 157.2 jit_solution(9103295661325818256)
XLA Ops:
  0.6 0.2 collective-permute-start
  0.9 1.3 collective-permute-start.2
  2.1 14.3 %collective-permute-done.rest_1_ = bf16[128,2560]{1,0:T(8,128)(2,1)S(1)} collective-permute-done((bf16[128,2560]{1,0:T(8,128)(2,1)}, bf16[128,2560]{1,0:T(8,128)(2,1)S(1)}, u32[]{:S(2)}, u32[]{:S(2)}) %collective-permute-start) | collective-permute-done | bytes 655392 | tf_op jit(solution)/shard_map/ppermute | solution.py:167
  16.5 0.2 collective-permute-start.1
  16.7 0.0 collective-permute-done.2.rest_2_
  16.7 1.3 collective-permute-start.3
  18.0 1.3 broadcast_in_dim.13
  19.3 8.0 %all-to-all-start = ((s32[16,6,128]{2,1,0:T(8,128)}), s32[16,6,128]{2,1,0:T(8,128)S(1)}, u32[]{:S(2)}, u32[]{:S(2)}) async-start(s32[16,6,128]{2,1,0:T(8,128)} %broadcast_in_dim.13), calls=%async_computation | async-start | bytes 131072 | tf_op jit(solution)/shard_map/all_to_all | solution.py:163
  27.3 1.3 copy-done
  28.5 0.7 copy-done.6
  29.2 0.7 copy-done.7
  29.9 3.1 %pack.1 = (bf16[1152,768]{1,0:T(8,128)(2,1)}, s32[6,128]{1,0:T(8,128)S(1)}) custom-call(s32[6,128]{1,0:T(8,128)S(1)} %bitcast.16, bf16[6,128]{1,0:T(8,128)(2,1)S(1)} %bitcast.17, bf16[6,128,768]{2,1,0:T(8,128)(2,1)S(1)} %bitcast.12), custom_call_target="tpu_custom_call" | custom-call | tf_op jit(solution)/shard_map/pack/pallas_call | solution.py:52
  33.1 3.2 %all-to-all-done.ids_ref = s32[16,6,128]{2,1,0:T(8,128)S(1)} async-done(((s32[16,6,128]{2,1,0:T(8,128)}), s32[16,6,128]{2,1,0:T(8,128)S(1)}, u32[]{:S(2)}, u32[]{:S(2)}) %all-to-all-start) | async-done | bytes 49184 | tf_op jit(solution)/shard_map/all_to_all | solution.py:163
  36.2 0.0 collective-permute-done.1.rest_3_
  36.2 0.0 collective-permute-done.3.rest_4_
  36.2 1.1 collective-permute-start.4
  37.4 0.4 collective-permute-start.5
  37.7 14.5 %collective-permute-done.4.rest_5_ = bf16[128,2560]{1,0:T(8,128)(2,1)S(1)} collective-permute-done((bf16[128,2560]{1,0:T(8,128)(2,1)S(1)}, bf16[128,2560]{1,0:T(8,128)(2,1)S(1)}, u32[]{:S(2)}, u32[]{:S(2)}) %collective-permute-start.4) | collective-permute-done | bytes 655392 | tf_op jit(solution)/shard_map/ppermute | solution.py:167
  52.2 1.1 collective-permute-start.6
  53.4 0.0 collective-permute-done.5.rest_6_
  53.4 0.4 collective-permute-start.7
  53.8 6.5 %collective-permute-done.6.rest_7_ = bf16[64,2560]{1,0:T(8,128)(2,1)} collective-permute-done((bf16[64,2560]{1,0:T(8,128)(2,1)S(1)}, bf16[64,2560]{1,0:T(8,128)(2,1)}, u32[]{:S(2)}, u32[]{:S(2)}) %collective-permute-start.6) | collective-permute-done | bytes 327712 | tf_op jit(solution)/shard_map/ppermute | solution.py:173
  60.4 0.9 collective-permute-done.7.rest_8_
  61.3 0.0 copy-done.15
  61.3 7.0 %all-to-all-start.2 = ((bf16[16,72,768]{2,1,0:T(8,128)(2,1)}), bf16[16,72,768]{2,1,0:T(8,128)(2,1)}, u32[]{:S(2)}, u32[]{:S(2)}) async-start(bf16[16,72,768]{2,1,0:T(8,128)(2,1)} %bitcast.9), calls=%async_computation.2 | async-start | bytes 3538944 | tf_op jit(solution)/shard_map/all_to_all | solution.py:368
  68.2 0.0 copy-done.9
  68.2 0.4 collective-permute-start.8
  68.7 0.1 collective-permute-start.10
  68.8 0.4 collective-permute-start.9
  69.2 0.1 collective-permute-start.11
  69.3 0.4 collective-permute-start.12
  69.7 0.7 collective-permute-done.8.rest_9_
  70.4 0.4 collective-permute-start.13
  70.8 1.5 collective-permute-done.10.rest_11_
  72.3 0.4 collective-permute-start.14
  72.7 2.4 %collective-permute-done.9.rest_10_ = bf16[128,2560]{1,0:T(8,128)(2,1)S(1)} collective-permute-done((bf16[128,2560]{1,0:T(8,128)(2,1)S(1)}, bf16[128,2560]{1,0:T(8,128)(2,1)S(1)}, u32[]{:S(2)}, u32[]{:S(2)}) %collective-permute-start.9) | collective-permute-done | bytes 655392 | tf_op jit(solution)/shard_map/ppermute | solution.py:178
  75.1 0.4 collective-permute-start.15
  75.5 0.0 collective-permute-done.11.rest_12_
  75.5 0.5 copy-done.20
  75.9 0.4 collective-permute-start.16
  76.3 0.5 copy-done.21
  76.8 0.0 collective-permute-done.12.rest_13_
  76.9 0.2 collective-permute-done.15.rest_16_
  77.1 0.8 collective-permute-done.16.rest_17_
  77.9 0.0 collective-permute-done.13.rest_14_
  77.9 0.0 collective-permute-done.14.rest_15_
  77.9 0.0 copy-done.13
  78.0 1.1 copy-done.16
  79.0 19.1 %upstream.1 = bf16[16,72,768]{2,1,0:T(8,128)(2,1)} custom-call(s32[1]{0:T(128)} %bitcast.4.me_ref, s32[16,6,128]{2,1,0:T(8,128)S(1)} %all-to-all-done.ids_ref, bf16[768,2560]{1,0:T(8,128)(2,1)} %bitcast.18, bf16[128,2560]{1,0:T(8,128)(2,1)S(1)} %copy-done.9, bf16[128,2560]{1,0:T(8,128)(2,1)S(1)} %collective-permute-done.rest_1_, ...), custom_call_target="tpu_custom_call" | custom-call | flops 8053063680 | bytes 14417920 | tf_op jit(solution)/shard_map/upstream/pallas_call | solution.py:244
  98.2 0.0 copy-start.8
  98.2 10.6 %all-to-all-done.2.hidden_ref = bf16[16,72,768]{2,1,0:T(8,128)(2,1)} async-done(((bf16[16,72,768]{2,1,0:T(8,128)(2,1)}), bf16[16,72,768]{2,1,0:T(8,128)(2,1)}, u32[]{:S(2)}, u32[]{:S(2)}) %all-to-all-start.2) | async-done | bytes 1769504 | tf_op jit(solution)/shard_map/all_to_all | solution.py:368
  108.8 4.9 %all-to-all-start.1 = ((bf16[16,72,768]{2,1,0:T(8,128)(2,1)}), bf16[16,72,768]{2,1,0:T(8,128)(2,1)S(1)}, u32[]{:S(2)}, u32[]{:S(2)}) async-start(bf16[16,72,768]{2,1,0:T(8,128)(2,1)} %upstream.1), calls=%async_computation.1 | async-start | bytes 3538944 | tf_op jit(solution)/shard_map/all_to_all | solution.py:372
  113.7 0.1 copy.10.gates_ref
  114.4 0.1 copy.9
  114.6 0.1 pad_add_fusion.scalar_ref
  114.6 1.1 copy-done.3
  115.7 1.1 copy-done.5
  116.8 1.1 copy-done.10
  117.9 1.1 copy-done.12
  119.0 1.1 copy-done.14
  120.1 1.1 copy-done.17
  121.2 18.1 %weight_sum.1 = bf16[768,2560]{1,0:T(8,128)(2,1)} custom-call(s32[2]{0:T(128)S(1)} %pad_add_fusion.scalar_ref, s32[16,6,128]{2,1,0:T(8,128)S(1)} %all-to-all-done.ids_ref, bf16[16,72,768]{2,1,0:T(8,128)(2,1)} %all-to-all-done.2.hidden_ref, bf16[128,2560]{1,0:T(8,128)(2,1)S(1)} %copy-done.10, bf16[128,2560]{1,0:T(8,128)(2,1)S(1)} %copy-done.12, ...), custom_call_target="tpu_custom_call" | custom-call | flops 8053063680 | bytes 14417920 | tf_op jit(solution)/shard_map/weight_sum/pallas_call | solution.py:296
  139.3 14.7 %all-to-all-done.1 = bf16[16,72,768]{2,1,0:T(8,128)(2,1)S(1)} async-done(((bf16[16,72,768]{2,1,0:T(8,128)(2,1)}), bf16[16,72,768]{2,1,0:T(8,128)(2,1)S(1)}, u32[]{:S(2)}, u32[]{:S(2)}) %all-to-all-start.1) | async-done | bytes 1769504 | tf_op jit(solution)/shard_map/all_to_all | solution.py:372
  154.0 3.2 %unpack.1 = (bf16[6,128,768]{2,1,0:T(8,128)(2,1)}, bf16[6,128]{1,0:T(8,128)(2,1)}) custom-call(s32[128,6]{1,0:T(8,128)S(1)} %bitcast.14, bf16[128,6]{1,0:T(8,128)(2,1)S(1)} %copy.10.gates_ref, bf16[6,128,768]{2,1,0:T(8,128)(2,1)S(1)} %bitcast.13, bf16[1152,768]{1,0:T(8,128)(2,1)S(1)} %bitcast.11), custom_call_target="tpu_custom_call" | custom-call | tf_op jit(solution)/shard_map/unpack/pallas_call | solution.py:335
  (30 shorter events, 0.1 us)
Async XLA Ops:
  0.6 15.9 %collective-permute-start = (bf16[128,2560]{1,0:T(8,128)(2,1)}, bf16[128,2560]{1,0:T(8,128)(2,1)S(1)}, u32[]{:S(2)}, u32[]{:S(2)}) collective-permute-start(bf16[128,2560]{1,0:T(8,128)(2,1)} %rest_0_.3), channel_id=1, source_target_pairs={{0,4},{1,5},{4,8},{5,9},{8,12},{9,13},{12,14},{13,15},{14,10},{15,... | collective-permute-start | bytes 1966088 | tf_op jit(solution)/shard_map/ppermute | solution.py:167
  0.9 15.8 %collective-permute-start.2 = (bf16[128,2560]{1,0:T(8,128)(2,1)}, bf16[128,2560]{1,0:T(8,128)(2,1)S(1)}, u32[]{:S(2)}, u32[]{:S(2)}) collective-permute-start(bf16[128,2560]{1,0:T(8,128)(2,1)} %rest_0_.3), channel_id=1, source_target_pairs={{0,2},{1,3},{4,0},{5,1},{8,4},{9,5},{12,8},{13,9},{14,12},{15,13},... | collective-permute-start | bytes 1966088 | tf_op jit(solution)/shard_map/ppermute | solution.py:168
  16.5 61.4 %copy-start.11 = (bf16[128,2560]{1,0:T(8,128)(2,1)}, bf16[128,2560]{1,0:T(8,128)(2,1)S(1)}, u32[]{:S(2)}) copy-start(bf16[128,2560]{1,0:T(8,128)(2,1)S(1)} %collective-permute-done.rest_1_) | copy-start | bytes 1966084
  16.5 19.7 %collective-permute-start.1 = (bf16[128,2560]{1,0:T(8,128)(2,1)S(1)}, bf16[128,2560]{1,0:T(8,128)(2,1)S(1)}, u32[]{:S(2)}, u32[]{:S(2)}) collective-permute-start(bf16[128,2560]{1,0:T(8,128)(2,1)S(1)} %collective-permute-done.rest_1_), channel_id=1, source_target_pairs={{0,4},{1,5},{4,8},{5,9},{8,12},{9,13},{12,14},{13,15},{14,10},{15,... | collective-permute-start | bytes 1966088 | tf_op jit(solution)/shard_map/ppermute | solution.py:167
  16.7 61.3 %copy-start.13 = (bf16[128,2560]{1,0:T(8,128)(2,1)}, bf16[128,2560]{1,0:T(8,128)(2,1)S(1)}, u32[]{:S(2)}) copy-start(bf16[128,2560]{1,0:T(8,128)(2,1)S(1)} %collective-permute-done.2.rest_2_) | copy-start | bytes 1966084
  16.7 19.5 %collective-permute-start.3 = (bf16[128,2560]{1,0:T(8,128)(2,1)S(1)}, bf16[128,2560]{1,0:T(8,128)(2,1)}, u32[]{:S(2)}, u32[]{:S(2)}) collective-permute-start(bf16[128,2560]{1,0:T(8,128)(2,1)S(1)} %collective-permute-done.2.rest_2_), channel_id=1, source_target_pairs={{0,2},{1,3},{4,0},{5,1},{8,4},{9,5},{12,8},{13,9},{14,12},{15,13},... | collective-permute-start | bytes 1966088 | tf_op jit(solution)/shard_map/ppermute | solution.py:168
  19.3 16.9 %all-to-all-start = ((s32[16,6,128]{2,1,0:T(8,128)}), s32[16,6,128]{2,1,0:T(8,128)S(1)}, u32[]{:S(2)}, u32[]{:S(2)}) async-start(s32[16,6,128]{2,1,0:T(8,128)} %broadcast_in_dim.13), calls=%async_computation | async-start | bytes 131072 | tf_op jit(solution)/shard_map/all_to_all | solution.py:163
  27.3 1.3 copy-start
  28.5 0.7 copy-start.6
  29.2 0.7 copy-start.7
  36.2 25.0 %copy-start.15 = (bf16[128,2560]{1,0:T(8,128)(2,1)}, bf16[128,2560]{1,0:T(8,128)(2,1)S(1)}, u32[]{:S(2)}) copy-start(bf16[128,2560]{1,0:T(8,128)(2,1)S(1)} %collective-permute-done.1.rest_3_) | copy-start | bytes 1966084
  36.2 16.0 %collective-permute-start.4 = (bf16[128,2560]{1,0:T(8,128)(2,1)S(1)}, bf16[128,2560]{1,0:T(8,128)(2,1)S(1)}, u32[]{:S(2)}, u32[]{:S(2)}) collective-permute-start(bf16[128,2560]{1,0:T(8,128)(2,1)S(1)} %collective-permute-done.1.rest_3_), channel_id=1, source_target_pairs={{0,4},{1,5},{4,8},{5,9},{8,12},{9,13},{12,14},{13,15},{14,10},{15,... | collective-permute-start | bytes 1966088 | tf_op jit(solution)/shard_map/ppermute | solution.py:167
  37.4 16.0 %collective-permute-start.5 = (bf16[128,2560]{1,0:T(8,128)(2,1)}, bf16[128,2560]{1,0:T(8,128)(2,1)S(1)}, u32[]{:S(2)}, u32[]{:S(2)}) collective-permute-start(bf16[128,2560]{1,0:T(8,128)(2,1)} %collective-permute-done.3.rest_4_), channel_id=1, source_target_pairs={{0,2},{1,3},{4,0},{5,1},{8,4},{9,5},{12,8},{13,9},{14,12},{15,13},... | collective-permute-start | bytes 1966088 | tf_op jit(solution)/shard_map/ppermute | solution.py:168
  52.2 25.7 %copy-start.2 = (bf16[128,2560]{1,0:T(8,128)(2,1)}, bf16[128,2560]{1,0:T(8,128)(2,1)S(1)}, u32[]{:S(2)}) copy-start(bf16[128,2560]{1,0:T(8,128)(2,1)S(1)} %collective-permute-done.4.rest_5_) | copy-start | bytes 1966084
  52.2 8.1 %collective-permute-start.6 = (bf16[64,2560]{1,0:T(8,128)(2,1)S(1)}, bf16[64,2560]{1,0:T(8,128)(2,1)}, u32[]{:S(2)}, u32[]{:S(2)}) collective-permute-start(bf16[64,2560]{1,0:T(8,128)(2,1)S(1)} %slice.8), channel_id=1, source_target_pairs={{0,4},{1,5},{4,8},{5,9},{8,12},{9,13},{12,14},{13,15},{14,10},{15,... | collective-permute-start | bytes 983048 | tf_op jit(solution)/shard_map/ppermute | solution.py:173
  53.4 24.6 %copy-start.4 = (bf16[128,2560]{1,0:T(8,128)(2,1)}, bf16[128,2560]{1,0:T(8,128)(2,1)S(1)}, u32[]{:S(2)}) copy-start(bf16[128,2560]{1,0:T(8,128)(2,1)S(1)} %collective-permute-done.5.rest_6_) | copy-start | bytes 1966084
  53.4 7.9 %collective-permute-start.7 = (bf16[64,2560]{1,0:T(8,128)(2,1)S(1)}, bf16[64,2560]{1,0:T(8,128)(2,1)}, u32[]{:S(2)}, u32[]{:S(2)}) collective-permute-start(bf16[64,2560]{1,0:T(8,128)(2,1)S(1)} %slice.9), channel_id=1, source_target_pairs={{0,2},{1,3},{4,0},{5,1},{8,4},{9,5},{12,8},{13,9},{14,12},{15,13},... | collective-permute-start | bytes 983048 | tf_op jit(solution)/shard_map/ppermute | solution.py:174
  61.3 7.0 %copy-start.9 = (bf16[128,2560]{1,0:T(8,128)(2,1)S(1)}, bf16[128,2560]{1,0:T(8,128)(2,1)}, u32[]{:S(2)}) copy-start(bf16[128,2560]{1,0:T(8,128)(2,1)} %rest_0_.3) | copy-start | bytes 1966084
  61.3 47.5 %all-to-all-start.2 = ((bf16[16,72,768]{2,1,0:T(8,128)(2,1)}), bf16[16,72,768]{2,1,0:T(8,128)(2,1)}, u32[]{:S(2)}, u32[]{:S(2)}) async-start(bf16[16,72,768]{2,1,0:T(8,128)(2,1)} %bitcast.9), calls=%async_computation.2 | async-start | bytes 3538944 | tf_op jit(solution)/shard_map/all_to_all | solution.py:368
  68.2 2.2 %collective-permute-start.8 = (bf16[128,2560]{1,0:T(8,128)(2,1)S(1)}, bf16[128,2560]{1,0:T(8,128)(2,1)S(1)}, u32[]{:S(2)}, u32[]{:S(2)}) collective-permute-start(bf16[128,2560]{1,0:T(8,128)(2,1)S(1)} %copy-done.9), channel_id=1, source_target_pairs={{0,1},{1,0},{2,3},{3,2},{4,5},{5,4},{6,7},{7,6},{8,9},{9,8},{10,11... | collective-permute-start | bytes 1966088 | tf_op jit(solution)/shard_map/ppermute | solution.py:178
  68.7 3.6 %collective-permute-start.10 = (bf16[128,2560]{1,0:T(8,128)(2,1)S(1)}, bf16[128,2560]{1,0:T(8,128)(2,1)S(1)}, u32[]{:S(2)}, u32[]{:S(2)}) collective-permute-start(bf16[128,2560]{1,0:T(8,128)(2,1)S(1)} %collective-permute-done.2.rest_2_), channel_id=1, source_target_pairs={{0,1},{1,0},{2,3},{3,2},{4,5},{5,4},{6,7},{7,6},{8,9},{9,8},{10,11... | collective-permute-start | bytes 1966088 | tf_op jit(solution)/shard_map/ppermute | solution.py:178
  68.8 6.3 %collective-permute-start.9 = (bf16[128,2560]{1,0:T(8,128)(2,1)S(1)}, bf16[128,2560]{1,0:T(8,128)(2,1)S(1)}, u32[]{:S(2)}, u32[]{:S(2)}) collective-permute-start(bf16[128,2560]{1,0:T(8,128)(2,1)S(1)} %collective-permute-done.rest_1_), channel_id=1, source_target_pairs={{0,1},{1,0},{2,3},{3,2},{4,5},{5,4},{6,7},{7,6},{8,9},{9,8},{10,11... | collective-permute-start | bytes 1966088 | tf_op jit(solution)/shard_map/ppermute | solution.py:178
  69.2 6.3 %collective-permute-start.11 = (bf16[128,2560]{1,0:T(8,128)(2,1)}, bf16[128,2560]{1,0:T(8,128)(2,1)S(1)}, u32[]{:S(2)}, u32[]{:S(2)}) collective-permute-start(bf16[128,2560]{1,0:T(8,128)(2,1)} %copy-done.15), channel_id=1, source_target_pairs={{0,1},{1,0},{2,3},{3,2},{4,5},{5,4},{6,7},{7,6},{8,9},{9,8},{10,11... | collective-permute-start | bytes 1966088 | tf_op jit(solution)/shard_map/ppermute | solution.py:178
  69.3 7.5 %collective-permute-start.12 = (bf16[128,2560]{1,0:T(8,128)(2,1)}, bf16[128,2560]{1,0:T(8,128)(2,1)}, u32[]{:S(2)}, u32[]{:S(2)}) collective-permute-start(bf16[128,2560]{1,0:T(8,128)(2,1)} %collective-permute-done.3.rest_4_), channel_id=1, source_target_pairs={{0,1},{1,0},{2,3},{3,2},{4,5},{5,4},{6,7},{7,6},{8,9},{9,8},{10,11... | collective-permute-start | bytes 1966088 | tf_op jit(solution)/shard_map/ppermute | solution.py:178
  70.4 4.7 %copy-start.18 = (bf16[128,2560]{1,0:T(8,128)(2,1)}, bf16[128,2560]{1,0:T(8,128)(2,1)S(1)}, u32[]{:S(2)}) copy-start(bf16[128,2560]{1,0:T(8,128)(2,1)S(1)} %collective-permute-done.8.rest_9_) | copy-start | bytes 1966084
  70.4 7.5 %collective-permute-start.13 = (bf16[128,2560]{1,0:T(8,128)(2,1)S(1)}, bf16[128,2560]{1,0:T(8,128)(2,1)}, u32[]{:S(2)}, u32[]{:S(2)}) collective-permute-start(bf16[128,2560]{1,0:T(8,128)(2,1)S(1)} %collective-permute-done.4.rest_5_), channel_id=1, source_target_pairs={{0,1},{1,0},{2,3},{3,2},{4,5},{5,4},{6,7},{7,6},{8,9},{9,8},{10,11... | collective-permute-start | bytes 1966088 | tf_op jit(solution)/shard_map/ppermute | solution.py:178
  72.3 3.2 %copy-start.19 = (bf16[128,2560]{1,0:T(8,128)(2,1)}, bf16[128,2560]{1,0:T(8,128)(2,1)S(1)}, u32[]{:S(2)}) copy-start(bf16[128,2560]{1,0:T(8,128)(2,1)S(1)} %collective-permute-done.10.rest_11_) | copy-start | bytes 1966084
  72.3 5.6 %collective-permute-start.14 = (bf16[128,2560]{1,0:T(8,128)(2,1)S(1)}, bf16[128,2560]{1,0:T(8,128)(2,1)}, u32[]{:S(2)}, u32[]{:S(2)}) collective-permute-start(bf16[128,2560]{1,0:T(8,128)(2,1)S(1)} %collective-permute-done.5.rest_6_), channel_id=1, source_target_pairs={{0,1},{1,0},{2,3},{3,2},{4,5},{5,4},{6,7},{7,6},{8,9},{9,8},{10,11... | collective-permute-start | bytes 1966088 | tf_op jit(solution)/shard_map/ppermute | solution.py:178
  75.1 0.8 copy-start.20
  75.1 2.0 %collective-permute-start.15 = (bf16[64,2560]{1,0:T(8,128)(2,1)}, bf16[64,2560]{1,0:T(8,128)(2,1)}, u32[]{:S(2)}, u32[]{:S(2)}) collective-permute-start(bf16[64,2560]{1,0:T(8,128)(2,1)} %collective-permute-done.6.rest_7_), channel_id=1, source_target_pairs={{0,1},{1,0},{2,3},{3,2},{4,5},{5,4},{6,7},{7,6},{8,9},{9,8},{10,11... | collective-permute-start | bytes 983048 | tf_op jit(solution)/shard_map/ppermute | solution.py:178
  75.9 0.9 copy-start.21
  75.9 2.0 %collective-permute-start.16 = (bf16[64,2560]{1,0:T(8,128)(2,1)}, bf16[64,2560]{1,0:T(8,128)(2,1)}, u32[]{:S(2)}, u32[]{:S(2)}) collective-permute-start(bf16[64,2560]{1,0:T(8,128)(2,1)} %collective-permute-done.7.rest_8_), channel_id=1, source_target_pairs={{0,1},{1,0},{2,3},{3,2},{4,5},{5,4},{6,7},{7,6},{8,9},{9,8},{10,11... | collective-permute-start | bytes 983048 | tf_op jit(solution)/shard_map/ppermute | solution.py:178
  78.0 1.1 copy-start.16
  98.2 15.5 %copy-start.8 = (bf16[128,6]{0,1:T(8,128)(2,1)S(1)}, bf16[128,6]{0,1:T(8,128)(2,1)}, u32[]{:S(2)}) copy-start(bf16[128,6]{0,1:T(8,128)(2,1)} %param.9) | copy-start | bytes 4612
  108.8 45.3 %all-to-all-start.1 = ((bf16[16,72,768]{2,1,0:T(8,128)(2,1)}), bf16[16,72,768]{2,1,0:T(8,128)(2,1)S(1)}, u32[]{:S(2)}, u32[]{:S(2)}) async-start(bf16[16,72,768]{2,1,0:T(8,128)(2,1)} %upstream.1), calls=%async_computation.1 | async-start | bytes 3538944 | tf_op jit(solution)/shard_map/all_to_all | solution.py:372
  114.6 1.1 copy-start.3
  115.7 1.1 copy-start.5
  116.8 1.1 copy-start.10
  117.9 1.1 copy-start.12
  119.0 1.1 copy-start.14
  120.1 1.1 copy-start.17
  121.2 32.9 %copy-start.1 = (bf16[128,6,768]{2,0,1:T(8,128)(2,1)S(1)}, bf16[128,6,768]{2,0,1:T(8,128)(2,1)}, u32[]{:S(2)}) copy-start(bf16[128,6,768]{2,0,1:T(8,128)(2,1)} %param.7) | copy-start | bytes 3538948

commit v3 on v1

--- a/solution.py
+++ b/solution.py
@@ -8,7 +8,7 @@
 from jax.sharding import PartitionSpec as P
 
 F32, BF16, I32 = jnp.float32, jnp.bfloat16, jnp.int32
-VMEM_LIMIT = 48 * 1024 * 1024
+VMEM_LIMIT = 62 * 1024 * 1024
 
 
 def whole(memory_space=pltpu.VMEM):
@@ -33,7 +33,7 @@
         place_ref[k : k + 1, :] = jnp.sum(
             jnp.where(ids_ref[k : k + 1, :] == expert, target, 0), axis=0, keepdims=True
         )
-        table[k * tokens : (k + 1) * tokens, :] = hidden_ref[:, k, :]
+        table[k * tokens : (k + 1) * tokens, :] = hidden_ref[k]
     rows = out_ref.shape[0]
     step = 128
     for first in range(0, rows, step):
@@ -47,8 +47,8 @@
         ).astype(BF16)
 
 
-def pack(ids_t, gates_t, saved_hidden, experts, capacity):
-    tokens, top_count, hidden_units = saved_hidden.shape
+def pack(ids_t, gates_t, hidden_t, experts, capacity):
+    top_count, tokens, hidden_units = hidden_t.shape
     return pl.pallas_call(
         functools.partial(pack_kernel, experts, capacity),
         out_shape=(
@@ -63,7 +63,7 @@
         ],
         compiler_params=pltpu.CompilerParams(vmem_limit_bytes=VMEM_LIMIT),
         name="pack",
-    )(ids_t, gates_t, saved_hidden)
+    )(ids_t, gates_t, hidden_t)
 
 
 def source_rank(ids, expert, tokens):
@@ -144,54 +144,394 @@
     )(scalars, ids_all, recv_hidden, grads)
 
 
-def unpack_kernel(place_ref, gates_ref, hidden_ref, back_ref, grad_ref, gate_ref, select):
+RING = 8
+ID_ROWS = 8
+PARTS = 4
+UNPACK_FLOPS = 40_000_000_000
+OFFSETS = (0, -1, 1, -2, 2, -3, 3, 4)
+SWAP = [(i, i ^ 1) for i in range(16)]
+
+
+def ring_device(position, core):
+    z, y = (position, 0) if position < 4 else (7 - position, 1)
+    return (z * 2 + y) * 2 + core
+
+
+def ring_shift(step):
+    return [
+        (ring_device(p, core), ring_device((p + step) % RING, core))
+        for p in range(RING)
+        for core in range(2)
+    ]
+
+
+def ring_position(device):
+    z, y = device >> 2, (device >> 1) & 1
+    return jnp.where(y == 0, z, 7 - z)
+
+
+def ring_pack_kernel(capacity, me_ref, ids_ref, gates_ref, hidden_ref, *rest):
+    outs, (place_ref, table, select, blocks, sems) = rest[:RING], rest[RING:]
+    top_count, tokens = ids_ref.shape
+    experts = 2 * RING
+    expert = lax.broadcasted_iota(I32, (experts, tokens), 0)
+    named = jnp.zeros((experts, tokens), F32)
+    for k in range(top_count):
+        named = named + (ids_ref[k : k + 1, :] == expert).astype(F32)
+    rank = jnp.dot(named.astype(BF16), earlier(tokens), preferred_element_type=F32).astype(I32)
+    me = me_ref[0]
+    target = (ring_position(expert) * 2 + ((expert & 1) ^ (me & 1))) * capacity + rank
+    for k in range(top_count):
+        place_ref[k : k + 1, :] = jnp.sum(
+            jnp.where(ids_ref[k : k + 1, :] == expert, target, 0), axis=0, keepdims=True
+        )
+        table[k * tokens : (k + 1) * tokens, :] = hidden_ref[k]
+    step = 2 * capacity
+    copies = []
+    for d in range(RING):
+        row = lax.broadcasted_iota(I32, (step, tokens), 0) + ((ring_position(me) + d) & 7) * step
+        for k in range(top_count):
+            select[:, k * tokens : (k + 1) * tokens] = jnp.where(
+                place_ref[k : k + 1, :] == row, gates_ref[k : k + 1, :].astype(F32), 0.0
+            ).astype(BF16)
+        blocks[d] = jnp.dot(select[...], table[...], preferred_element_type=F32).astype(BF16)
+        copies.append(pltpu.make_async_copy(blocks.at[d], outs[d], sems.at[d]))
+        copies[-1].start()
+    for copy in copies:
+        copy.wait()
+
+
+def ring_pack(me, ids_t, gates_t, hidden_t, capacity):
+    top_count, tokens, hidden_units = hidden_t.shape
+    block = jax.ShapeDtypeStruct((2 * capacity, hidden_units), BF16)
+    *blocks, place = pl.pallas_call(
+        functools.partial(ring_pack_kernel, capacity),
+        out_shape=(block,) * RING + (jax.ShapeDtypeStruct((top_count, tokens), I32),),
+        in_specs=[whole(pltpu.SMEM)] + [whole()] * 3,
+        out_specs=(whole(pltpu.HBM),) * RING + (whole(),),
+        scratch_shapes=[
+            pltpu.VMEM((top_count * tokens, hidden_units), BF16),
+            pltpu.VMEM((2 * capacity, top_count * tokens), BF16),
+            pltpu.VMEM((RING, 2 * capacity, hidden_units), BF16),
+            pltpu.SemaphoreType.DMA((RING,)),
+        ],
+        compiler_params=pltpu.CompilerParams(vmem_limit_bytes=VMEM_LIMIT),
+        cost_estimate=pl.CostEstimate(flops=3_000_000_000, bytes_accessed=5_000_000, transcendentals=0),
+        name="pack",
+    )(me, ids_t, gates_t, hidden_t)
+    return blocks, place
+
+
+def both_ranks(ids, me, capacity, tokens):
+    own = source_rank(ids, me, tokens)
+    other = source_rank(ids, me ^ 1, tokens)
+    return own, jnp.where(other >= 0, other + capacity, -1)
+
+
+def load(refs, buffer, sems, first):
+    copies, at = [], 0
+    for n, ref in enumerate(refs):
+        copies.append(
+            pltpu.make_async_copy(ref, buffer.at[pl.ds(at, ref.shape[0])], sems.at[first + n])
+        )
+        copies[-1].start()
+        at += ref.shape[0]
+    return copies
+
+
+def load_pieces(refs, grads, ids, sems, first):
+    tokens = ids.shape[2]
+    rows, routes, at = [], [], 0
+    for n, ref in enumerate(refs):
+        extra = ref.shape[0] % 16
+        count = ref.shape[0] - extra
+        rows.append(
+            pltpu.make_async_copy(
+                ref.at[pl.ds(0, count)], grads.at[pl.ds(at, count)], sems.at[first + 2 * n]
+            )
+        )
+        at += count
+        if extra:
+            routes.append(
+                pltpu.make_async_copy(
+                    ref.at[pl.ds(count, extra), pl.ds(0, tokens)],
+                    ids.at[at // tokens - 1],
+                    sems.at[first + 2 * n + 1],
+                )
+            )
+    for copy in routes + rows:
+        copy.start()
+    return routes, rows
+
+
+def ring_upstream_kernel(capacity, offsets, pieces, me_ref, own_ref, other_ref, *rest):
+    blocks = len(offsets)
+    grad_refs, (out_ref, weights, grads, ids, dense, rows, sems, out_sems) = rest[:pieces], rest[-8:]
+    tokens = ids.shape[2]
+    me = me_ref[0]
+    routes, loads = load_pieces(grad_refs, grads, ids, sems, 2)
+    loads += routes
+    weight_loads = [
+        pltpu.make_async_copy(own_ref, weights.at[0], sems.at[0]),
+        pltpu.make_async_copy(other_ref, weights.at[1], sems.at[1]),
+    ]
+    for copy in weight_loads:
+        copy.start()
+    for copy in loads:
+        copy.wait()
+    for i in range(2):
+        weight_loads[i].wait()
+        product = lax.dot_general(
+            grads[...], weights[i], (((1,), (1,)), ((), ())), preferred_element_type=F32
+        ).astype(BF16)
+        for b in range(blocks):
+            dense[b, i * tokens : (i + 1) * tokens, :] = product[b * tokens : (b + 1) * tokens, :]
+    row = lax.broadcasted_iota(I32, (2 * capacity, 2 * tokens), 0)
+    copies = []
+    for b, offset in enumerate(offsets):
+        ranks = both_ranks(ids[b].astype(F32).astype(I32), me, capacity, tokens)
+        choose = (jnp.concatenate(ranks, axis=1) == row).astype(F32).astype(BF16)
+        rows[b] = jnp.dot(choose, dense[b], preferred_element_type=F32).astype(BF16)
+        goal = out_ref.at[(ring_position(me) + offset + RING) & 7]
+        copies.append(pltpu.make_async_copy(rows.at[b], goal, out_sems.at[b]))
+        copies[-1].start()
+    for copy in copies:
+        copy.wait()
+
+
+def ring_upstream(me, tokens, offsets, pieces, so_far, own_weight, other_weight, capacity):
+    hidden_units, width = own_weight.shape
+    blocks = len(offsets)
+    return pl.pallas_call(
+        functools.partial(ring_upstream_kernel, capacity, offsets, len(pieces)),
+        out_shape=jax.ShapeDtypeStruct((RING, 2 * capacity, hidden_units), BF16),
+        in_specs=[whole(pltpu.SMEM)] + [whole(pltpu.HBM)] * (2 + len(pieces) + len(so_far)),
+        out_specs=whole(pltpu.HBM),
+        input_output_aliases={3 + len(pieces): 0} if so_far else {},
+        scratch_shapes=[
+            pltpu.VMEM((2, hidden_units, width), BF16),
+            pltpu.VMEM((blocks * tokens, width), BF16),
+            pltpu.VMEM((blocks, ID_ROWS, tokens), BF16),
+            pltpu.VMEM((blocks, 2 * tokens, hidden_units), BF16),
+            pltpu.VMEM((blocks, 2 * capacity, hidden_units), BF16),
+            pltpu.SemaphoreType.DMA((2 + 2 * len(pieces),)),
+            pltpu.SemaphoreType.DMA((blocks,)),
+        ],
+        compiler_params=pltpu.CompilerParams(vmem_limit_bytes=VMEM_LIMIT),
+        cost_estimate=pl.CostEstimate(
+            flops=4 * blocks * tokens * hidden_units * width,
+            bytes_accessed=2 * (blocks * tokens + 2 * hidden_units) * width,
+            transcendentals=0,
+        ),
+        name="upstream",
+    )(me, own_weight, other_weight, *pieces, *so_far)
+
+
+def ring_weight_kernel(capacity, other, pieces, me_ref, *rest):
+    grad_refs, hidden_refs = rest[:pieces], rest[pieces : pieces + RING]
+    outs, (grads, ids, hidden, dense, sems) = rest[pieces + RING : -5], rest[-5:]
+    tokens = ids.shape[2]
+    me = me_ref[0]
+    routes, grad_loads = load_pieces(grad_refs, grads, ids, sems, 0)
+    loads = [
+        pltpu.make_async_copy(ref, hidden.at[q], sems.at[2 * pieces + q])
+        for q, ref in enumerate(hidden_refs)
+    ]
+    for copy in loads:
+        copy.start()
+    for copy in routes + loads:
+        copy.wait()
+    row = lax.broadcasted_iota(I32, (2 * capacity, tokens), 0)
+    for q in range(RING):
+        rank = both_ranks(ids[q].astype(F32).astype(I32), me, capacity, tokens)[other]
+        choose = (rank == row).astype(F32).astype(BF16)
+        dense[:, q * tokens : (q + 1) * tokens] = lax.dot_general(
+            hidden[q], choose, (((0,), (0,)), ((), ())), preferred_element_type=F32
+        ).astype(BF16)
+    for copy in grad_loads:
+        copy.wait()
+    width = grads.shape[1]
+    step = 256
+
+    @pl.loop(0, width // step)
+    def _(n):
+        at = pl.ds(pl.multiple_of(n * step, step), step)
+        total = jnp.dot(dense[...], grads[:, at], preferred_element_type=F32)
+        height = total.shape[0] // len(outs)
+        for part, part_ref in enumerate(outs):
+            part_ref[:, at] = total[part * height : (part + 1) * height].astype(BF16)
+
+
+def ring_weight_sum(me, tokens, pieces, hidden, other, capacity):
+    width = pieces[0].shape[1]
+    hidden_units = hidden[0].shape[1]
+    result = jax.ShapeDtypeStruct((hidden_units // PARTS, width), BF16)
+    return pl.pallas_call(
+        functools.partial(ring_weight_kernel, capacity, other, len(pieces)),
+        out_shape=(result,) * PARTS,
+        in_specs=[whole(pltpu.SMEM)] + [whole(pltpu.HBM)] * (len(pieces) + RING),
+        out_specs=(whole(),) * PARTS,
+        scratch_shapes=[
+            pltpu.VMEM((RING * tokens, width), BF16),
+            pltpu.VMEM((RING, ID_ROWS, tokens), BF16),
+            pltpu.VMEM((RING, 2 * capacity, hidden_units), BF16),
+            pltpu.VMEM((hidden_units, RING * tokens), BF16),
+            pltpu.SemaphoreType.DMA((2 * len(pieces) + RING,)),
+        ],
+        compiler_params=pltpu.CompilerParams(vmem_limit_bytes=VMEM_LIMIT),
+        cost_estimate=pl.CostEstimate(flops=1_000_000, bytes_accessed=1_000_000, transcendentals=0),
+        name="weight_other" if other else "weight_own",
+    )(me, *pieces, *hidden)
+
+
+def add_kernel(trained_ref, *rest):
+    parts = len(rest) // 2
+    own_refs, came_refs, out_ref = rest[:parts], rest[parts : 2 * parts], rest[-1]
+    trained, at = trained_ref[0].astype(F32), 0
+    for own_ref, came_ref in zip(own_refs, came_refs):
+        height = own_ref.shape[0]
+        total = own_ref[...].astype(F32) + came_ref[...].astype(F32)
+        out_ref[at : at + height, :] = (total * trained).astype(BF16)
+        at += height
+
+
+def add_parts(trained, own, came):
+    height, width = own[0].shape
+    step = 512
+    part = pl.BlockSpec((height, step), lambda n: (0, n))
+    rows = height * len(own)
+    return pl.pallas_call(
+        add_kernel,
+        out_shape=jax.ShapeDtypeStruct((rows, width), BF16),
+        grid=(width // step,),
+        in_specs=[whole(pltpu.SMEM)] + [part] * (2 * len(own)),
+        out_specs=pl.BlockSpec((rows, step), lambda n: (0, n)),
+        compiler_params=pltpu.CompilerParams(vmem_limit_bytes=VMEM_LIMIT),
+        cost_estimate=pl.CostEstimate(flops=1_000_000, bytes_accessed=1_000_000, transcendentals=0),
+        name="weight_add",
+    )(trained, *own, *came)
+
+
+def unpack_kernel(place_ref, gates_ref, hidden_ref, *rest):
+    back_refs, (grad_ref, gate_ref, select, sums, back, sems) = rest[:-6], rest[-6:]
     tokens, top_count = place_ref.shape
-    rows = back_ref.shape[0]
+    rows = back.shape[0]
+    copies = load(back_refs, back, sems, 0)
+    lane = lax.broadcasted_iota(I32, (tokens, rows), 1)
     for k in range(top_count):
-        lane = lax.broadcasted_iota(I32, (tokens, rows), 1)
-        select[...] = (place_ref[:, k : k + 1] == lane).astype(F32).astype(BF16)
-        up = jnp.dot(select[...], back_ref[...], preferred_element_type=F32)
-        grad_ref[:, k, :] = (gates_ref[:, k : k + 1].astype(F32) * up).astype(BF16)
-        gate_ref[:, k : k + 1] = jnp.sum(
-            hidden_ref[:, k, :].astype(F32) * up, axis=1, keepdims=True
-        ).astype(BF16)
-
-
-def unpack(place, gates, saved_hidden, back):
-    tokens, top_count, hidden_units = saved_hidden.shape
+        select[k * tokens : (k + 1) * tokens, :] = (
+            (place_ref[:, k : k + 1] == lane).astype(F32).astype(BF16)
+        )
+    sums[...] = jnp.zeros_like(sums)
+    for copy in copies:
+        copy.wait()
+    up = jnp.dot(select[...], back[...], preferred_element_type=F32)
+    for k in range(top_count):
+        mine = up[k * tokens : (k + 1) * tokens, :]
+        grad_ref[k] = (gates_ref[:, k : k + 1].astype(F32) * mine).astype(BF16)
+        sums[:, k : k + 1] = jnp.sum(hidden_ref[k].astype(F32) * mine, axis=1, keepdims=True)
+    gate_ref[...] = sums[...].T[:top_count, :].astype(BF16)
+
+
+def unpack(place, gates, hidden_t, back):
+    top_count, tokens, hidden_units = hidden_t.shape
+    rows = sum(block.shape[0] for block in back)
     return pl.pallas_call(
         unpack_kernel,
         out_shape=(
-            jax.ShapeDtypeStruct((tokens, top_count, hidden_units), BF16),
-            jax.ShapeDtypeStruct((tokens, top_count), BF16),
-        ),
-        in_specs=[whole()] * 4,
+            jax.ShapeDtypeStruct((top_count, tokens, hidden_units), BF16),
+            jax.ShapeDtypeStruct((top_count, tokens), BF16),
+        ),
+        in_specs=[whole()] * 3 + [whole(pltpu.HBM)] * len(back),
         out_specs=(whole(), whole()),
-        scratch_shapes=[pltpu.VMEM((tokens, back.shape[0]), BF16)],
-        compiler_params=pltpu.CompilerParams(vmem_limit_bytes=VMEM_LIMIT),
+        scratch_shapes=[
+            pltpu.VMEM((top_count * tokens, rows), BF16),
+            pltpu.VMEM((tokens, 128), F32),
+            pltpu.VMEM((rows, hidden_units), BF16),
+            pltpu.SemaphoreType.DMA((len(back),)),
+        ],
+        compiler_params=pltpu.CompilerParams(vmem_limit_bytes=VMEM_LIMIT),
+        cost_estimate=pl.CostEstimate(
+            flops=UNPACK_FLOPS, bytes_accessed=6 * rows * hidden_units, transcendentals=0
+        ),
         name="unpack",
-    )(place, gates, saved_hidden, back)
-
-
-def local(out_grad, saved_hidden, expert_ids, gate_weights, trained, down_weight):
+    )(place, gates, hidden_t, *back)
+
+
+def ring_exchange(out_grad, hidden_t, ids_t, gates_t, scalars, weight, capacity):
+    def send(value, step):
+        return lax.ppermute(value, "expert", ring_shift(step))
+
+    me = scalars[:1]
+    tokens, width = out_grad.shape
+    half = tokens // 2
+    spare = ((0, ID_ROWS - ids_t.shape[0]), (0, width - tokens))
+    block = jnp.concatenate([out_grad, jnp.pad(ids_t.astype(BF16), spare, constant_values=-1)])
+    packed, place = ring_pack(me, ids_t, gates_t, hidden_t, capacity)
+    other_weight = lax.ppermute(weight, "expert", SWAP)
+    barrier = lax.optimization_barrier
+    hidden = [None] * RING
+
+    def send_hidden(*chosen):
+        for q in chosen:
+            hidden[q] = send(packed[-OFFSETS[q] % RING], -OFFSETS[q] % RING)
+
+    ahead, behind = send(block, 1), send(block, -1)
+    ahead, behind, *packed = barrier((ahead, behind, *packed))
+    pieces = [block, ahead, behind]
+    hidden[0] = packed[0]
+    ahead, behind = send(ahead, 1), send(behind, -1)
+    ahead, behind, other_weight = barrier((ahead, behind, other_weight))
+    pieces += [ahead, behind]
+    upstream_of = functools.partial(
+        ring_upstream, me, tokens, own_weight=weight, other_weight=other_weight, capacity=capacity
+    )
+    ahead, behind = send(ahead, 1), send(behind, -1)
+    send_hidden(3, 4)
+    up = upstream_of(OFFSETS[:5], pieces[:5], ())
+    ahead, behind, hidden[3], hidden[4], up = barrier((ahead, behind, hidden[3], hidden[4], up))
+    pieces += [ahead, behind]
+    pieces += [send(ahead[:half], 1), send(behind[half:], -1)]
+    send_hidden(5, 6, 7, 1, 2)
+    up = upstream_of(OFFSETS[5:], pieces[5:], (up,))
+    *hidden, up = barrier((*hidden, up))
+    groups = [[ring_device(p, core) for p in range(RING)] for core in range(2)]
+    back = lax.all_to_all(up, "expert", 0, 0, axis_index_groups=groups, tiled=True)
+    theirs = ring_weight_sum(me, tokens, pieces, hidden, True, capacity)
+    came = [lax.ppermute(part, "expert", SWAP) for part in theirs]
+    own = ring_weight_sum(me, tokens, pieces, hidden, False, capacity)
+    weight_grad = add_parts(scalars[1:], own, came)
+    place, weight_grad = barrier((place, weight_grad))
+    return place, [back.reshape(-1, back.shape[2])], weight_grad
+
+
+def gather_exchange(out_grad, hidden_t, ids_t, gates_t, scalars, weight, capacity):
     experts = lax.axis_size("expert")
-    tokens, top_count, hidden_units = saved_hidden.shape
-    capacity = min(tokens, 3 * tokens * top_count // (2 * experts))
-    ids_t = expert_ids.T
-    me = lax.axis_index("expert").astype(I32)
+    hidden_units = weight.shape[0]
     ids_all = lax.all_gather(ids_t, "expert", axis=0)
+    packed, place = pack(ids_t, gates_t, hidden_t, experts, capacity)
     grads = lax.all_gather(out_grad, "expert", axis=0, tiled=True)
-    packed, place_t = pack(ids_t, gate_weights.T, saved_hidden, experts, capacity)
     recv_hidden = lax.all_to_all(
         packed.reshape(experts, capacity, hidden_units), "expert", 0, 0, tiled=True
     )
-    up = upstream(me[None], ids_all, grads, down_weight[0], capacity)
+    up = upstream(scalars[:1], ids_all, grads, weight, capacity)
     back = lax.all_to_all(up, "expert", 0, 0, tiled=True)
-    weight_grad = weight_sum(jnp.stack([me, trained[0]]), ids_all, recv_hidden, grads)
-    hidden_grad, gate_grad = unpack(
-        place_t.T, gate_weights, saved_hidden, back.reshape(experts * capacity, hidden_units)
+    weight_grad = weight_sum(scalars, ids_all, recv_hidden, grads)
+    return place, [back.reshape(experts * capacity, hidden_units)], weight_grad
+
+
+def local(out_grad, saved_hidden, expert_ids, gate_weights, trained, down_weight):
+    experts = lax.axis_size("expert")
+    tokens, top_count, _ = saved_hidden.shape
+    capacity = min(tokens, 3 * tokens * top_count // (2 * experts))
+    hidden_t = saved_hidden.transpose(1, 0, 2)
+    scalars = jnp.stack([lax.axis_index("expert").astype(I32), trained[0]])
+    exchange = ring_exchange if experts == 2 * RING else gather_exchange
+    place, back, weight_grad = exchange(
+        out_grad, hidden_t, expert_ids.T, gate_weights.T, scalars, down_weight[0], capacity
     )
-    return hidden_grad, gate_grad, weight_grad[None]
+    hidden_grad, gate_grad = unpack(place.T, gate_weights, hidden_t, back)
+    return hidden_grad.transpose(1, 0, 2), gate_grad.T, weight_grad[None]
 
 
 def solution(mesh):

time: 221 us -> 153 us (0.69)
  blocking collectives: 73 us -> 0 us
  between operations: 14.8 us -> 1.64 us
  starting transfers between devices: 13.2 us -> 26.1 us
  Pallas kernels: 52.2 us -> 63.3 us
  local copies, waits for them, and re-layouts: 8.68 us -> 3.44 us
  waiting for transfers between devices: 58.1 us -> 55.4 us
    all_gather x1 -> x0, blocking collectives: 73 us -> none  [local(): ids_all = lax.all_gather(ids_t, 'expert', axis=0)]
    ppermute x0 -> x20, waiting for transfers between devices: none -> 55.4 us  [the longest x15 55.4 us: send(): return lax.ppermute(value, 'expert', ring_shift(step))]
    all_gather x1 -> x0, waiting for transfers between devices: 34.2 us -> none  [local(): grads = lax.all_gather(out_grad, 'expert', axis=0, tiled=True)]
    all_to_all x2 -> x1, waiting for transfers between devices: 23.2 us -> 0.01 us  [ring_exchange(): lax.all_to_all(up, 'expert', 0, 0, axis_index_groups=groups, tiled=True)]
    ppermute x0 -> x20, starting transfers between devices: none -> 22.4 us  [the longest x15 14.9 us: send(): return lax.ppermute(value, 'expert', ring_shift(step))]
    pallas_call x4 -> x7, Pallas kernels: 52.2 us -> 63.3 us  [the longest x2 25.3 us: ring_weight_sum(): pl.pallas_call(functools.partial(ring_weight_kernel, capacity, other, len...]
    all_to_all x2 -> x1, starting transfers between devices: 13.2 us -> 3.72 us  [ring_exchange(): lax.all_to_all(up, 'expert', 0, 0, axis_index_groups=groups, tiled=True)]
    unnamed x14 -> x23, local copies, waits for them, and re-layouts: 8.57 us -> 2.67 us
  transfers between devices with their start and end apart: 3 -> 21, of which waited for: 2 -> 7; matrix products, arithmetic and copies ran while one was open for 1% -> 2% of each run, Pallas kernels for 21% -> 38%
where the time goes in v3:
time: 153 us; the launch traced here: 152 us
  Pallas kernels  63.3 us (41%)
  waiting for transfers between devices  55.4 us (36%)
  starting transfers between devices  26.1 us (17%)
  local copies, waits for them, and re-layouts  3.44 us (2%)
  other arithmetic  1.82 us (1%)
  between operations  1.64 us (1%)
    ppermute x15, waiting for transfers between devices, send(): return lax.ppermute(value, 'expert', ring_shift(step))  55.4 us
    pallas_call x2, Pallas kernels, ring_weight_sum(): pl.pallas_call(functools.partial(ring_weight_kernel, capacity, other, len...  25.3 us
    pallas_call x2, Pallas kernels, ring_upstream(): pl.pallas_call(functools.partial(ring_upstream_kernel, capacity, offsets,...  20.7 us
    ppermute x15, starting transfers between devices, send(): return lax.ppermute(value, 'expert', ring_shift(step))  14.9 us
    pallas_call x1, Pallas kernels, add_parts(): pl.pallas_call(add_kernel, out_shape=jax.ShapeDtypeStruct((rows, width),...  7.05 us
    ppermute x4, starting transfers between devices, ring_exchange(): came = [lax.ppermute(part, 'expert', SWAP) for part in theirs]  6.73 us
    pallas_call x1, Pallas kernels, unpack(): pl.pallas_call(unpack_kernel, out_shape=(jax.ShapeDtypeStruct((top_count,...  5.65 us
    pallas_call x1, Pallas kernels, ring_pack(): pl.pallas_call(functools.partial(ring_pack_kernel, capacity), out_shape=(...  4.53 us
  transfers between devices with their start and end apart: 21, of which 7 were waited for; matrix products, arithmetic and copies ran while one was open for 2% of the time, Pallas kernels for 38%

profile of v3, /device:TPU:13, one launch (start us, length us, event | category | flops | bytes accessed | tf_op | source)
XLA Modules:
  0.0 151.7 jit_solution(10636112032560212500)
XLA Ops:
  0.6 0.7 collective-permute-start.4
  1.4 0.7 bitcast_convert_fusion
  2.1 1.1 fusion.1.rest_0_
  3.2 0.0 copy-start.2
  3.2 0.2 collective-permute-start
  3.4 1.3 collective-permute-start.1
  4.7 4.5 %pack.1 = (bf16[144,768]{1,0:T(8,128)(2,1)}, bf16[144,768]{1,0:T(8,128)(2,1)}, bf16[144,768]{1,0:T(8,128)(2,1)}, bf16[144,768]{1,0:T(8,128)(2,1)}, bf16[144,768]...) custom-call(s32[1]{0:T(128)} %bitcast.me_ref, ...), custom_call_target="tpu_custom_call" | custom-call | flops 3000000000 | bytes 5000000 | tf_op jit(solution)/shard_map/pack/pallas_call | solution.py:207
  9.3 0.0 copy-done.2
  9.3 11.3 %collective-permute-done.rest_1_ = bf16[136,2560]{1,0:T(8,128)(2,1)S(1)} collective-permute-done((bf16[136,2560]{1,0:T(8,128)(2,1)S(1)}, bf16[136,2560]{1,0:T(8,128)(2,1)S(1)}, u32[]{:S(2)}, u32[]{:S(2)}) %collective-permute-start) | collective-permute-done | bytes 696352 | tf_op jit(solution)/shard_map/ppermute | solution.py:463
  20.6 0.0 collective-permute-done.1.rest_2_
  20.6 0.2 collective-permute-start.2
  20.8 1.2 collective-permute-start.3
  22.1 14.8 %collective-permute-done.2.rest_3_ = bf16[136,2560]{1,0:T(8,128)(2,1)} collective-permute-done((bf16[136,2560]{1,0:T(8,128)(2,1)S(1)}, bf16[136,2560]{1,0:T(8,128)(2,1)}, u32[]{:S(2)}, u32[]{:S(2)}) %collective-permute-start.2) | collective-permute-done | bytes 696352 | tf_op jit(solution)/shard_map/ppermute | solution.py:463
  36.8 0.3 collective-permute-done.3.rest_4_
  37.2 0.0 collective-permute-done.4.other_ref
  37.2 0.0 copy-done.5
  37.2 0.8 collective-permute-start.5
  38.0 0.6 collective-permute-start.6
  38.6 1.8 %collective-permute-start.7 = (bf16[144,768]{1,0:T(8,128)(2,1)}, bf16[144,768]{1,0:T(8,128)(2,1)S(1)}, u32[]{:S(2)}, u32[]{:S(2)}) collective-permute-start(bf16[144,768]{1,0:T(8,128)(2,1)} %get-tuple-element.64), channel_id=1, source_target_pairs={{0,8},{1,9},{4,12},{5,13},{8,14},{9,15},{12,10},{13,11},{14,6},{15... | collective-permute-start | bytes 663560 | tf_op jit(solution)/shard_map/ppermute | solution.py:463
  40.5 0.5 collective-permute-start.8
  41.0 12.1 %upstream.2.rest_4_ = bf16[8,144,768]{2,1,0:T(8,128)(2,1)} custom-call(s32[1]{0:T(128)} %bitcast.me_ref, bf16[768,2560]{1,0:T(8,128)(2,1)} %bitcast.12, bf16[768,2560]{1,0:T(8,128)(2,1)} %collective-permute-done.4.other_ref, bf16[136,2560]{1,0:T(8,128)(2,1)} %copy-done.2, bf16[136,2560]{1,0:T(8,128)(2,1)} %copy-done.5, ...), custom_call_target="tpu_custom_call" | custom-call | flops 5033164800 | bytes 11141120 | tf_op jit(solution)/shard_map/upstream/pallas_call | solution.py:305
  53.1 4.4 %collective-permute-done.7.rest_12_ = bf16[144,768]{1,0:T(8,128)(2,1)S(1)} collective-permute-done((bf16[144,768]{1,0:T(8,128)(2,1)}, bf16[144,768]{1,0:T(8,128)(2,1)S(1)}, u32[]{:S(2)}, u32[]{:S(2)}) %collective-permute-start.7) | collective-permute-done | bytes 221216 | tf_op jit(solution)/shard_map/ppermute | solution.py:463
  57.6 5.5 %collective-permute-done.8.rest_13_ = bf16[144,768]{1,0:T(8,128)(2,1)S(1)} collective-permute-done((bf16[144,768]{1,0:T(8,128)(2,1)}, bf16[144,768]{1,0:T(8,128)(2,1)S(1)}, u32[]{:S(2)}, u32[]{:S(2)}) %collective-permute-start.8) | collective-permute-done | bytes 221216 | tf_op jit(solution)/shard_map/ppermute | solution.py:463
  63.0 0.0 collective-permute-done.5.rest_0_.rest_5_
  63.0 0.0 collective-permute-done.6.rest_1_.rest_6_
  63.0 0.7 copy-done.8
  63.7 0.4 collective-permute-start.10
  64.2 1.2 collective-permute-start.9
  65.3 0.1 collective-permute-start.11
  65.4 1.4 collective-permute-start.12
  66.8 1.6 %collective-permute-start.13 = (bf16[144,768]{1,0:T(8,128)(2,1)}, bf16[144,768]{1,0:T(8,128)(2,1)}, u32[]{:S(2)}, u32[]{:S(2)}) collective-permute-start(bf16[144,768]{1,0:T(8,128)(2,1)} %get-tuple-element.74), channel_id=1, source_target_pairs={{0,12},{1,13},{4,14},{5,15},{8,10},{9,11},{12,6},{13,7},{14,2},{15... | collective-permute-start | bytes 663560 | tf_op jit(solution)/shard_map/ppermute | solution.py:463
  68.4 1.8 %collective-permute-done.9.rest_2_.rest_7_ = bf16[64,2560]{1,0:T(8,128)(2,1)S(1)} collective-permute-done((bf16[64,2560]{1,0:T(8,128)(2,1)S(1)}, bf16[64,2560]{1,0:T(8,128)(2,1)S(1)}, u32[]{:S(2)}, u32[]{:S(2)}) %collective-permute-start.9) | collective-permute-done | bytes 327712 | tf_op jit(solution)/shard_map/ppermute | solution.py:463
  70.1 2.1 %collective-permute-start.14 = (bf16[144,768]{1,0:T(8,128)(2,1)}, bf16[144,768]{1,0:T(8,128)(2,1)}, u32[]{:S(2)}, u32[]{:S(2)}) collective-permute-start(bf16[144,768]{1,0:T(8,128)(2,1)} %get-tuple-element.75), channel_id=1, source_target_pairs={{0,10},{1,11},{4,6},{5,7},{8,2},{9,3},{12,0},{13,1},{14,4},{15,5},... | collective-permute-start | bytes 663560 | tf_op jit(solution)/shard_map/ppermute | solution.py:463
  72.3 0.0 collective-permute-done.10.rest_3_.rest_8_
  72.3 0.0 copy-done.4
  72.3 1.3 collective-permute-start.15
  73.6 0.0 copy-done.1
  73.6 0.0 copy-done
  73.6 0.0 copy-done.3
  73.6 8.6 %upstream.3 = bf16[8,144,768]{2,1,0:T(8,128)(2,1)} custom-call(s32[1]{0:T(128)} %bitcast.me_ref, bf16[768,2560]{1,0:T(8,128)(2,1)} %bitcast.13, bf16[768,2560]{1,0:T(8,128)(2,1)} %collective-permute-done.4.other_ref, bf16[136,2560]{1,0:T(8,128)(2,1)} %copy-done.1, bf16[136,2560]{1,0:T(8,128)(2,1)} %copy-done, ...), custom_call_target="tpu_custom_call", output_to_operand_aliasing={{}: (7, {})} | custom-call | flops 3019898880 | bytes 9830400 | tf_op jit(solution)/shard_map/upstream/pallas_call | solution.py:305
  82.2 0.0 copy-done.7
  82.2 0.0 collective-permute-done.11.rest_10_
  82.2 0.0 collective-permute-done.12.rest_11_
  82.2 0.0 collective-permute-done.13.rest_14_
  82.2 0.0 collective-permute-done.14.rest_15_
  82.2 17.3 %collective-permute-done.15.rest_16_ = bf16[144,768]{1,0:T(8,128)(2,1)} collective-permute-done((bf16[144,768]{1,0:T(8,128)(2,1)}, bf16[144,768]{1,0:T(8,128)(2,1)}, u32[]{:S(2)}, u32[]{:S(2)}) %collective-permute-start.15) | collective-permute-done | bytes 221216 | tf_op jit(solution)/shard_map/ppermute | solution.py:463
  99.6 3.7 %all-to-all-start = ((bf16[8,144,768]{2,1,0:T(8,128)(2,1)}), bf16[8,144,768]{2,1,0:T(8,128)(2,1)S(1)}, u32[]{:S(2)}, u32[]{:S(2)}) async-start(bf16[8,144,768]{2,1,0:T(8,128)(2,1)} %upstream.3), calls=%async_computation | async-start | bytes 3538944 | tf_op jit(solution)/shard_map/all_to_all | solution.py:499
  103.3 0.0 copy-start.10
  103.3 12.7 %weight_other.1 = (bf16[192,2560]{1,0:T(8,128)(2,1)}, bf16[192,2560]{1,0:T(8,128)(2,1)}, bf16[192,2560]{1,0:T(8,128)(2,1)}, bf16[192,2560]{1,0:T(8,128)(2,1)}) custom-call(s32[1]{0:T(128)} %bitcast.me_ref, bf16[136,2560]{1,0:T(8,128)(2,1)} %copy-done.2, bf16[136,2560]{1,0:T(8,128)(2,1)} %copy-done.5, bf16[136,2560]{1,0:T(8,128)(2,1)} %collective-permute-done.1.rest_2_, ...), custom_call_target="tpu_custom_call" | custom-call | flops 1000000 | bytes 1000000 | tf_op jit(solution)/shard_map/weight_other/pallas_call | solution.py:369
  116.0 6.1 %collective-permute-start.16 = (bf16[192,2560]{1,0:T(8,128)(2,1)}, bf16[192,2560]{1,0:T(8,128)(2,1)}, u32[]{:S(2)}, u32[]{:S(2)}) collective-permute-start(bf16[192,2560]{1,0:T(8,128)(2,1)} %get-tuple-element.90), channel_id=1, source_target_pairs={{0,1},{1,0},{2,3},{3,2},{4,5},{5,4},{6,7},{7,6},{8,9},{9,8},{10,11... | collective-permute-start | bytes 2949128 | tf_op jit(solution)/shard_map/ppermute | solution.py:501
  122.1 0.1 collective-permute-start.17
  122.2 0.4 collective-permute-start.18
  122.6 0.1 collective-permute-start.19
  122.7 0.7 copy.11.gates_ref
  124.1 12.7 %weight_own.1 = (bf16[192,2560]{1,0:T(8,128)(2,1)}, bf16[192,2560]{1,0:T(8,128)(2,1)}, bf16[192,2560]{1,0:T(8,128)(2,1)}, bf16[192,2560]{1,0:T(8,128)(2,1)}) custom-call(s32[1]{0:T(128)} %bitcast.me_ref, bf16[136,2560]{1,0:T(8,128)(2,1)} %copy-done.2, bf16[136,2560]{1,0:T(8,128)(2,1)} %copy-done.5, bf16[136,2560]{1,0:T(8,128)(2,1)} %collective-permute-done.1.rest_2_, ...), custom_call_target="tpu_custom_call" | custom-call | flops 1000000 | bytes 1000000 | tf_op jit(solution)/shard_map/weight_own/pallas_call | solution.py:369
  136.8 0.0 collective-permute-done.16.rest_4_
  136.8 0.0 collective-permute-done.17.rest_5_
  136.8 0.0 collective-permute-done.18.rest_6_
  136.8 0.0 collective-permute-done.19.rest_7_
  136.8 7.1 %weight_add.1 = bf16[768,2560]{1,0:T(8,128)(2,1)} custom-call(s32[1]{0:T(128)S(6)} %copy.13.trained_ref, bf16[192,2560]{1,0:T(8,128)(2,1)} %get-tuple-element.86.rest_0_, bf16[192,2560]{1,0:T(8,128)(2,1)} %get-tuple-element.87.rest_1_, bf16[192,2560]{1,0:T(8,128)(2,1)} %get-tuple-element.88.rest_2_, bf16[192,2560]{1,0:T(8,128)(2,1)} %get-tuple-element.89.rest_3_, ...), custom_call_target="tpu_custom_call" | custom-call | flops 1000000 | bytes 1000000 | tf_op jit(solution)/shard_map/weight_add/pallas_call | solution.py:403
  143.9 0.7 copy.10
  144.6 0.0 all-to-all-done
  144.6 1.2 copy-done.6
  145.8 5.6 %unpack.1 = (bf16[6,128,768]{2,1,0:T(8,128)(2,1)}, bf16[6,128]{1,0:T(8,128)(2,1)}) custom-call(s32[128,6]{1,0:T(8,128)} %bitcast.16, bf16[128,6]{1,0:T(8,128)(2,1)} %copy.11.gates_ref, bf16[6,128,768]{2,1,0:T(8,128)(2,1)} %bitcast.20, bf16[1152,768]{1,0:T(8,128)(2,1)} %bitcast.15), custom_call_target="tpu_custom_call" | custom-call | flops 40000000000 | bytes 5308416 | tf_op jit(solution)/shard_map/unpack/pallas_call | solution.py:439
  (13 shorter events, 0.1 us)
Async XLA Ops:
  0.6 36.5 %collective-permute-start.4 = (bf16[768,2560]{1,0:T(8,128)(2,1)}, bf16[768,2560]{1,0:T(8,128)(2,1)}, u32[]{:S(2)}, u32[]{:S(2)}) collective-permute-start(bf16[768,2560]{1,0:T(8,128)(2,1)} %bitcast.11), channel_id=1, source_target_pairs={{0,1},{1,0},{2,3},{3,2},{4,5},{5,4},{6,7},{7,6},{8,9},{9,8},{10,11... | collective-permute-start | bytes 11796488 | tf_op jit(solution)/shard_map/ppermute | solution.py:471
  3.2 6.1 %copy-start.2 = (bf16[136,2560]{1,0:T(8,128)(2,1)}, bf16[136,2560]{1,0:T(8,128)(2,1)S(1)}, u32[]{:S(2)}) copy-start(bf16[136,2560]{1,0:T(8,128)(2,1)S(1)} %fusion.1.rest_0_) | copy-start | bytes 2088964
  3.2 17.4 %collective-permute-start = (bf16[136,2560]{1,0:T(8,128)(2,1)S(1)}, bf16[136,2560]{1,0:T(8,128)(2,1)S(1)}, u32[]{:S(2)}, u32[]{:S(2)}) collective-permute-start(bf16[136,2560]{1,0:T(8,128)(2,1)S(1)} %fusion.1.rest_0_), channel_id=1, source_target_pairs={{0,4},{1,5},{4,8},{5,9},{8,12},{9,13},{12,14},{13,15},{14,10},{15,... | collective-permute-start | bytes 2088968 | tf_op jit(solution)/shard_map/ppermute | solution.py:463
  3.4 17.2 %collective-permute-start.1 = (bf16[136,2560]{1,0:T(8,128)(2,1)S(1)}, bf16[136,2560]{1,0:T(8,128)(2,1)}, u32[]{:S(2)}, u32[]{:S(2)}) collective-permute-start(bf16[136,2560]{1,0:T(8,128)(2,1)S(1)} %fusion.1.rest_0_), channel_id=1, source_target_pairs={{0,2},{1,3},{4,0},{5,1},{8,4},{9,5},{12,8},{13,9},{14,12},{15,13},... | collective-permute-start | bytes 2088968 | tf_op jit(solution)/shard_map/ppermute | solution.py:463
  20.6 16.6 %copy-start.5 = (bf16[136,2560]{1,0:T(8,128)(2,1)}, bf16[136,2560]{1,0:T(8,128)(2,1)S(1)}, u32[]{:S(2)}) copy-start(bf16[136,2560]{1,0:T(8,128)(2,1)S(1)} %collective-permute-done.rest_1_) | copy-start | bytes 2088964
  20.6 16.3 %collective-permute-start.2 = (bf16[136,2560]{1,0:T(8,128)(2,1)S(1)}, bf16[136,2560]{1,0:T(8,128)(2,1)}, u32[]{:S(2)}, u32[]{:S(2)}) collective-permute-start(bf16[136,2560]{1,0:T(8,128)(2,1)S(1)} %collective-permute-done.rest_1_), channel_id=1, source_target_pairs={{0,4},{1,5},{4,8},{5,9},{8,12},{9,13},{12,14},{13,15},{14,10},{15,... | collective-permute-start | bytes 2088968 | tf_op jit(solution)/shard_map/ppermute | solution.py:463
  20.8 16.3 %collective-permute-start.3 = (bf16[136,2560]{1,0:T(8,128)(2,1)}, bf16[136,2560]{1,0:T(8,128)(2,1)}, u32[]{:S(2)}, u32[]{:S(2)}) collective-permute-start(bf16[136,2560]{1,0:T(8,128)(2,1)} %collective-permute-done.1.rest_2_), channel_id=1, source_target_pairs={{0,2},{1,3},{4,0},{5,1},{8,4},{9,5},{12,8},{13,9},{14,12},{15,13},... | collective-permute-start | bytes 2088968 | tf_op jit(solution)/shard_map/ppermute | solution.py:463
  37.2 25.9 %collective-permute-start.5 = (bf16[136,2560]{1,0:T(8,128)(2,1)}, bf16[136,2560]{1,0:T(8,128)(2,1)S(1)}, u32[]{:S(2)}, u32[]{:S(2)}) collective-permute-start(bf16[136,2560]{1,0:T(8,128)(2,1)} %collective-permute-done.2.rest_3_), channel_id=1, source_target_pairs={{0,4},{1,5},{4,8},{5,9},{8,12},{9,13},{12,14},{13,15},{14,10},{15,... | collective-permute-start | bytes 2088968 | tf_op jit(solution)/shard_map/ppermute | solution.py:463
  38.0 25.0 %collective-permute-start.6 = (bf16[136,2560]{1,0:T(8,128)(2,1)}, bf16[136,2560]{1,0:T(8,128)(2,1)S(1)}, u32[]{:S(2)}, u32[]{:S(2)}) collective-permute-start(bf16[136,2560]{1,0:T(8,128)(2,1)} %collective-permute-done.3.rest_4_), channel_id=1, source_target_pairs={{0,2},{1,3},{4,0},{5,1},{8,4},{9,5},{12,8},{13,9},{14,12},{15,13},... | collective-permute-start | bytes 2088968 | tf_op jit(solution)/shard_map/ppermute | solution.py:463
  38.6 18.9 %collective-permute-start.7 = (bf16[144,768]{1,0:T(8,128)(2,1)}, bf16[144,768]{1,0:T(8,128)(2,1)S(1)}, u32[]{:S(2)}, u32[]{:S(2)}) collective-permute-start(bf16[144,768]{1,0:T(8,128)(2,1)} %get-tuple-element.64), channel_id=1, source_target_pairs={{0,8},{1,9},{4,12},{5,13},{8,14},{9,15},{12,10},{13,11},{14,6},{15... | collective-permute-start | bytes 663560 | tf_op jit(solution)/shard_map/ppermute | solution.py:463
  40.5 22.5 %collective-permute-start.8 = (bf16[144,768]{1,0:T(8,128)(2,1)}, bf16[144,768]{1,0:T(8,128)(2,1)S(1)}, u32[]{:S(2)}, u32[]{:S(2)}) collective-permute-start(bf16[144,768]{1,0:T(8,128)(2,1)} %get-tuple-element.65), channel_id=1, source_target_pairs={{0,6},{1,7},{4,2},{5,3},{8,0},{9,1},{12,4},{13,5},{14,8},{15,9},{1... | collective-permute-start | bytes 663560 | tf_op jit(solution)/shard_map/ppermute | solution.py:463
  57.6 24.6 %copy-start.7 = (bf16[144,768]{1,0:T(8,128)(2,1)}, bf16[144,768]{1,0:T(8,128)(2,1)S(1)}, u32[]{:S(2)}) copy-start(bf16[144,768]{1,0:T(8,128)(2,1)S(1)} %collective-permute-done.7.rest_12_) | copy-start | bytes 663556
  63.0 0.7 copy-start.8
  63.0 10.6 %copy-start.1 = (bf16[136,2560]{1,0:T(8,128)(2,1)}, bf16[136,2560]{1,0:T(8,128)(2,1)S(1)}, u32[]{:S(2)}) copy-start(bf16[136,2560]{1,0:T(8,128)(2,1)S(1)} %collective-permute-done.5.rest_0_.rest_5_) | copy-start | bytes 2088964
  63.7 9.9 %copy-start = (bf16[136,2560]{1,0:T(8,128)(2,1)}, bf16[136,2560]{1,0:T(8,128)(2,1)S(1)}, u32[]{:S(2)}) copy-start(bf16[136,2560]{1,0:T(8,128)(2,1)S(1)} %collective-permute-done.6.rest_1_.rest_6_) | copy-start | bytes 2088964
  63.7 8.6 %collective-permute-start.10 = (bf16[72,2560]{1,0:T(8,128)(2,1)S(1)}, bf16[72,2560]{1,0:T(8,128)(2,1)S(1)}, u32[]{:S(2)}, u32[]{:S(2)}) collective-permute-start(bf16[72,2560]{1,0:T(8,128)(2,1)S(1)} %slice.7), channel_id=1, source_target_pairs={{0,2},{1,3},{4,0},{5,1},{8,4},{9,5},{12,8},{13,9},{14,12},{15,13},... | collective-permute-start | bytes 1105928 | tf_op jit(solution)/shard_map/ppermute | solution.py:463
  64.2 6.0 %collective-permute-start.9 = (bf16[64,2560]{1,0:T(8,128)(2,1)S(1)}, bf16[64,2560]{1,0:T(8,128)(2,1)S(1)}, u32[]{:S(2)}, u32[]{:S(2)}) collective-permute-start(bf16[64,2560]{1,0:T(8,128)(2,1)S(1)} %slice.6), channel_id=1, source_target_pairs={{0,4},{1,5},{4,8},{5,9},{8,12},{9,13},{12,14},{13,15},{14,10},{15,... | collective-permute-start | bytes 983048 | tf_op jit(solution)/shard_map/ppermute | solution.py:463
  65.3 16.9 %collective-permute-start.11 = (bf16[144,768]{1,0:T(8,128)(2,1)}, bf16[144,768]{1,0:T(8,128)(2,1)}, u32[]{:S(2)}, u32[]{:S(2)}) collective-permute-start(bf16[144,768]{1,0:T(8,128)(2,1)} %get-tuple-element.70), channel_id=1, source_target_pairs={{0,4},{1,5},{4,8},{5,9},{8,12},{9,13},{12,14},{13,15},{14,10},{15,... | collective-permute-start | bytes 663560 | tf_op jit(solution)/shard_map/ppermute | solution.py:463
  65.4 16.8 %collective-permute-start.12 = (bf16[144,768]{1,0:T(8,128)(2,1)}, bf16[144,768]{1,0:T(8,128)(2,1)}, u32[]{:S(2)}, u32[]{:S(2)}) collective-permute-start(bf16[144,768]{1,0:T(8,128)(2,1)} %get-tuple-element.71), channel_id=1, source_target_pairs={{0,2},{1,3},{4,0},{5,1},{8,4},{9,5},{12,8},{13,9},{14,12},{15,13},... | collective-permute-start | bytes 663560 | tf_op jit(solution)/shard_map/ppermute | solution.py:463
  66.8 15.4 %collective-permute-start.13 = (bf16[144,768]{1,0:T(8,128)(2,1)}, bf16[144,768]{1,0:T(8,128)(2,1)}, u32[]{:S(2)}, u32[]{:S(2)}) collective-permute-start(bf16[144,768]{1,0:T(8,128)(2,1)} %get-tuple-element.74), channel_id=1, source_target_pairs={{0,12},{1,13},{4,14},{5,15},{8,10},{9,11},{12,6},{13,7},{14,2},{15... | collective-permute-start | bytes 663560 | tf_op jit(solution)/shard_map/ppermute | solution.py:463
  70.1 2.2 %copy-start.4 = (bf16[64,2560]{1,0:T(8,128)(2,1)}, bf16[64,2560]{1,0:T(8,128)(2,1)S(1)}, u32[]{:S(2)}) copy-start(bf16[64,2560]{1,0:T(8,128)(2,1)S(1)} %collective-permute-done.9.rest_2_.rest_7_) | copy-start | bytes 983044
  70.1 12.1 %collective-permute-start.14 = (bf16[144,768]{1,0:T(8,128)(2,1)}, bf16[144,768]{1,0:T(8,128)(2,1)}, u32[]{:S(2)}, u32[]{:S(2)}) collective-permute-start(bf16[144,768]{1,0:T(8,128)(2,1)} %get-tuple-element.75), channel_id=1, source_target_pairs={{0,10},{1,11},{4,6},{5,7},{8,2},{9,3},{12,0},{13,1},{14,4},{15,5},... | collective-permute-start | bytes 663560 | tf_op jit(solution)/shard_map/ppermute | solution.py:463
  72.3 1.3 copy-start.3
  72.3 27.3 %collective-permute-start.15 = (bf16[144,768]{1,0:T(8,128)(2,1)}, bf16[144,768]{1,0:T(8,128)(2,1)}, u32[]{:S(2)}, u32[]{:S(2)}) collective-permute-start(bf16[144,768]{1,0:T(8,128)(2,1)} %get-tuple-element.76), channel_id=1, source_target_pairs={{0,14},{1,15},{4,10},{5,11},{8,6},{9,7},{12,2},{13,3},{14,0},{15,1... | collective-permute-start | bytes 663560 | tf_op jit(solution)/shard_map/ppermute | solution.py:463
  99.6 45.1 %all-to-all-start = ((bf16[8,144,768]{2,1,0:T(8,128)(2,1)}), bf16[8,144,768]{2,1,0:T(8,128)(2,1)S(1)}, u32[]{:S(2)}, u32[]{:S(2)}) async-start(bf16[8,144,768]{2,1,0:T(8,128)(2,1)} %upstream.3), calls=%async_computation | async-start | bytes 3538944 | tf_op jit(solution)/shard_map/all_to_all | solution.py:499
  103.3 19.4 %copy-start.10 = (bf16[128,6]{0,1:T(8,128)(2,1)S(1)}, bf16[128,6]{0,1:T(8,128)(2,1)}, u32[]{:S(2)}) copy-start(bf16[128,6]{0,1:T(8,128)(2,1)} %param.9) | copy-start | bytes 4612
  116.0 20.8 %collective-permute-start.16 = (bf16[192,2560]{1,0:T(8,128)(2,1)}, bf16[192,2560]{1,0:T(8,128)(2,1)}, u32[]{:S(2)}, u32[]{:S(2)}) collective-permute-start(bf16[192,2560]{1,0:T(8,128)(2,1)} %get-tuple-element.90), channel_id=1, source_target_pairs={{0,1},{1,0},{2,3},{3,2},{4,5},{5,4},{6,7},{7,6},{8,9},{9,8},{10,11... | collective-permute-start | bytes 2949128 | tf_op jit(solution)/shard_map/ppermute | solution.py:501
  122.1 14.7 %collective-permute-start.17 = (bf16[192,2560]{1,0:T(8,128)(2,1)}, bf16[192,2560]{1,0:T(8,128)(2,1)}, u32[]{:S(2)}, u32[]{:S(2)}) collective-permute-start(bf16[192,2560]{1,0:T(8,128)(2,1)} %get-tuple-element.91), channel_id=1, source_target_pairs={{0,1},{1,0},{2,3},{3,2},{4,5},{5,4},{6,7},{7,6},{8,9},{9,8},{10,11... | collective-permute-start | bytes 2949128 | tf_op jit(solution)/shard_map/ppermute | solution.py:501
  122.2 14.6 %collective-permute-start.18 = (bf16[192,2560]{1,0:T(8,128)(2,1)}, bf16[192,2560]{1,0:T(8,128)(2,1)}, u32[]{:S(2)}, u32[]{:S(2)}) collective-permute-start(bf16[192,2560]{1,0:T(8,128)(2,1)} %get-tuple-element.92), channel_id=1, source_target_pairs={{0,1},{1,0},{2,3},{3,2},{4,5},{5,4},{6,7},{7,6},{8,9},{9,8},{10,11... | collective-permute-start | bytes 2949128 | tf_op jit(solution)/shard_map/ppermute | solution.py:501
  122.6 14.2 %collective-permute-start.19 = (bf16[192,2560]{1,0:T(8,128)(2,1)}, bf16[192,2560]{1,0:T(8,128)(2,1)}, u32[]{:S(2)}, u32[]{:S(2)}) collective-permute-start(bf16[192,2560]{1,0:T(8,128)(2,1)} %get-tuple-element.93), channel_id=1, source_target_pairs={{0,1},{1,0},{2,3},{3,2},{4,5},{5,4},{6,7},{7,6},{8,9},{9,8},{10,11... | collective-permute-start | bytes 2949128 | tf_op jit(solution)/shard_map/ppermute | solution.py:501
  136.8 7.1 %copy-start.9 = (s32[6,128]{1,0:T(8,128)S(1)}, s32[6,128]{1,0:T(8,128)}, u32[]{:S(2)}) copy-start(s32[6,128]{1,0:T(8,128)} %get-tuple-element.94) | copy-start | bytes 9220
  144.6 1.2 copy-start.6

commit v4 on v3

--- a/solution.py
+++ b/solution.py
@@ -145,6 +145,7 @@
 
 
 RING = 8
+ADD_LIMIT = 24 * 1024 * 1024
 ID_ROWS = 8
 PARTS = 4
 UNPACK_FLOPS = 40_000_000_000
@@ -351,7 +352,7 @@
     for copy in grad_loads:
         copy.wait()
     width = grads.shape[1]
-    step = 256
+    step = 512
 
     @pl.loop(0, width // step)
     def _(n):
@@ -385,47 +386,52 @@
 
 
 def add_kernel(trained_ref, *rest):
-    parts = len(rest) // 2
-    own_refs, came_refs, out_ref = rest[:parts], rest[parts : 2 * parts], rest[-1]
-    trained, at = trained_ref[0].astype(F32), 0
-    for own_ref, came_ref in zip(own_refs, came_refs):
-        height = own_ref.shape[0]
-        total = own_ref[...].astype(F32) + came_ref[...].astype(F32)
-        out_ref[at : at + height, :] = (total * trained).astype(BF16)
-        at += height
+    own_refs, came_refs, (out_ref, own, came, sums, sems) = rest[:PARTS], rest[PARTS : 2 * PARTS], rest[-5:]
+    trained = trained_ref[0].astype(F32)
+    height = own.shape[1]
+    loads = []
+    for part in range(PARTS):
+        for n, (ref, buffer) in enumerate(((own_refs[part], own), (came_refs[part], came))):
+            loads.append(pltpu.make_async_copy(ref, buffer.at[part], sems.at[n, part]))
+            loads[-1].start()
+    stores = []
+    for part in range(PARTS):
+        loads[2 * part].wait()
+        loads[2 * part + 1].wait()
+        total = own[part].astype(F32) + came[part].astype(F32)
+        sums[part] = (total * trained).astype(BF16)
+        goal = out_ref.at[pl.ds(part * height, height)]
+        stores.append(pltpu.make_async_copy(sums.at[part], goal, sems.at[2, part]))
+        stores[-1].start()
+    for copy in stores:
+        copy.wait()
 
 
 def add_parts(trained, own, came):
     height, width = own[0].shape
-    step = 512
-    part = pl.BlockSpec((height, step), lambda n: (0, n))
-    rows = height * len(own)
     return pl.pallas_call(
         add_kernel,
-        out_shape=jax.ShapeDtypeStruct((rows, width), BF16),
-        grid=(width // step,),
-        in_specs=[whole(pltpu.SMEM)] + [part] * (2 * len(own)),
-        out_specs=pl.BlockSpec((rows, step), lambda n: (0, n)),
-        compiler_params=pltpu.CompilerParams(vmem_limit_bytes=VMEM_LIMIT),
+        out_shape=jax.ShapeDtypeStruct((height * PARTS, width), BF16),
+        in_specs=[whole(pltpu.SMEM)] + [whole(pltpu.HBM)] * (2 * PARTS),
+        out_specs=whole(pltpu.HBM),
+        scratch_shapes=[pltpu.VMEM((PARTS, height, width), BF16)] * 3
+        + [pltpu.SemaphoreType.DMA((3, PARTS))],
+        compiler_params=pltpu.CompilerParams(vmem_limit_bytes=ADD_LIMIT),
         cost_estimate=pl.CostEstimate(flops=1_000_000, bytes_accessed=1_000_000, transcendentals=0),
         name="weight_add",
     )(trained, *own, *came)
 
 
-def unpack_kernel(place_ref, gates_ref, hidden_ref, *rest):
-    back_refs, (grad_ref, gate_ref, select, sums, back, sems) = rest[:-6], rest[-6:]
+def unpack_kernel(place_ref, gates_ref, hidden_ref, back_ref, grad_ref, gate_ref, select, sums):
     tokens, top_count = place_ref.shape
-    rows = back.shape[0]
-    copies = load(back_refs, back, sems, 0)
+    rows = back_ref.shape[0]
     lane = lax.broadcasted_iota(I32, (tokens, rows), 1)
     for k in range(top_count):
         select[k * tokens : (k + 1) * tokens, :] = (
             (place_ref[:, k : k + 1] == lane).astype(F32).astype(BF16)
         )
     sums[...] = jnp.zeros_like(sums)
-    for copy in copies:
-        copy.wait()
-    up = jnp.dot(select[...], back[...], preferred_element_type=F32)
+    up = jnp.dot(select[...], back_ref[...], preferred_element_type=F32)
     for k in range(top_count):
         mine = up[k * tokens : (k + 1) * tokens, :]
         grad_ref[k] = (gates_ref[:, k : k + 1].astype(F32) * mine).astype(BF16)
@@ -442,15 +448,13 @@
             jax.ShapeDtypeStruct((top_count, tokens, hidden_units), BF16),
             jax.ShapeDtypeStruct((top_count, tokens), BF16),
         ),
-        in_specs=[whole()] * 3 + [whole(pltpu.HBM)] * len(back),
+        in_specs=[whole()] * 3 + [whole()] * len(back),
         out_specs=(whole(), whole()),
         scratch_shapes=[
             pltpu.VMEM((top_count * tokens, rows), BF16),
             pltpu.VMEM((tokens, 128), F32),
-            pltpu.VMEM((rows, hidden_units), BF16),
-            pltpu.SemaphoreType.DMA((len(back),)),
         ],
-        compiler_params=pltpu.CompilerParams(vmem_limit_bytes=VMEM_LIMIT),
+        compiler_params=pltpu.CompilerParams(vmem_limit_bytes=24 * 1024 * 1024),
         cost_estimate=pl.CostEstimate(
             flops=UNPACK_FLOPS, bytes_accessed=6 * rows * hidden_units, transcendentals=0
         ),

time: 153 us -> 148 us (0.967)
  Pallas kernels: 63.3 us -> 56 us
  local copies, waits for them, and re-layouts: 3.44 us -> 5.82 us
    pallas_call x1, Pallas kernels: 7.05 us -> 3.96 us  [add_parts(): pl.pallas_call(add_kernel, out_shape=jax.ShapeDtypeStruct((height * PARTS...]
    unnamed x23 -> x31, local copies, waits for them, and re-layouts: 2.67 us -> 5.66 us
    pallas_call x1, Pallas kernels: 5.65 us -> 3.11 us  [unpack(): pl.pallas_call(unpack_kernel, out_shape=(jax.ShapeDtypeStruct((top_count,...]
    pallas_call x2, Pallas kernels: 25.3 us -> 23.6 us  [ring_weight_sum(): pl.pallas_call(functools.partial(ring_weight_kernel, capacity, other, len...]
  transfers between devices with their start and end apart: 21 -> 21, of which waited for: 7 -> 7; matrix products, arithmetic and copies ran while one was open for 2% -> 1% of each run, Pallas kernels for 38% -> 36%
where the time goes in v4:
time: 148 us; the launch traced here: 147 us
  Pallas kernels  56 us (38%)
  waiting for transfers between devices  55.4 us (37%)
  starting transfers between devices  26.1 us (18%)
  local copies, waits for them, and re-layouts  5.82 us (4%)
  other arithmetic  1.82 us (1%)
  between operations  1.5 us (1%)
    ppermute x15, waiting for transfers between devices, send(): return lax.ppermute(value, 'expert', ring_shift(step))  55.3 us
    pallas_call x2, Pallas kernels, ring_weight_sum(): pl.pallas_call(functools.partial(ring_weight_kernel, capacity, other, len...  23.6 us
    pallas_call x2, Pallas kernels, ring_upstream(): pl.pallas_call(functools.partial(ring_upstream_kernel, capacity, offsets,...  20.7 us
    ppermute x15, starting transfers between devices, send(): return lax.ppermute(value, 'expert', ring_shift(step))  14.9 us
    ppermute x4, starting transfers between devices, ring_exchange(): came = [lax.ppermute(part, 'expert', SWAP) for part in theirs]  6.75 us
    unnamed x31, local copies, waits for them, and re-layouts  5.66 us
    pallas_call x1, Pallas kernels, ring_pack(): pl.pallas_call(functools.partial(ring_pack_kernel, capacity), out_shape=(...  4.55 us
    pallas_call x1, Pallas kernels, add_parts(): pl.pallas_call(add_kernel, out_shape=jax.ShapeDtypeStruct((height * PARTS...  3.96 us
  transfers between devices with their start and end apart: 21, of which 7 were waited for; matrix products, arithmetic and copies ran while one was open for 1% of the time, Pallas kernels for 36%

profile of v4, /device:TPU:13, one launch (start us, length us, event | category | flops | bytes accessed | tf_op | source)
XLA Modules:
  0.0 146.6 jit_solution(6013416440179352833)
XLA Ops:
  0.6 0.7 collective-permute-start.4
  1.4 0.7 bitcast_convert_fusion
  2.1 1.1 fusion.1.rest_0_
  3.2 0.0 copy-start.7
  3.2 0.2 collective-permute-start
  3.4 1.3 collective-permute-start.1
  4.7 4.5 %pack.1 = (bf16[144,768]{1,0:T(8,128)(2,1)}, bf16[144,768]{1,0:T(8,128)(2,1)}, bf16[144,768]{1,0:T(8,128)(2,1)}, bf16[144,768]{1,0:T(8,128)(2,1)}, bf16[144,768]...) custom-call(s32[1]{0:T(128)} %bitcast.me_ref, ...), custom_call_target="tpu_custom_call" | custom-call | flops 3000000000 | bytes 5000000 | tf_op jit(solution)/shard_map/pack/pallas_call | solution.py:208
  9.3 11.3 %collective-permute-done.rest_1_ = bf16[136,2560]{1,0:T(8,128)(2,1)S(1)} collective-permute-done((bf16[136,2560]{1,0:T(8,128)(2,1)S(1)}, bf16[136,2560]{1,0:T(8,128)(2,1)S(1)}, u32[]{:S(2)}, u32[]{:S(2)}) %collective-permute-start) | collective-permute-done | bytes 696352 | tf_op jit(solution)/shard_map/ppermute | solution.py:467
  20.6 0.0 collective-permute-done.1.rest_2_
  20.6 0.2 collective-permute-start.2
  20.8 1.2 collective-permute-start.3
  22.1 14.8 %collective-permute-done.2.rest_3_ = bf16[136,2560]{1,0:T(8,128)(2,1)} collective-permute-done((bf16[136,2560]{1,0:T(8,128)(2,1)S(1)}, bf16[136,2560]{1,0:T(8,128)(2,1)}, u32[]{:S(2)}, u32[]{:S(2)}) %collective-permute-start.2) | collective-permute-done | bytes 696352 | tf_op jit(solution)/shard_map/ppermute | solution.py:467
  36.8 0.3 collective-permute-done.3.rest_4_
  37.2 0.0 collective-permute-done.4.other_ref
  37.2 0.0 copy-done.10
  37.2 0.8 collective-permute-start.5
  38.0 0.6 collective-permute-start.6
  38.6 1.8 %collective-permute-start.7 = (bf16[144,768]{1,0:T(8,128)(2,1)}, bf16[144,768]{1,0:T(8,128)(2,1)S(1)}, u32[]{:S(2)}, u32[]{:S(2)}) collective-permute-start(bf16[144,768]{1,0:T(8,128)(2,1)} %get-tuple-element.64), channel_id=1, source_target_pairs={{0,8},{1,9},{4,12},{5,13},{8,14},{9,15},{12,10},{13,11},{14,6},{15... | collective-permute-start | bytes 663560 | tf_op jit(solution)/shard_map/ppermute | solution.py:467
  40.5 0.5 collective-permute-start.8
  41.0 12.1 %upstream.2.rest_4_ = bf16[8,144,768]{2,1,0:T(8,128)(2,1)} custom-call(s32[1]{0:T(128)} %bitcast.me_ref, bf16[768,2560]{1,0:T(8,128)(2,1)} %bitcast.16, bf16[768,2560]{1,0:T(8,128)(2,1)} %collective-permute-done.4.other_ref, bf16[136,2560]{1,0:T(8,128)(2,1)} %copy-done.7, bf16[136,2560]{1,0:T(8,128)(2,1)} %copy-done.10, ...), custom_call_target="tpu_custom_call" | custom-call | flops 5033164800 | bytes 11141120 | tf_op jit(solution)/shard_map/upstream/pallas_call | solution.py:306
  53.1 4.4 %collective-permute-done.7.rest_12_ = bf16[144,768]{1,0:T(8,128)(2,1)S(1)} collective-permute-done((bf16[144,768]{1,0:T(8,128)(2,1)}, bf16[144,768]{1,0:T(8,128)(2,1)S(1)}, u32[]{:S(2)}, u32[]{:S(2)}) %collective-permute-start.7) | collective-permute-done | bytes 221216 | tf_op jit(solution)/shard_map/ppermute | solution.py:467
  57.6 5.5 %collective-permute-done.8.rest_13_ = bf16[144,768]{1,0:T(8,128)(2,1)S(1)} collective-permute-done((bf16[144,768]{1,0:T(8,128)(2,1)}, bf16[144,768]{1,0:T(8,128)(2,1)S(1)}, u32[]{:S(2)}, u32[]{:S(2)}) %collective-permute-start.8) | collective-permute-done | bytes 221216 | tf_op jit(solution)/shard_map/ppermute | solution.py:467
  63.0 0.0 collective-permute-done.5.rest_0_.rest_5_
  63.0 0.0 collective-permute-done.6.rest_1_.rest_6_
  63.0 0.7 copy-done.12
  63.7 0.4 collective-permute-start.10
  64.2 1.2 collective-permute-start.9
  65.3 0.1 collective-permute-start.11
  65.4 1.4 collective-permute-start.12
  66.8 1.6 %collective-permute-start.13 = (bf16[144,768]{1,0:T(8,128)(2,1)}, bf16[144,768]{1,0:T(8,128)(2,1)}, u32[]{:S(2)}, u32[]{:S(2)}) collective-permute-start(bf16[144,768]{1,0:T(8,128)(2,1)} %get-tuple-element.74), channel_id=1, source_target_pairs={{0,12},{1,13},{4,14},{5,15},{8,10},{9,11},{12,6},{13,7},{14,2},{15... | collective-permute-start | bytes 663560 | tf_op jit(solution)/shard_map/ppermute | solution.py:467
  68.4 1.8 %collective-permute-done.9.rest_2_.rest_7_ = bf16[64,2560]{1,0:T(8,128)(2,1)S(1)} collective-permute-done((bf16[64,2560]{1,0:T(8,128)(2,1)S(1)}, bf16[64,2560]{1,0:T(8,128)(2,1)S(1)}, u32[]{:S(2)}, u32[]{:S(2)}) %collective-permute-start.9) | collective-permute-done | bytes 327712 | tf_op jit(solution)/shard_map/ppermute | solution.py:467
  70.2 2.1 %collective-permute-start.14 = (bf16[144,768]{1,0:T(8,128)(2,1)}, bf16[144,768]{1,0:T(8,128)(2,1)}, u32[]{:S(2)}, u32[]{:S(2)}) collective-permute-start(bf16[144,768]{1,0:T(8,128)(2,1)} %get-tuple-element.75), channel_id=1, source_target_pairs={{0,10},{1,11},{4,6},{5,7},{8,2},{9,3},{12,0},{13,1},{14,4},{15,5},... | collective-permute-start | bytes 663560 | tf_op jit(solution)/shard_map/ppermute | solution.py:467
  72.3 0.0 collective-permute-done.10.rest_3_.rest_8_
  72.3 0.0 copy-done.9
  72.3 1.3 collective-permute-start.15
  73.6 0.0 copy-done.5
  73.6 8.6 %upstream.3 = bf16[8,144,768]{2,1,0:T(8,128)(2,1)} custom-call(s32[1]{0:T(128)} %bitcast.me_ref, bf16[768,2560]{1,0:T(8,128)(2,1)} %bitcast.17, bf16[768,2560]{1,0:T(8,128)(2,1)} %collective-permute-done.4.other_ref, bf16[136,2560]{1,0:T(8,128)(2,1)} %copy-done.6, bf16[136,2560]{1,0:T(8,128)(2,1)} %copy-done.5, ...), custom_call_target="tpu_custom_call", output_to_operand_aliasing={{}: (7, {})} | custom-call | flops 3019898880 | bytes 9830400 | tf_op jit(solution)/shard_map/upstream/pallas_call | solution.py:306
  82.2 0.0 collective-permute-done.11.rest_10_
  82.2 0.0 collective-permute-done.12.rest_11_
  82.2 0.0 collective-permute-done.13.rest_14_
  82.2 0.0 collective-permute-done.14.rest_15_
  82.3 17.3 %collective-permute-done.15.rest_16_ = bf16[144,768]{1,0:T(8,128)(2,1)} collective-permute-done((bf16[144,768]{1,0:T(8,128)(2,1)}, bf16[144,768]{1,0:T(8,128)(2,1)}, u32[]{:S(2)}, u32[]{:S(2)}) %collective-permute-start.15) | collective-permute-done | bytes 221216 | tf_op jit(solution)/shard_map/ppermute | solution.py:467
  99.6 3.7 %all-to-all-start = ((bf16[8,144,768]{2,1,0:T(8,128)(2,1)}), bf16[8,144,768]{2,1,0:T(8,128)(2,1)S(1)}, u32[]{:S(2)}, u32[]{:S(2)}) async-start(bf16[8,144,768]{2,1,0:T(8,128)(2,1)} %upstream.3), calls=%async_computation | async-start | bytes 3538944 | tf_op jit(solution)/shard_map/all_to_all | solution.py:503
  103.3 0.0 copy-start.14
  103.3 11.8 %weight_other.1 = (bf16[192,2560]{1,0:T(8,128)(2,1)}, bf16[192,2560]{1,0:T(8,128)(2,1)}, bf16[192,2560]{1,0:T(8,128)(2,1)}, bf16[192,2560]{1,0:T(8,128)(2,1)}) custom-call(s32[1]{0:T(128)} %bitcast.me_ref, bf16[136,2560]{1,0:T(8,128)(2,1)} %copy-done.7, bf16[136,2560]{1,0:T(8,128)(2,1)} %copy-done.10, bf16[136,2560]{1,0:T(8,128)(2,1)} %collective-permute-done.1.rest_2_, ...), custom_call_target="tpu_custom_call" | custom-call | flops 1000000 | bytes 1000000 | tf_op jit(solution)/shard_map/weight_other/pallas_call | solution.py:370
  115.1 6.2 %collective-permute-start.16 = (bf16[192,2560]{1,0:T(8,128)(2,1)}, bf16[192,2560]{1,0:T(8,128)(2,1)}, u32[]{:S(2)}, u32[]{:S(2)}) collective-permute-start(bf16[192,2560]{1,0:T(8,128)(2,1)} %get-tuple-element.90), channel_id=1, source_target_pairs={{0,1},{1,0},{2,3},{3,2},{4,5},{5,4},{6,7},{7,6},{8,9},{9,8},{10,11... | collective-permute-start | bytes 2949128 | tf_op jit(solution)/shard_map/ppermute | solution.py:505
  121.3 0.1 collective-permute-start.17
  121.4 0.4 collective-permute-start.18
  121.8 0.1 collective-permute-start.19
  121.9 0.1 copy.11.gates_ref
  122.7 11.8 %weight_own.1 = (bf16[192,2560]{1,0:T(8,128)(2,1)}, bf16[192,2560]{1,0:T(8,128)(2,1)}, bf16[192,2560]{1,0:T(8,128)(2,1)}, bf16[192,2560]{1,0:T(8,128)(2,1)}) custom-call(s32[1]{0:T(128)} %bitcast.me_ref, bf16[136,2560]{1,0:T(8,128)(2,1)} %copy-done.7, bf16[136,2560]{1,0:T(8,128)(2,1)} %copy-done.10, bf16[136,2560]{1,0:T(8,128)(2,1)} %collective-permute-done.1.rest_2_, ...), custom_call_target="tpu_custom_call" | custom-call | flops 1000000 | bytes 1000000 | tf_op jit(solution)/shard_map/weight_own/pallas_call | solution.py:370
  134.5 0.0 collective-permute-done.16.rest_4_
  134.5 0.0 collective-permute-done.17.rest_5_
  134.5 0.0 collective-permute-done.18.rest_6_
  134.5 0.0 collective-permute-done.19.rest_7_
  134.5 0.0 copy-start
  134.6 1.2 copy-done
  135.8 1.2 copy-done.1
  137.0 1.2 copy-done.2
  138.2 1.2 copy-done.3
  139.4 4.0 %weight_add.1 = bf16[768,2560]{1,0:T(8,128)(2,1)} custom-call(s32[1]{0:T(128)S(6)} %copy.13.trained_ref, bf16[192,2560]{1,0:T(8,128)(2,1)S(1)} %copy-done, bf16[192,2560]{1,0:T(8,128)(2,1)S(1)} %copy-done.1, bf16[192,2560]{1,0:T(8,128)(2,1)S(1)} %copy-done.2, bf16[192,2560]{1,0:T(8,128)(2,1)S(1)} %copy-done.3, ...), custom_call_target="tpu_custom_call" | custom-call | flops 1000000 | bytes 1000000 | tf_op jit(solution)/shard_map/weight_add/pallas_call | solution.py:412
  143.3 0.1 copy.10
  143.5 0.0 all-to-all-done
  143.5 3.1 %unpack.1 = (bf16[6,128,768]{2,1,0:T(8,128)(2,1)}, bf16[6,128]{1,0:T(8,128)(2,1)}) custom-call(s32[128,6]{1,0:T(8,128)S(1)} %bitcast.12, bf16[128,6]{1,0:T(8,128)(2,1)S(1)} %copy.11.gates_ref, bf16[6,128,768]{2,1,0:T(8,128)(2,1)S(1)} %bitcast.14, bf16[1152,768]{1,0:T(8,128)(2,1)S(1)} %bitcast.11), custom_call_target="tpu_custom_call" | custom-call | flops 40000000000 | bytes 5308416 | tf_op jit(solution)/shard_map/unpack/pallas_call | solution.py:445
  (21 shorter events, 0.1 us)
Async XLA Ops:
  0.6 36.5 %collective-permute-start.4 = (bf16[768,2560]{1,0:T(8,128)(2,1)}, bf16[768,2560]{1,0:T(8,128)(2,1)}, u32[]{:S(2)}, u32[]{:S(2)}) collective-permute-start(bf16[768,2560]{1,0:T(8,128)(2,1)} %bitcast.15), channel_id=1, source_target_pairs={{0,1},{1,0},{2,3},{3,2},{4,5},{5,4},{6,7},{7,6},{8,9},{9,8},{10,11... | collective-permute-start | bytes 11796488 | tf_op jit(solution)/shard_map/ppermute | solution.py:475
  3.2 6.1 %copy-start.7 = (bf16[136,2560]{1,0:T(8,128)(2,1)}, bf16[136,2560]{1,0:T(8,128)(2,1)S(1)}, u32[]{:S(2)}) copy-start(bf16[136,2560]{1,0:T(8,128)(2,1)S(1)} %fusion.1.rest_0_) | copy-start | bytes 2088964
  3.2 17.4 %collective-permute-start = (bf16[136,2560]{1,0:T(8,128)(2,1)S(1)}, bf16[136,2560]{1,0:T(8,128)(2,1)S(1)}, u32[]{:S(2)}, u32[]{:S(2)}) collective-permute-start(bf16[136,2560]{1,0:T(8,128)(2,1)S(1)} %fusion.1.rest_0_), channel_id=1, source_target_pairs={{0,4},{1,5},{4,8},{5,9},{8,12},{9,13},{12,14},{13,15},{14,10},{15,... | collective-permute-start | bytes 2088968 | tf_op jit(solution)/shard_map/ppermute | solution.py:467
  3.4 17.2 %collective-permute-start.1 = (bf16[136,2560]{1,0:T(8,128)(2,1)S(1)}, bf16[136,2560]{1,0:T(8,128)(2,1)}, u32[]{:S(2)}, u32[]{:S(2)}) collective-permute-start(bf16[136,2560]{1,0:T(8,128)(2,1)S(1)} %fusion.1.rest_0_), channel_id=1, source_target_pairs={{0,2},{1,3},{4,0},{5,1},{8,4},{9,5},{12,8},{13,9},{14,12},{15,13},... | collective-permute-start | bytes 2088968 | tf_op jit(solution)/shard_map/ppermute | solution.py:467
  20.6 16.6 %copy-start.10 = (bf16[136,2560]{1,0:T(8,128)(2,1)}, bf16[136,2560]{1,0:T(8,128)(2,1)S(1)}, u32[]{:S(2)}) copy-start(bf16[136,2560]{1,0:T(8,128)(2,1)S(1)} %collective-permute-done.rest_1_) | copy-start | bytes 2088964
  20.6 16.3 %collective-permute-start.2 = (bf16[136,2560]{1,0:T(8,128)(2,1)S(1)}, bf16[136,2560]{1,0:T(8,128)(2,1)}, u32[]{:S(2)}, u32[]{:S(2)}) collective-permute-start(bf16[136,2560]{1,0:T(8,128)(2,1)S(1)} %collective-permute-done.rest_1_), channel_id=1, source_target_pairs={{0,4},{1,5},{4,8},{5,9},{8,12},{9,13},{12,14},{13,15},{14,10},{15,... | collective-permute-start | bytes 2088968 | tf_op jit(solution)/shard_map/ppermute | solution.py:467
  20.8 16.3 %collective-permute-start.3 = (bf16[136,2560]{1,0:T(8,128)(2,1)}, bf16[136,2560]{1,0:T(8,128)(2,1)}, u32[]{:S(2)}, u32[]{:S(2)}) collective-permute-start(bf16[136,2560]{1,0:T(8,128)(2,1)} %collective-permute-done.1.rest_2_), channel_id=1, source_target_pairs={{0,2},{1,3},{4,0},{5,1},{8,4},{9,5},{12,8},{13,9},{14,12},{15,13},... | collective-permute-start | bytes 2088968 | tf_op jit(solution)/shard_map/ppermute | solution.py:467
  37.2 25.9 %collective-permute-start.5 = (bf16[136,2560]{1,0:T(8,128)(2,1)}, bf16[136,2560]{1,0:T(8,128)(2,1)S(1)}, u32[]{:S(2)}, u32[]{:S(2)}) collective-permute-start(bf16[136,2560]{1,0:T(8,128)(2,1)} %collective-permute-done.2.rest_3_), channel_id=1, source_target_pairs={{0,4},{1,5},{4,8},{5,9},{8,12},{9,13},{12,14},{13,15},{14,10},{15,... | collective-permute-start | bytes 2088968 | tf_op jit(solution)/shard_map/ppermute | solution.py:467
  38.0 25.0 %collective-permute-start.6 = (bf16[136,2560]{1,0:T(8,128)(2,1)}, bf16[136,2560]{1,0:T(8,128)(2,1)S(1)}, u32[]{:S(2)}, u32[]{:S(2)}) collective-permute-start(bf16[136,2560]{1,0:T(8,128)(2,1)} %collective-permute-done.3.rest_4_), channel_id=1, source_target_pairs={{0,2},{1,3},{4,0},{5,1},{8,4},{9,5},{12,8},{13,9},{14,12},{15,13},... | collective-permute-start | bytes 2088968 | tf_op jit(solution)/shard_map/ppermute | solution.py:467
  38.6 18.9 %collective-permute-start.7 = (bf16[144,768]{1,0:T(8,128)(2,1)}, bf16[144,768]{1,0:T(8,128)(2,1)S(1)}, u32[]{:S(2)}, u32[]{:S(2)}) collective-permute-start(bf16[144,768]{1,0:T(8,128)(2,1)} %get-tuple-element.64), channel_id=1, source_target_pairs={{0,8},{1,9},{4,12},{5,13},{8,14},{9,15},{12,10},{13,11},{14,6},{15... | collective-permute-start | bytes 663560 | tf_op jit(solution)/shard_map/ppermute | solution.py:467
  40.5 22.5 %collective-permute-start.8 = (bf16[144,768]{1,0:T(8,128)(2,1)}, bf16[144,768]{1,0:T(8,128)(2,1)S(1)}, u32[]{:S(2)}, u32[]{:S(2)}) collective-permute-start(bf16[144,768]{1,0:T(8,128)(2,1)} %get-tuple-element.65), channel_id=1, source_target_pairs={{0,6},{1,7},{4,2},{5,3},{8,0},{9,1},{12,4},{13,5},{14,8},{15,9},{1... | collective-permute-start | bytes 663560 | tf_op jit(solution)/shard_map/ppermute | solution.py:467
  57.6 24.6 %copy-start.11 = (bf16[144,768]{1,0:T(8,128)(2,1)}, bf16[144,768]{1,0:T(8,128)(2,1)S(1)}, u32[]{:S(2)}) copy-start(bf16[144,768]{1,0:T(8,128)(2,1)S(1)} %collective-permute-done.7.rest_12_) | copy-start | bytes 663556
  63.0 0.7 copy-start.12
  63.0 10.6 %copy-start.6 = (bf16[136,2560]{1,0:T(8,128)(2,1)}, bf16[136,2560]{1,0:T(8,128)(2,1)S(1)}, u32[]{:S(2)}) copy-start(bf16[136,2560]{1,0:T(8,128)(2,1)S(1)} %collective-permute-done.5.rest_0_.rest_5_) | copy-start | bytes 2088964
  63.7 9.9 %copy-start.5 = (bf16[136,2560]{1,0:T(8,128)(2,1)}, bf16[136,2560]{1,0:T(8,128)(2,1)S(1)}, u32[]{:S(2)}) copy-start(bf16[136,2560]{1,0:T(8,128)(2,1)S(1)} %collective-permute-done.6.rest_1_.rest_6_) | copy-start | bytes 2088964
  63.7 8.6 %collective-permute-start.10 = (bf16[72,2560]{1,0:T(8,128)(2,1)S(1)}, bf16[72,2560]{1,0:T(8,128)(2,1)S(1)}, u32[]{:S(2)}, u32[]{:S(2)}) collective-permute-start(bf16[72,2560]{1,0:T(8,128)(2,1)S(1)} %slice.7), channel_id=1, source_target_pairs={{0,2},{1,3},{4,0},{5,1},{8,4},{9,5},{12,8},{13,9},{14,12},{15,13},... | collective-permute-start | bytes 1105928 | tf_op jit(solution)/shard_map/ppermute | solution.py:467
  64.2 6.0 %collective-permute-start.9 = (bf16[64,2560]{1,0:T(8,128)(2,1)S(1)}, bf16[64,2560]{1,0:T(8,128)(2,1)S(1)}, u32[]{:S(2)}, u32[]{:S(2)}) collective-permute-start(bf16[64,2560]{1,0:T(8,128)(2,1)S(1)} %slice.6), channel_id=1, source_target_pairs={{0,4},{1,5},{4,8},{5,9},{8,12},{9,13},{12,14},{13,15},{14,10},{15,... | collective-permute-start | bytes 983048 | tf_op jit(solution)/shard_map/ppermute | solution.py:467
  65.3 16.9 %collective-permute-start.11 = (bf16[144,768]{1,0:T(8,128)(2,1)}, bf16[144,768]{1,0:T(8,128)(2,1)}, u32[]{:S(2)}, u32[]{:S(2)}) collective-permute-start(bf16[144,768]{1,0:T(8,128)(2,1)} %get-tuple-element.70), channel_id=1, source_target_pairs={{0,4},{1,5},{4,8},{5,9},{8,12},{9,13},{12,14},{13,15},{14,10},{15,... | collective-permute-start | bytes 663560 | tf_op jit(solution)/shard_map/ppermute | solution.py:467
  65.4 16.8 %collective-permute-start.12 = (bf16[144,768]{1,0:T(8,128)(2,1)}, bf16[144,768]{1,0:T(8,128)(2,1)}, u32[]{:S(2)}, u32[]{:S(2)}) collective-permute-start(bf16[144,768]{1,0:T(8,128)(2,1)} %get-tuple-element.71), channel_id=1, source_target_pairs={{0,2},{1,3},{4,0},{5,1},{8,4},{9,5},{12,8},{13,9},{14,12},{15,13},... | collective-permute-start | bytes 663560 | tf_op jit(solution)/shard_map/ppermute | solution.py:467
  66.8 15.4 %collective-permute-start.13 = (bf16[144,768]{1,0:T(8,128)(2,1)}, bf16[144,768]{1,0:T(8,128)(2,1)}, u32[]{:S(2)}, u32[]{:S(2)}) collective-permute-start(bf16[144,768]{1,0:T(8,128)(2,1)} %get-tuple-element.74), channel_id=1, source_target_pairs={{0,12},{1,13},{4,14},{5,15},{8,10},{9,11},{12,6},{13,7},{14,2},{15... | collective-permute-start | bytes 663560 | tf_op jit(solution)/shard_map/ppermute | solution.py:467
  70.2 2.2 %copy-start.9 = (bf16[64,2560]{1,0:T(8,128)(2,1)}, bf16[64,2560]{1,0:T(8,128)(2,1)S(1)}, u32[]{:S(2)}) copy-start(bf16[64,2560]{1,0:T(8,128)(2,1)S(1)} %collective-permute-done.9.rest_2_.rest_7_) | copy-start | bytes 983044
  70.2 12.1 %collective-permute-start.14 = (bf16[144,768]{1,0:T(8,128)(2,1)}, bf16[144,768]{1,0:T(8,128)(2,1)}, u32[]{:S(2)}, u32[]{:S(2)}) collective-permute-start(bf16[144,768]{1,0:T(8,128)(2,1)} %get-tuple-element.75), channel_id=1, source_target_pairs={{0,10},{1,11},{4,6},{5,7},{8,2},{9,3},{12,0},{13,1},{14,4},{15,5},... | collective-permute-start | bytes 663560 | tf_op jit(solution)/shard_map/ppermute | solution.py:467
  72.3 1.3 copy-start.8
  72.3 27.2 %collective-permute-start.15 = (bf16[144,768]{1,0:T(8,128)(2,1)}, bf16[144,768]{1,0:T(8,128)(2,1)}, u32[]{:S(2)}, u32[]{:S(2)}) collective-permute-start(bf16[144,768]{1,0:T(8,128)(2,1)} %get-tuple-element.76), channel_id=1, source_target_pairs={{0,14},{1,15},{4,10},{5,11},{8,6},{9,7},{12,2},{13,3},{14,0},{15,1... | collective-permute-start | bytes 663560 | tf_op jit(solution)/shard_map/ppermute | solution.py:467
  99.6 43.9 %all-to-all-start = ((bf16[8,144,768]{2,1,0:T(8,128)(2,1)}), bf16[8,144,768]{2,1,0:T(8,128)(2,1)S(1)}, u32[]{:S(2)}, u32[]{:S(2)}) async-start(bf16[8,144,768]{2,1,0:T(8,128)(2,1)} %upstream.3), calls=%async_computation | async-start | bytes 3538944 | tf_op jit(solution)/shard_map/all_to_all | solution.py:503
  103.3 18.6 %copy-start.14 = (bf16[128,6]{0,1:T(8,128)(2,1)S(1)}, bf16[128,6]{0,1:T(8,128)(2,1)}, u32[]{:S(2)}) copy-start(bf16[128,6]{0,1:T(8,128)(2,1)} %param.9) | copy-start | bytes 4612
  115.1 19.4 %collective-permute-start.16 = (bf16[192,2560]{1,0:T(8,128)(2,1)}, bf16[192,2560]{1,0:T(8,128)(2,1)}, u32[]{:S(2)}, u32[]{:S(2)}) collective-permute-start(bf16[192,2560]{1,0:T(8,128)(2,1)} %get-tuple-element.90), channel_id=1, source_target_pairs={{0,1},{1,0},{2,3},{3,2},{4,5},{5,4},{6,7},{7,6},{8,9},{9,8},{10,11... | collective-permute-start | bytes 2949128 | tf_op jit(solution)/shard_map/ppermute | solution.py:505
  121.3 13.2 %collective-permute-start.17 = (bf16[192,2560]{1,0:T(8,128)(2,1)}, bf16[192,2560]{1,0:T(8,128)(2,1)}, u32[]{:S(2)}, u32[]{:S(2)}) collective-permute-start(bf16[192,2560]{1,0:T(8,128)(2,1)} %get-tuple-element.91), channel_id=1, source_target_pairs={{0,1},{1,0},{2,3},{3,2},{4,5},{5,4},{6,7},{7,6},{8,9},{9,8},{10,11... | collective-permute-start | bytes 2949128 | tf_op jit(solution)/shard_map/ppermute | solution.py:505
  121.4 13.2 %collective-permute-start.18 = (bf16[192,2560]{1,0:T(8,128)(2,1)}, bf16[192,2560]{1,0:T(8,128)(2,1)}, u32[]{:S(2)}, u32[]{:S(2)}) collective-permute-start(bf16[192,2560]{1,0:T(8,128)(2,1)} %get-tuple-element.92), channel_id=1, source_target_pairs={{0,1},{1,0},{2,3},{3,2},{4,5},{5,4},{6,7},{7,6},{8,9},{9,8},{10,11... | collective-permute-start | bytes 2949128 | tf_op jit(solution)/shard_map/ppermute | solution.py:505
  121.8 12.7 %collective-permute-start.19 = (bf16[192,2560]{1,0:T(8,128)(2,1)}, bf16[192,2560]{1,0:T(8,128)(2,1)}, u32[]{:S(2)}, u32[]{:S(2)}) collective-permute-start(bf16[192,2560]{1,0:T(8,128)(2,1)} %get-tuple-element.93), channel_id=1, source_target_pairs={{0,1},{1,0},{2,3},{3,2},{4,5},{5,4},{6,7},{7,6},{8,9},{9,8},{10,11... | collective-permute-start | bytes 2949128 | tf_op jit(solution)/shard_map/ppermute | solution.py:505
  134.5 1.2 copy-start
  135.7 1.2 copy-start.1
  136.9 1.2 copy-start.2
  138.2 1.2 copy-start.3
  139.4 4.0 %copy-start.13 = (s32[6,128]{1,0:T(8,128)S(1)}, s32[6,128]{1,0:T(8,128)}, u32[]{:S(2)}) copy-start(s32[6,128]{1,0:T(8,128)} %get-tuple-element.94) | copy-start | bytes 9220
  139.4 4.1 %copy-start.4 = (bf16[128,6,768]{2,0,1:T(8,128)(2,1)S(1)}, bf16[128,6,768]{2,0,1:T(8,128)(2,1)}, u32[]{:S(2)}) copy-start(bf16[128,6,768]{2,0,1:T(8,128)(2,1)} %param.7) | copy-start | bytes 3538948

commit v5 on v4

--- a/solution.py
+++ b/solution.py
@@ -145,6 +145,8 @@
 
 
 RING = 8
+COLUMNS = 4
+COPIES = 2 * COLUMNS + 1
 ADD_LIMIT = 24 * 1024 * 1024
 ID_ROWS = 8
 PARTS = 4
@@ -241,23 +243,26 @@
 
 
 def load_pieces(refs, grads, ids, sems, first):
-    tokens = ids.shape[2]
+    half, wide = ids.shape[2] // 2, grads.shape[1] // COLUMNS
     rows, routes, at = [], [], 0
-    for n, ref in enumerate(refs):
+    for ref in refs:
         extra = ref.shape[0] % 16
-        count = ref.shape[0] - extra
-        rows.append(
-            pltpu.make_async_copy(
-                ref.at[pl.ds(0, count)], grads.at[pl.ds(at, count)], sems.at[first + 2 * n]
-            )
-        )
-        at += count
+        for base in range(0, ref.shape[0] - extra, half * COLUMNS):
+            for column in range(COLUMNS):
+                rows.append(
+                    pltpu.make_async_copy(
+                        ref.at[pl.ds(base + column * half, half)],
+                        grads.at[pl.ds(at, half), pl.ds(column * wide, wide)],
+                        sems.at[first + len(rows) + len(routes)],
+                    )
+                )
+            at += half
         if extra:
             routes.append(
                 pltpu.make_async_copy(
-                    ref.at[pl.ds(count, extra), pl.ds(0, tokens)],
-                    ids.at[at // tokens - 1],
-                    sems.at[first + 2 * n + 1],
+                    ref.at[pl.ds(ref.shape[0] - extra, extra), pl.ds(0, 2 * half)],
+                    ids.at[at // (2 * half) - 1],
+                    sems.at[first + len(rows) + len(routes)],
                 )
             )
     for copy in routes + rows:
@@ -315,7 +320,7 @@
             pltpu.VMEM((blocks, ID_ROWS, tokens), BF16),
             pltpu.VMEM((blocks, 2 * tokens, hidden_units), BF16),
             pltpu.VMEM((blocks, 2 * capacity, hidden_units), BF16),
-            pltpu.SemaphoreType.DMA((2 + 2 * len(pieces),)),
+            pltpu.SemaphoreType.DMA((2 + COPIES * blocks,)),
             pltpu.SemaphoreType.DMA((blocks,)),
         ],
         compiler_params=pltpu.CompilerParams(vmem_limit_bytes=VMEM_LIMIT),
@@ -335,7 +340,7 @@
     me = me_ref[0]
     routes, grad_loads = load_pieces(grad_refs, grads, ids, sems, 0)
     loads = [
-        pltpu.make_async_copy(ref, hidden.at[q], sems.at[2 * pieces + q])
+        pltpu.make_async_copy(ref, hidden.at[q], sems.at[COPIES * RING + q])
         for q, ref in enumerate(hidden_refs)
     ]
     for copy in loads:
@@ -364,7 +369,7 @@
 
 
 def ring_weight_sum(me, tokens, pieces, hidden, other, capacity):
-    width = pieces[0].shape[1]
+    width = pieces[0].shape[1] * COLUMNS
     hidden_units = hidden[0].shape[1]
     result = jax.ShapeDtypeStruct((hidden_units // PARTS, width), BF16)
     return pl.pallas_call(
@@ -377,7 +382,7 @@
             pltpu.VMEM((RING, ID_ROWS, tokens), BF16),
             pltpu.VMEM((RING, 2 * capacity, hidden_units), BF16),
             pltpu.VMEM((hidden_units, RING * tokens), BF16),
-            pltpu.SemaphoreType.DMA((2 * len(pieces) + RING,)),
+            pltpu.SemaphoreType.DMA((COPIES * RING + RING,)),
         ],
         compiler_params=pltpu.CompilerParams(vmem_limit_bytes=VMEM_LIMIT),
         cost_estimate=pl.CostEstimate(flops=1_000_000, bytes_accessed=1_000_000, transcendentals=0),
@@ -468,9 +473,11 @@
 
     me = scalars[:1]
     tokens, width = out_grad.shape
-    half = tokens // 2
-    spare = ((0, ID_ROWS - ids_t.shape[0]), (0, width - tokens))
-    block = jnp.concatenate([out_grad, jnp.pad(ids_t.astype(BF16), spare, constant_values=-1)])
+    half, wide = tokens // 2, width // COLUMNS
+    cut = half * COLUMNS
+    rows = out_grad.reshape(2, half, COLUMNS, wide).transpose(0, 2, 1, 3).reshape(2 * cut, wide)
+    spare = ((0, ID_ROWS - ids_t.shape[0]), (0, wide - tokens))
+    block = jnp.concatenate([rows, jnp.pad(ids_t.astype(BF16), spare, constant_values=-1)])
     packed, place = ring_pack(me, ids_t, gates_t, hidden_t, capacity)
     other_weight = lax.ppermute(weight, "expert", SWAP)
     barrier = lax.optimization_barrier
@@ -493,9 +500,11 @@
     ahead, behind = send(ahead, 1), send(behind, -1)
     send_hidden(3, 4)
     up = upstream_of(OFFSETS[:5], pieces[:5], ())
-    ahead, behind, hidden[3], hidden[4], up = barrier((ahead, behind, hidden[3], hidden[4], up))
     pieces += [ahead, behind]
-    pieces += [send(ahead[:half], 1), send(behind[half:], -1)]
+    ahead, behind, hidden[3], hidden[4], up = barrier(
+        (ahead[:cut], behind[cut:], hidden[3], hidden[4], up)
+    )
+    pieces += [send(ahead, 1), send(behind, -1)]
     send_hidden(5, 6, 7, 1, 2)
     up = upstream_of(OFFSETS[5:], pieces[5:], (up,))
     *hidden, up = barrier((*hidden, up))

time: 148 us -> 146 us (0.986)
  waiting for transfers between devices: 55.4 us -> 52.1 us
  Pallas kernels: 56 us -> 58 us
  other arithmetic: 1.82 us -> 0.06 us
    ppermute x15, waiting for transfers between devices: 55.3 us -> 52.1 us  [send(): return lax.ppermute(value, 'expert', ring_shift(step))]
    reshape x0 -> x2, local copies, waits for them, and re-layouts: none -> 1.73 us  [ring_exchange(): out_grad.reshape(2, half, COLUMNS, wide).transpose(0, 2, 1, 3)]
    unnamed x31 -> x33, local copies, waits for them, and re-layouts: 5.66 us -> 5.29 us
  transfers between devices with their start and end apart: 21 -> 21, of which waited for: 7 -> 7; matrix products, arithmetic and copies ran while one was open for 1% -> 1% of each run, Pallas kernels for 36% -> 38%
where the time goes in v5:
time: 146 us; the launch traced here: 144 us
  Pallas kernels  58 us (40%)
  waiting for transfers between devices  52.1 us (36%)
  starting transfers between devices  25.4 us (17%)
  local copies, waits for them, and re-layouts  7.19 us (5%)
  between operations  1.58 us (1%)
    ppermute x15, waiting for transfers between devices, send(): return lax.ppermute(value, 'expert', ring_shift(step))  52.1 us
    pallas_call x2, Pallas kernels, ring_weight_sum(): pl.pallas_call(functools.partial(ring_weight_kernel, capacity, other, len...  25 us
    pallas_call x2, Pallas kernels, ring_upstream(): pl.pallas_call(functools.partial(ring_upstream_kernel, capacity, offsets,...  21.4 us
    ppermute x15, starting transfers between devices, send(): return lax.ppermute(value, 'expert', ring_shift(step))  14.8 us
    ppermute x4, starting transfers between devices, ring_exchange(): came = [lax.ppermute(part, 'expert', SWAP) for part in theirs]  6.18 us
    unnamed x33, local copies, waits for them, and re-layouts  5.29 us
    pallas_call x1, Pallas kernels, ring_pack(): pl.pallas_call(functools.partial(ring_pack_kernel, capacity), out_shape=(...  4.54 us
    pallas_call x1, Pallas kernels, add_parts(): pl.pallas_call(add_kernel, out_shape=jax.ShapeDtypeStruct((height * PARTS...  3.96 us
  transfers between devices with their start and end apart: 21, of which 7 were waited for; matrix products, arithmetic and copies ran while one was open for 1% of the time, Pallas kernels for 38%

profile of v5, /device:TPU:13, one launch (start us, length us, event | category | flops | bytes accessed | tf_op | source)
XLA Modules:
  0.0 144.4 jit_solution(8280196336938030776)
XLA Ops:
  0.6 0.0 copy-start.14
  0.6 0.7 collective-permute-start.4
  1.4 1.7 %reshape.15 = bf16[2,64,4,640]{3,2,1,0:T(4,128)(2,1)S(1)} reshape(bf16[128,2560]{1,0:T(8,128)(2,1)} %param.6) | data formatting | bytes 1310720 | tf_op jit(solution)/shard_map/reshape | solution.py:478
  3.0 0.1 copy.10
  3.1 0.1 fusion.1.rest_0_
  3.2 0.0 copy-start.7
  3.2 0.2 collective-permute-start
  3.4 1.3 collective-permute-start.1
  4.7 4.5 %pack.1 = (bf16[144,768]{1,0:T(8,128)(2,1)}, bf16[144,768]{1,0:T(8,128)(2,1)}, bf16[144,768]{1,0:T(8,128)(2,1)}, bf16[144,768]{1,0:T(8,128)(2,1)}, bf16[144,768]...) custom-call(s32[1]{0:T(128)} %bitcast.me_ref, ...), custom_call_target="tpu_custom_call" | custom-call | flops 3000000000 | bytes 5000000 | tf_op jit(solution)/shard_map/pack/pallas_call | solution.py:210
  9.3 10.5 %collective-permute-done.rest_1_ = bf16[520,640]{1,0:T(8,128)(2,1)S(1)} collective-permute-done((bf16[520,640]{1,0:T(8,128)(2,1)S(1)}, bf16[520,640]{1,0:T(8,128)(2,1)S(1)}, u32[]{:S(2)}, u32[]{:S(2)}) %collective-permute-start) | collective-permute-done | bytes 665632 | tf_op jit(solution)/shard_map/ppermute | solution.py:472
  19.8 0.0 collective-permute-done.1.rest_2_
  19.8 0.2 collective-permute-start.2
  20.1 1.3 collective-permute-start.3
  21.4 14.2 %collective-permute-done.2.rest_3_ = bf16[520,640]{1,0:T(8,128)(2,1)S(1)} collective-permute-done((bf16[520,640]{1,0:T(8,128)(2,1)S(1)}, bf16[520,640]{1,0:T(8,128)(2,1)S(1)}, u32[]{:S(2)}, u32[]{:S(2)}) %collective-permute-start.2) | collective-permute-done | bytes 665632 | tf_op jit(solution)/shard_map/ppermute | solution.py:472
  35.5 0.0 collective-permute-done.3.rest_4_
  35.5 0.0 copy-done.10
  35.5 0.0 collective-permute-done.4.other_ref
  35.6 1.4 collective-permute-start.6
  36.9 0.2 collective-permute-start.5
  37.1 1.8 %collective-permute-start.7 = (bf16[144,768]{1,0:T(8,128)(2,1)}, bf16[144,768]{1,0:T(8,128)(2,1)}, u32[]{:S(2)}, u32[]{:S(2)}) collective-permute-start(bf16[144,768]{1,0:T(8,128)(2,1)} %get-tuple-element.64), channel_id=1, source_target_pairs={{0,8},{1,9},{4,12},{5,13},{8,14},{9,15},{12,10},{13,11},{14,6},{15... | collective-permute-start | bytes 663560 | tf_op jit(solution)/shard_map/ppermute | solution.py:472
  38.9 0.6 collective-permute-start.8
  39.5 12.6 %upstream.2.rest_4_ = bf16[8,144,768]{2,1,0:T(8,128)(2,1)} custom-call(s32[1]{0:T(128)} %bitcast.me_ref, bf16[768,2560]{1,0:T(8,128)(2,1)} %bitcast.19, bf16[768,2560]{1,0:T(8,128)(2,1)} %collective-permute-done.4.other_ref, bf16[520,640]{1,0:T(8,128)(2,1)} %copy-done.7, bf16[520,640]{1,0:T(8,128)(2,1)} %copy-done.10, bf16[520,640]{1,0:T(8,128)(2,1)} %copy-done.11, ...), custom_call_target="tpu_custom_call" | custom-call | flops 5033164800 | bytes 11141120 | tf_op jit(solution)/shard_map/upstream/pallas_call | solution.py:311
  52.0 0.0 collective-permute-done.6.rest_1_.rest_6_
  52.1 0.0 collective-permute-done.5.rest_0_.rest_5_
  52.1 4.5 %collective-permute-done.7.rest_12_ = bf16[144,768]{1,0:T(8,128)(2,1)} collective-permute-done((bf16[144,768]{1,0:T(8,128)(2,1)}, bf16[144,768]{1,0:T(8,128)(2,1)}, u32[]{:S(2)}, u32[]{:S(2)}) %collective-permute-start.7) | collective-permute-done | bytes 221216 | tf_op jit(solution)/shard_map/ppermute | solution.py:472
  56.7 4.2 %collective-permute-done.8.rest_13_ = bf16[144,768]{1,0:T(8,128)(2,1)} collective-permute-done((bf16[144,768]{1,0:T(8,128)(2,1)}, bf16[144,768]{1,0:T(8,128)(2,1)}, u32[]{:S(2)}, u32[]{:S(2)}) %collective-permute-start.8) | collective-permute-done | bytes 221216 | tf_op jit(solution)/shard_map/ppermute | solution.py:472
  60.8 0.2 collective-permute-start.10
  61.0 1.3 collective-permute-start.9
  62.3 0.0 collective-permute-start.11
  62.4 1.4 collective-permute-start.12
  63.8 1.3 collective-permute-start.13
  65.0 1.9 %collective-permute-done.9.rest_2_.rest_7_ = bf16[256,640]{1,0:T(8,128)(2,1)S(1)} collective-permute-done((bf16[256,640]{1,0:T(8,128)(2,1)S(1)}, bf16[256,640]{1,0:T(8,128)(2,1)S(1)}, u32[]{:S(2)}, u32[]{:S(2)}) %collective-permute-start.9) | collective-permute-done | bytes 327712 | tf_op jit(solution)/shard_map/ppermute | solution.py:472
  67.0 3.2 %collective-permute-start.14 = (bf16[144,768]{1,0:T(8,128)(2,1)}, bf16[144,768]{1,0:T(8,128)(2,1)}, u32[]{:S(2)}, u32[]{:S(2)}) collective-permute-start(bf16[144,768]{1,0:T(8,128)(2,1)} %get-tuple-element.75), channel_id=1, source_target_pairs={{0,10},{1,11},{4,6},{5,7},{8,2},{9,3},{12,0},{13,1},{14,4},{15,5},... | collective-permute-start | bytes 663560 | tf_op jit(solution)/shard_map/ppermute | solution.py:472
  70.2 0.0 collective-permute-done.10.rest_3_.rest_8_
  70.2 0.4 collective-permute-start.15
  70.6 0.3 copy-done.8
  70.9 8.9 %upstream.3 = bf16[8,144,768]{2,1,0:T(8,128)(2,1)} custom-call(s32[1]{0:T(128)} %bitcast.me_ref, bf16[768,2560]{1,0:T(8,128)(2,1)} %bitcast.20, bf16[768,2560]{1,0:T(8,128)(2,1)} %collective-permute-done.4.other_ref, bf16[520,640]{1,0:T(8,128)(2,1)} %copy-done.6, bf16[520,640]{1,0:T(8,128)(2,1)} %copy-done.5, ...), custom_call_target="tpu_custom_call", output_to_operand_aliasing={{}: (7, {})} | custom-call | flops 3019898880 | bytes 9830400 | tf_op jit(solution)/shard_map/upstream/pallas_call | solution.py:311
  79.8 0.0 collective-permute-done.11.rest_10_
  79.8 0.0 collective-permute-done.12.rest_11_
  79.8 0.0 collective-permute-done.13.rest_14_
  79.8 10.0 %collective-permute-done.14.rest_15_ = bf16[144,768]{1,0:T(8,128)(2,1)} collective-permute-done((bf16[144,768]{1,0:T(8,128)(2,1)}, bf16[144,768]{1,0:T(8,128)(2,1)}, u32[]{:S(2)}, u32[]{:S(2)}) %collective-permute-start.14) | collective-permute-done | bytes 221216 | tf_op jit(solution)/shard_map/ppermute | solution.py:472
  89.8 6.8 %collective-permute-done.15.rest_16_ = bf16[144,768]{1,0:T(8,128)(2,1)} collective-permute-done((bf16[144,768]{1,0:T(8,128)(2,1)}, bf16[144,768]{1,0:T(8,128)(2,1)}, u32[]{:S(2)}, u32[]{:S(2)}) %collective-permute-start.15) | collective-permute-done | bytes 221216 | tf_op jit(solution)/shard_map/ppermute | solution.py:472
  96.6 3.7 %all-to-all-start = ((bf16[8,144,768]{2,1,0:T(8,128)(2,1)}), bf16[8,144,768]{2,1,0:T(8,128)(2,1)S(1)}, u32[]{:S(2)}, u32[]{:S(2)}) async-start(bf16[8,144,768]{2,1,0:T(8,128)(2,1)} %upstream.3), calls=%async_computation | async-start | bytes 3538944 | tf_op jit(solution)/shard_map/all_to_all | solution.py:512
  100.3 0.0 copy-start.15
  100.3 12.5 %weight_other.1 = (bf16[192,2560]{1,0:T(8,128)(2,1)}, bf16[192,2560]{1,0:T(8,128)(2,1)}, bf16[192,2560]{1,0:T(8,128)(2,1)}, bf16[192,2560]{1,0:T(8,128)(2,1)}) custom-call(s32[1]{0:T(128)} %bitcast.me_ref, bf16[520,640]{1,0:T(8,128)(2,1)} %copy-done.7, bf16[520,640]{1,0:T(8,128)(2,1)} %copy-done.10, bf16[520,640]{1,0:T(8,128)(2,1)} %copy-done.11, ...), custom_call_target="tpu_custom_call" | custom-call | flops 1000000 | bytes 1000000 | tf_op jit(solution)/shard_map/weight_other/pallas_call | solution.py:375
  112.8 5.6 %collective-permute-start.16 = (bf16[192,2560]{1,0:T(8,128)(2,1)}, bf16[192,2560]{1,0:T(8,128)(2,1)}, u32[]{:S(2)}, u32[]{:S(2)}) collective-permute-start(bf16[192,2560]{1,0:T(8,128)(2,1)} %get-tuple-element.90), channel_id=1, source_target_pairs={{0,1},{1,0},{2,3},{3,2},{4,5},{5,4},{6,7},{7,6},{8,9},{9,8},{10,11... | collective-permute-start | bytes 2949128 | tf_op jit(solution)/shard_map/ppermute | solution.py:514
  118.4 0.1 collective-permute-start.17
  118.5 0.4 collective-permute-start.18
  118.9 0.1 collective-permute-start.19
  119.0 0.1 copy.12.gates_ref
  119.8 12.5 %weight_own.1 = (bf16[192,2560]{1,0:T(8,128)(2,1)}, bf16[192,2560]{1,0:T(8,128)(2,1)}, bf16[192,2560]{1,0:T(8,128)(2,1)}, bf16[192,2560]{1,0:T(8,128)(2,1)}) custom-call(s32[1]{0:T(128)} %bitcast.me_ref, bf16[520,640]{1,0:T(8,128)(2,1)} %copy-done.7, bf16[520,640]{1,0:T(8,128)(2,1)} %copy-done.10, bf16[520,640]{1,0:T(8,128)(2,1)} %copy-done.11, ...), custom_call_target="tpu_custom_call" | custom-call | flops 1000000 | bytes 1000000 | tf_op jit(solution)/shard_map/weight_own/pallas_call | solution.py:375
  132.3 0.0 collective-permute-done.16.rest_4_
  132.3 0.0 collective-permute-done.17.rest_5_
  132.3 0.0 collective-permute-done.18.rest_6_
  132.4 0.0 collective-permute-done.19.rest_7_
  132.4 0.0 copy-start
  132.4 1.2 copy-done
  133.6 1.2 copy-done.1
  134.8 1.2 copy-done.2
  136.0 1.2 copy-done.3
  137.2 4.0 %weight_add.1 = bf16[768,2560]{1,0:T(8,128)(2,1)} custom-call(s32[1]{0:T(128)S(6)} %copy.14.trained_ref, bf16[192,2560]{1,0:T(8,128)(2,1)S(1)} %copy-done, bf16[192,2560]{1,0:T(8,128)(2,1)S(1)} %copy-done.1, bf16[192,2560]{1,0:T(8,128)(2,1)S(1)} %copy-done.2, bf16[192,2560]{1,0:T(8,128)(2,1)S(1)} %copy-done.3, ...), custom_call_target="tpu_custom_call" | custom-call | flops 1000000 | bytes 1000000 | tf_op jit(solution)/shard_map/weight_add/pallas_call | solution.py:417
  141.2 0.1 copy.11
  141.3 0.0 all-to-all-done
  141.3 3.1 %unpack.1 = (bf16[6,128,768]{2,1,0:T(8,128)(2,1)}, bf16[6,128]{1,0:T(8,128)(2,1)}) custom-call(s32[128,6]{1,0:T(8,128)S(1)} %bitcast.15, bf16[128,6]{1,0:T(8,128)(2,1)S(1)} %copy.12.gates_ref, bf16[6,128,768]{2,1,0:T(8,128)(2,1)S(1)} %bitcast.17, bf16[1152,768]{1,0:T(8,128)(2,1)S(1)} %bitcast.14), custom_call_target="tpu_custom_call" | custom-call | flops 40000000000 | bytes 5308416 | tf_op jit(solution)/shard_map/unpack/pallas_call | solution.py:450
  (25 shorter events, 0.1 us)
Async XLA Ops:
  0.6 2.5 %copy-start.14 = (s32[128,6]{0,1:T(8,128)S(1)}, s32[128,6]{0,1:T(8,128)}, u32[]{:S(2)}) copy-start(s32[128,6]{0,1:T(8,128)} %param.8) | copy-start | bytes 9220
  0.6 34.9 %collective-permute-start.4 = (bf16[768,2560]{1,0:T(8,128)(2,1)}, bf16[768,2560]{1,0:T(8,128)(2,1)}, u32[]{:S(2)}, u32[]{:S(2)}) collective-permute-start(bf16[768,2560]{1,0:T(8,128)(2,1)} %bitcast.18), channel_id=1, source_target_pairs={{0,1},{1,0},{2,3},{3,2},{4,5},{5,4},{6,7},{7,6},{8,9},{9,8},{10,11... | collective-permute-start | bytes 11796488 | tf_op jit(solution)/shard_map/ppermute | solution.py:482
  3.2 6.1 %copy-start.7 = (bf16[520,640]{1,0:T(8,128)(2,1)}, bf16[520,640]{1,0:T(8,128)(2,1)S(1)}, u32[]{:S(2)}) copy-start(bf16[520,640]{1,0:T(8,128)(2,1)S(1)} %fusion.1.rest_0_) | copy-start | bytes 1996804
  3.2 16.6 %collective-permute-start = (bf16[520,640]{1,0:T(8,128)(2,1)S(1)}, bf16[520,640]{1,0:T(8,128)(2,1)S(1)}, u32[]{:S(2)}, u32[]{:S(2)}) collective-permute-start(bf16[520,640]{1,0:T(8,128)(2,1)S(1)} %fusion.1.rest_0_), channel_id=1, source_target_pairs={{0,4},{1,5},{4,8},{5,9},{8,12},{9,13},{12,14},{13,15},{14,10},{15,... | collective-permute-start | bytes 1996808 | tf_op jit(solution)/shard_map/ppermute | solution.py:472
  3.4 16.4 %collective-permute-start.1 = (bf16[520,640]{1,0:T(8,128)(2,1)S(1)}, bf16[520,640]{1,0:T(8,128)(2,1)S(1)}, u32[]{:S(2)}, u32[]{:S(2)}) collective-permute-start(bf16[520,640]{1,0:T(8,128)(2,1)S(1)} %fusion.1.rest_0_), channel_id=1, source_target_pairs={{0,2},{1,3},{4,0},{5,1},{8,4},{9,5},{12,8},{13,9},{14,12},{15,13},... | collective-permute-start | bytes 1996808 | tf_op jit(solution)/shard_map/ppermute | solution.py:472
  19.8 15.7 %copy-start.10 = (bf16[520,640]{1,0:T(8,128)(2,1)}, bf16[520,640]{1,0:T(8,128)(2,1)S(1)}, u32[]{:S(2)}) copy-start(bf16[520,640]{1,0:T(8,128)(2,1)S(1)} %collective-permute-done.rest_1_) | copy-start | bytes 1996804
  19.8 15.7 %copy-start.11 = (bf16[520,640]{1,0:T(8,128)(2,1)}, bf16[520,640]{1,0:T(8,128)(2,1)S(1)}, u32[]{:S(2)}) copy-start(bf16[520,640]{1,0:T(8,128)(2,1)S(1)} %collective-permute-done.1.rest_2_) | copy-start | bytes 1996804
  19.8 15.7 %collective-permute-start.2 = (bf16[520,640]{1,0:T(8,128)(2,1)S(1)}, bf16[520,640]{1,0:T(8,128)(2,1)S(1)}, u32[]{:S(2)}, u32[]{:S(2)}) collective-permute-start(bf16[520,640]{1,0:T(8,128)(2,1)S(1)} %collective-permute-done.rest_1_), channel_id=1, source_target_pairs={{0,4},{1,5},{4,8},{5,9},{8,12},{9,13},{12,14},{13,15},{14,10},{15,... | collective-permute-start | bytes 1996808 | tf_op jit(solution)/shard_map/ppermute | solution.py:472
  20.1 15.5 %collective-permute-start.3 = (bf16[520,640]{1,0:T(8,128)(2,1)S(1)}, bf16[520,640]{1,0:T(8,128)(2,1)}, u32[]{:S(2)}, u32[]{:S(2)}) collective-permute-start(bf16[520,640]{1,0:T(8,128)(2,1)S(1)} %collective-permute-done.1.rest_2_), channel_id=1, source_target_pairs={{0,2},{1,3},{4,0},{5,1},{8,4},{9,5},{12,8},{13,9},{14,12},{15,13},... | collective-permute-start | bytes 1996808 | tf_op jit(solution)/shard_map/ppermute | solution.py:472
  35.5 3.9 %copy-start.12 = (bf16[520,640]{1,0:T(8,128)(2,1)}, bf16[520,640]{1,0:T(8,128)(2,1)S(1)}, u32[]{:S(2)}) copy-start(bf16[520,640]{1,0:T(8,128)(2,1)S(1)} %collective-permute-done.2.rest_3_) | copy-start | bytes 1996804
  35.6 16.4 %collective-permute-start.6 = (bf16[520,640]{1,0:T(8,128)(2,1)}, bf16[520,640]{1,0:T(8,128)(2,1)S(1)}, u32[]{:S(2)}, u32[]{:S(2)}) collective-permute-start(bf16[520,640]{1,0:T(8,128)(2,1)} %collective-permute-done.3.rest_4_), channel_id=1, source_target_pairs={{0,2},{1,3},{4,0},{5,1},{8,4},{9,5},{12,8},{13,9},{14,12},{15,13},... | collective-permute-start | bytes 1996808 | tf_op jit(solution)/shard_map/ppermute | solution.py:472
  36.9 15.2 %collective-permute-start.5 = (bf16[520,640]{1,0:T(8,128)(2,1)S(1)}, bf16[520,640]{1,0:T(8,128)(2,1)S(1)}, u32[]{:S(2)}, u32[]{:S(2)}) collective-permute-start(bf16[520,640]{1,0:T(8,128)(2,1)S(1)} %collective-permute-done.2.rest_3_), channel_id=1, source_target_pairs={{0,4},{1,5},{4,8},{5,9},{8,12},{9,13},{12,14},{13,15},{14,10},{15,... | collective-permute-start | bytes 1996808 | tf_op jit(solution)/shard_map/ppermute | solution.py:472
  37.1 19.6 %collective-permute-start.7 = (bf16[144,768]{1,0:T(8,128)(2,1)}, bf16[144,768]{1,0:T(8,128)(2,1)}, u32[]{:S(2)}, u32[]{:S(2)}) collective-permute-start(bf16[144,768]{1,0:T(8,128)(2,1)} %get-tuple-element.64), channel_id=1, source_target_pairs={{0,8},{1,9},{4,12},{5,13},{8,14},{9,15},{12,10},{13,11},{14,6},{15... | collective-permute-start | bytes 663560 | tf_op jit(solution)/shard_map/ppermute | solution.py:472
  38.9 22.0 %collective-permute-start.8 = (bf16[144,768]{1,0:T(8,128)(2,1)}, bf16[144,768]{1,0:T(8,128)(2,1)}, u32[]{:S(2)}, u32[]{:S(2)}) collective-permute-start(bf16[144,768]{1,0:T(8,128)(2,1)} %get-tuple-element.65), channel_id=1, source_target_pairs={{0,6},{1,7},{4,2},{5,3},{8,0},{9,1},{12,4},{13,5},{14,8},{15,9},{1... | collective-permute-start | bytes 663560 | tf_op jit(solution)/shard_map/ppermute | solution.py:472
  52.0 18.6 %copy-start.5 = (bf16[520,640]{1,0:T(8,128)(2,1)}, bf16[520,640]{1,0:T(8,128)(2,1)S(1)}, u32[]{:S(2)}) copy-start(bf16[520,640]{1,0:T(8,128)(2,1)S(1)} %collective-permute-done.6.rest_1_.rest_6_) | copy-start | bytes 1996804
  52.1 18.5 %copy-start.6 = (bf16[520,640]{1,0:T(8,128)(2,1)}, bf16[520,640]{1,0:T(8,128)(2,1)S(1)}, u32[]{:S(2)}) copy-start(bf16[520,640]{1,0:T(8,128)(2,1)S(1)} %collective-permute-done.5.rest_0_.rest_5_) | copy-start | bytes 1996804
  60.8 9.4 %collective-permute-start.10 = (bf16[264,640]{1,0:T(8,128)(2,1)S(1)}, bf16[264,640]{1,0:T(8,128)(2,1)S(1)}, u32[]{:S(2)}, u32[]{:S(2)}) collective-permute-start(bf16[264,640]{1,0:T(8,128)(2,1)S(1)} %slice.9), channel_id=1, source_target_pairs={{0,2},{1,3},{4,0},{5,1},{8,4},{9,5},{12,8},{13,9},{14,12},{15,13},... | collective-permute-start | bytes 1013768 | tf_op jit(solution)/shard_map/ppermute | solution.py:472
  61.0 5.9 %collective-permute-start.9 = (bf16[256,640]{1,0:T(8,128)(2,1)S(1)}, bf16[256,640]{1,0:T(8,128)(2,1)S(1)}, u32[]{:S(2)}, u32[]{:S(2)}) collective-permute-start(bf16[256,640]{1,0:T(8,128)(2,1)S(1)} %slice.8), channel_id=1, source_target_pairs={{0,4},{1,5},{4,8},{5,9},{8,12},{9,13},{12,14},{13,15},{14,10},{15,... | collective-permute-start | bytes 983048 | tf_op jit(solution)/shard_map/ppermute | solution.py:472
  62.3 17.5 %collective-permute-start.11 = (bf16[144,768]{1,0:T(8,128)(2,1)}, bf16[144,768]{1,0:T(8,128)(2,1)}, u32[]{:S(2)}, u32[]{:S(2)}) collective-permute-start(bf16[144,768]{1,0:T(8,128)(2,1)} %get-tuple-element.70), channel_id=1, source_target_pairs={{0,4},{1,5},{4,8},{5,9},{8,12},{9,13},{12,14},{13,15},{14,10},{15,... | collective-permute-start | bytes 663560 | tf_op jit(solution)/shard_map/ppermute | solution.py:472
  62.4 17.5 %collective-permute-start.12 = (bf16[144,768]{1,0:T(8,128)(2,1)}, bf16[144,768]{1,0:T(8,128)(2,1)}, u32[]{:S(2)}, u32[]{:S(2)}) collective-permute-start(bf16[144,768]{1,0:T(8,128)(2,1)} %get-tuple-element.71), channel_id=1, source_target_pairs={{0,2},{1,3},{4,0},{5,1},{8,4},{9,5},{12,8},{13,9},{14,12},{15,13},... | collective-permute-start | bytes 663560 | tf_op jit(solution)/shard_map/ppermute | solution.py:472
  63.8 16.0 %collective-permute-start.13 = (bf16[144,768]{1,0:T(8,128)(2,1)}, bf16[144,768]{1,0:T(8,128)(2,1)}, u32[]{:S(2)}, u32[]{:S(2)}) collective-permute-start(bf16[144,768]{1,0:T(8,128)(2,1)} %get-tuple-element.74), channel_id=1, source_target_pairs={{0,12},{1,13},{4,14},{5,15},{8,10},{9,11},{12,6},{13,7},{14,2},{15... | collective-permute-start | bytes 663560 | tf_op jit(solution)/shard_map/ppermute | solution.py:472
  67.0 3.7 %copy-start.9 = (bf16[256,640]{1,0:T(8,128)(2,1)}, bf16[256,640]{1,0:T(8,128)(2,1)S(1)}, u32[]{:S(2)}) copy-start(bf16[256,640]{1,0:T(8,128)(2,1)S(1)} %collective-permute-done.9.rest_2_.rest_7_) | copy-start | bytes 983044
  67.0 22.9 %collective-permute-start.14 = (bf16[144,768]{1,0:T(8,128)(2,1)}, bf16[144,768]{1,0:T(8,128)(2,1)}, u32[]{:S(2)}, u32[]{:S(2)}) collective-permute-start(bf16[144,768]{1,0:T(8,128)(2,1)} %get-tuple-element.75), channel_id=1, source_target_pairs={{0,10},{1,11},{4,6},{5,7},{8,2},{9,3},{12,0},{13,1},{14,4},{15,5},... | collective-permute-start | bytes 663560 | tf_op jit(solution)/shard_map/ppermute | solution.py:472
  70.2 0.7 copy-start.8
  70.2 26.4 %collective-permute-start.15 = (bf16[144,768]{1,0:T(8,128)(2,1)}, bf16[144,768]{1,0:T(8,128)(2,1)}, u32[]{:S(2)}, u32[]{:S(2)}) collective-permute-start(bf16[144,768]{1,0:T(8,128)(2,1)} %get-tuple-element.76), channel_id=1, source_target_pairs={{0,14},{1,15},{4,10},{5,11},{8,6},{9,7},{12,2},{13,3},{14,0},{15,1... | collective-permute-start | bytes 663560 | tf_op jit(solution)/shard_map/ppermute | solution.py:472
  96.6 44.7 %all-to-all-start = ((bf16[8,144,768]{2,1,0:T(8,128)(2,1)}), bf16[8,144,768]{2,1,0:T(8,128)(2,1)S(1)}, u32[]{:S(2)}, u32[]{:S(2)}) async-start(bf16[8,144,768]{2,1,0:T(8,128)(2,1)} %upstream.3), calls=%async_computation | async-start | bytes 3538944 | tf_op jit(solution)/shard_map/all_to_all | solution.py:512
  100.3 18.7 %copy-start.15 = (bf16[128,6]{0,1:T(8,128)(2,1)S(1)}, bf16[128,6]{0,1:T(8,128)(2,1)}, u32[]{:S(2)}) copy-start(bf16[128,6]{0,1:T(8,128)(2,1)} %param.9) | copy-start | bytes 4612
  112.8 19.5 %collective-permute-start.16 = (bf16[192,2560]{1,0:T(8,128)(2,1)}, bf16[192,2560]{1,0:T(8,128)(2,1)}, u32[]{:S(2)}, u32[]{:S(2)}) collective-permute-start(bf16[192,2560]{1,0:T(8,128)(2,1)} %get-tuple-element.90), channel_id=1, source_target_pairs={{0,1},{1,0},{2,3},{3,2},{4,5},{5,4},{6,7},{7,6},{8,9},{9,8},{10,11... | collective-permute-start | bytes 2949128 | tf_op jit(solution)/shard_map/ppermute | solution.py:514
  118.4 13.9 %collective-permute-start.17 = (bf16[192,2560]{1,0:T(8,128)(2,1)}, bf16[192,2560]{1,0:T(8,128)(2,1)}, u32[]{:S(2)}, u32[]{:S(2)}) collective-permute-start(bf16[192,2560]{1,0:T(8,128)(2,1)} %get-tuple-element.91), channel_id=1, source_target_pairs={{0,1},{1,0},{2,3},{3,2},{4,5},{5,4},{6,7},{7,6},{8,9},{9,8},{10,11... | collective-permute-start | bytes 2949128 | tf_op jit(solution)/shard_map/ppermute | solution.py:514
  118.5 13.8 %collective-permute-start.18 = (bf16[192,2560]{1,0:T(8,128)(2,1)}, bf16[192,2560]{1,0:T(8,128)(2,1)}, u32[]{:S(2)}, u32[]{:S(2)}) collective-permute-start(bf16[192,2560]{1,0:T(8,128)(2,1)} %get-tuple-element.92), channel_id=1, source_target_pairs={{0,1},{1,0},{2,3},{3,2},{4,5},{5,4},{6,7},{7,6},{8,9},{9,8},{10,11... | collective-permute-start | bytes 2949128 | tf_op jit(solution)/shard_map/ppermute | solution.py:514
  118.9 13.4 %collective-permute-start.19 = (bf16[192,2560]{1,0:T(8,128)(2,1)}, bf16[192,2560]{1,0:T(8,128)(2,1)}, u32[]{:S(2)}, u32[]{:S(2)}) collective-permute-start(bf16[192,2560]{1,0:T(8,128)(2,1)} %get-tuple-element.93), channel_id=1, source_target_pairs={{0,1},{1,0},{2,3},{3,2},{4,5},{5,4},{6,7},{7,6},{8,9},{9,8},{10,11... | collective-permute-start | bytes 2949128 | tf_op jit(solution)/shard_map/ppermute | solution.py:514
  132.4 1.2 copy-start
  133.6 1.2 copy-start.1
  134.8 1.2 copy-start.2
  136.0 1.2 copy-start.3
  137.2 4.0 %copy-start.13 = (s32[6,128]{1,0:T(8,128)S(1)}, s32[6,128]{1,0:T(8,128)}, u32[]{:S(2)}) copy-start(s32[6,128]{1,0:T(8,128)} %get-tuple-element.94) | copy-start | bytes 9220
  137.2 4.1 %copy-start.4 = (bf16[128,6,768]{2,0,1:T(8,128)(2,1)S(1)}, bf16[128,6,768]{2,0,1:T(8,128)(2,1)}, u32[]{:S(2)}) copy-start(bf16[128,6,768]{2,0,1:T(8,128)(2,1)} %param.7) | copy-start | bytes 3538948

commit v6 on v5

--- a/solution.py
+++ b/solution.py
@@ -498,14 +498,14 @@
         ring_upstream, me, tokens, own_weight=weight, other_weight=other_weight, capacity=capacity
     )
     ahead, behind = send(ahead, 1), send(behind, -1)
-    send_hidden(3, 4)
+    send_hidden(1, 2)
     up = upstream_of(OFFSETS[:5], pieces[:5], ())
     pieces += [ahead, behind]
-    ahead, behind, hidden[3], hidden[4], up = barrier(
-        (ahead[:cut], behind[cut:], hidden[3], hidden[4], up)
+    ahead, behind, hidden[1], hidden[2], up = barrier(
+        (ahead[:cut], behind[cut:], hidden[1], hidden[2], up)
     )
     pieces += [send(ahead, 1), send(behind, -1)]
-    send_hidden(5, 6, 7, 1, 2)
+    send_hidden(5, 6, 7, 3, 4)
     up = upstream_of(OFFSETS[5:], pieces[5:], (up,))
     *hidden, up = barrier((*hidden, up))
     groups = [[ring_device(p, core) for p in range(RING)] for core in range(2)]

time: 146 us -> 145 us (level)
  starting transfers between devices: 25.4 us -> 23.5 us
  waiting for transfers between devices: 52.1 us -> 53.6 us
    ppermute x15, starting transfers between devices: 14.8 us -> 12.8 us  [send(): return lax.ppermute(value, 'expert', ring_shift(step))]
where the time goes in v6:
time: 145 us; the launch traced here: 144 us
  Pallas kernels  58 us (40%)
  waiting for transfers between devices  53.6 us (37%)
  starting transfers between devices  23.5 us (16%)
  local copies, waits for them, and re-layouts  6.89 us (5%)
  between operations  1.56 us (1%)
    ppermute x15, waiting for transfers between devices, send(): return lax.ppermute(value, 'expert', ring_shift(step))  53.6 us
    pallas_call x2, Pallas kernels, ring_weight_sum(): pl.pallas_call(functools.partial(ring_weight_kernel, capacity, other, len...  25 us
    pallas_call x2, Pallas kernels, ring_upstream(): pl.pallas_call(functools.partial(ring_upstream_kernel, capacity, offsets,...  21.4 us
    ppermute x15, starting transfers between devices, send(): return lax.ppermute(value, 'expert', ring_shift(step))  12.8 us
    ppermute x4, starting transfers between devices, ring_exchange(): came = [lax.ppermute(part, 'expert', SWAP) for part in theirs]  5.47 us
    unnamed x33, local copies, waits for them, and re-layouts  4.98 us
    all_to_all x1, starting transfers between devices, ring_exchange(): lax.all_to_all(up, 'expert', 0, 0, axis_index_groups=groups, tiled=True)  4.55 us
    pallas_call x1, Pallas kernels, ring_pack(): pl.pallas_call(functools.partial(ring_pack_kernel, capacity), out_shape=(...  4.54 us
  transfers between devices with their start and end apart: 21, of which 7 were waited for; matrix products, arithmetic and copies ran while one was open for 1% of the time, Pallas kernels for 38%

profile of v6, /device:TPU:13, one launch (start us, length us, event | category | flops | bytes accessed | tf_op | source)
XLA Modules:
  0.0 143.6 jit_solution(6530850338204801475)
XLA Ops:
  0.6 0.0 copy-start.14
  0.6 0.7 collective-permute-start.4
  1.4 1.7 %reshape.15 = bf16[2,64,4,640]{3,2,1,0:T(4,128)(2,1)S(1)} reshape(bf16[128,2560]{1,0:T(8,128)(2,1)} %param.6) | data formatting | bytes 1310720 | tf_op jit(solution)/shard_map/reshape | solution.py:478
  3.0 0.1 copy.10
  3.1 0.1 fusion.1.rest_0_
  3.2 0.0 copy-start.7
  3.2 0.2 collective-permute-start
  3.4 1.3 collective-permute-start.1
  4.7 4.5 %pack.1 = (bf16[144,768]{1,0:T(8,128)(2,1)}, bf16[144,768]{1,0:T(8,128)(2,1)}, bf16[144,768]{1,0:T(8,128)(2,1)}, bf16[144,768]{1,0:T(8,128)(2,1)}, bf16[144,768]...) custom-call(s32[1]{0:T(128)} %bitcast.me_ref, ...), custom_call_target="tpu_custom_call" | custom-call | flops 3000000000 | bytes 5000000 | tf_op jit(solution)/shard_map/pack/pallas_call | solution.py:210
  9.3 0.0 copy-done.7
  9.3 10.5 %collective-permute-done.rest_1_ = bf16[520,640]{1,0:T(8,128)(2,1)S(1)} collective-permute-done((bf16[520,640]{1,0:T(8,128)(2,1)S(1)}, bf16[520,640]{1,0:T(8,128)(2,1)S(1)}, u32[]{:S(2)}, u32[]{:S(2)}) %collective-permute-start) | collective-permute-done | bytes 665632 | tf_op jit(solution)/shard_map/ppermute | solution.py:472
  19.8 0.0 collective-permute-done.1.rest_2_
  19.8 0.2 collective-permute-start.2
  20.1 1.3 collective-permute-start.3
  21.4 14.2 %collective-permute-done.2.rest_3_ = bf16[520,640]{1,0:T(8,128)(2,1)S(1)} collective-permute-done((bf16[520,640]{1,0:T(8,128)(2,1)S(1)}, bf16[520,640]{1,0:T(8,128)(2,1)S(1)}, u32[]{:S(2)}, u32[]{:S(2)}) %collective-permute-start.2) | collective-permute-done | bytes 665632 | tf_op jit(solution)/shard_map/ppermute | solution.py:472
  35.5 0.0 collective-permute-done.3.rest_4_
  35.5 0.0 copy-done.10
  35.5 0.0 collective-permute-done.4.other_ref
  35.6 1.4 collective-permute-start.6
  36.9 0.2 collective-permute-start.5
  37.1 0.8 collective-permute-start.7
  37.9 0.7 collective-permute-start.8
  38.6 12.6 %upstream.2.rest_4_ = bf16[8,144,768]{2,1,0:T(8,128)(2,1)} custom-call(s32[1]{0:T(128)} %bitcast.me_ref, bf16[768,2560]{1,0:T(8,128)(2,1)} %bitcast.19, bf16[768,2560]{1,0:T(8,128)(2,1)} %collective-permute-done.4.other_ref, bf16[520,640]{1,0:T(8,128)(2,1)} %copy-done.7, bf16[520,640]{1,0:T(8,128)(2,1)} %copy-done.10, bf16[520,640]{1,0:T(8,128)(2,1)} %copy-done.11, ...), custom_call_target="tpu_custom_call" | custom-call | flops 5033164800 | bytes 11141120 | tf_op jit(solution)/shard_map/upstream/pallas_call | solution.py:311
  51.1 0.0 collective-permute-done.6.rest_1_.rest_6_
  51.2 0.0 collective-permute-done.5.rest_0_.rest_5_
  51.2 0.0 copy-start.6
  51.2 4.7 %collective-permute-done.7.rest_10_ = bf16[144,768]{1,0:T(8,128)(2,1)} collective-permute-done((bf16[144,768]{1,0:T(8,128)(2,1)}, bf16[144,768]{1,0:T(8,128)(2,1)}, u32[]{:S(2)}, u32[]{:S(2)}) %collective-permute-start.7) | collective-permute-done | bytes 221216 | tf_op jit(solution)/shard_map/ppermute | solution.py:472
  56.0 0.0 collective-permute-done.8.rest_11_
  56.0 1.3 collective-permute-start.10
  57.2 0.2 collective-permute-start.9
  57.4 0.5 collective-permute-start.11
  58.0 1.8 %collective-permute-start.12 = (bf16[144,768]{1,0:T(8,128)(2,1)}, bf16[144,768]{1,0:T(8,128)(2,1)}, u32[]{:S(2)}, u32[]{:S(2)}) collective-permute-start(bf16[144,768]{1,0:T(8,128)(2,1)} %get-tuple-element.73), channel_id=1, source_target_pairs={{0,6},{1,7},{4,2},{5,3},{8,0},{9,1},{12,4},{13,5},{14,8},{15,9},{1... | collective-permute-start | bytes 663560 | tf_op jit(solution)/shard_map/ppermute | solution.py:472
  59.8 0.6 collective-permute-start.13
  60.4 3.0 %collective-permute-done.9.rest_2_.rest_7_ = bf16[256,640]{1,0:T(8,128)(2,1)S(1)} collective-permute-done((bf16[256,640]{1,0:T(8,128)(2,1)S(1)}, bf16[256,640]{1,0:T(8,128)(2,1)S(1)}, u32[]{:S(2)}, u32[]{:S(2)}) %collective-permute-start.9) | collective-permute-done | bytes 327712 | tf_op jit(solution)/shard_map/ppermute | solution.py:472
  63.5 1.2 collective-permute-start.14
  64.7 0.0 collective-permute-done.10.rest_3_.rest_8_
  64.7 1.1 collective-permute-start.15
  65.8 8.9 %upstream.3 = bf16[8,144,768]{2,1,0:T(8,128)(2,1)} custom-call(s32[1]{0:T(128)} %bitcast.me_ref, bf16[768,2560]{1,0:T(8,128)(2,1)} %bitcast.20, bf16[768,2560]{1,0:T(8,128)(2,1)} %collective-permute-done.4.other_ref, bf16[520,640]{1,0:T(8,128)(2,1)} %copy-done.6, bf16[520,640]{1,0:T(8,128)(2,1)} %copy-done.5, ...), custom_call_target="tpu_custom_call", output_to_operand_aliasing={{}: (7, {})} | custom-call | flops 3019898880 | bytes 9830400 | tf_op jit(solution)/shard_map/upstream/pallas_call | solution.py:311
  74.6 0.0 collective-permute-done.11.rest_12_
  74.6 0.0 collective-permute-done.12.rest_13_
  74.7 3.0 %collective-permute-done.13.rest_14_ = bf16[144,768]{1,0:T(8,128)(2,1)} collective-permute-done((bf16[144,768]{1,0:T(8,128)(2,1)}, bf16[144,768]{1,0:T(8,128)(2,1)}, u32[]{:S(2)}, u32[]{:S(2)}) %collective-permute-start.13) | collective-permute-done | bytes 221216 | tf_op jit(solution)/shard_map/ppermute | solution.py:472
  77.7 12.1 %collective-permute-done.14.rest_15_ = bf16[144,768]{1,0:T(8,128)(2,1)} collective-permute-done((bf16[144,768]{1,0:T(8,128)(2,1)}, bf16[144,768]{1,0:T(8,128)(2,1)}, u32[]{:S(2)}, u32[]{:S(2)}) %collective-permute-start.14) | collective-permute-done | bytes 221216 | tf_op jit(solution)/shard_map/ppermute | solution.py:472
  89.8 5.9 %collective-permute-done.15.rest_16_ = bf16[144,768]{1,0:T(8,128)(2,1)} collective-permute-done((bf16[144,768]{1,0:T(8,128)(2,1)}, bf16[144,768]{1,0:T(8,128)(2,1)}, u32[]{:S(2)}, u32[]{:S(2)}) %collective-permute-start.15) | collective-permute-done | bytes 221216 | tf_op jit(solution)/shard_map/ppermute | solution.py:472
  95.8 4.5 %all-to-all-start = ((bf16[8,144,768]{2,1,0:T(8,128)(2,1)}), bf16[8,144,768]{2,1,0:T(8,128)(2,1)S(1)}, u32[]{:S(2)}, u32[]{:S(2)}) async-start(bf16[8,144,768]{2,1,0:T(8,128)(2,1)} %upstream.3), calls=%async_computation | async-start | bytes 3538944 | tf_op jit(solution)/shard_map/all_to_all | solution.py:512
  100.3 12.5 %weight_other.1 = (bf16[192,2560]{1,0:T(8,128)(2,1)}, bf16[192,2560]{1,0:T(8,128)(2,1)}, bf16[192,2560]{1,0:T(8,128)(2,1)}, bf16[192,2560]{1,0:T(8,128)(2,1)}) custom-call(s32[1]{0:T(128)} %bitcast.me_ref, bf16[520,640]{1,0:T(8,128)(2,1)} %copy-done.7, bf16[520,640]{1,0:T(8,128)(2,1)} %copy-done.10, bf16[520,640]{1,0:T(8,128)(2,1)} %copy-done.11, ...), custom_call_target="tpu_custom_call" | custom-call | flops 1000000 | bytes 1000000 | tf_op jit(solution)/shard_map/weight_other/pallas_call | solution.py:375
  112.8 4.9 %collective-permute-start.16 = (bf16[192,2560]{1,0:T(8,128)(2,1)}, bf16[192,2560]{1,0:T(8,128)(2,1)}, u32[]{:S(2)}, u32[]{:S(2)}) collective-permute-start(bf16[192,2560]{1,0:T(8,128)(2,1)} %get-tuple-element.90), channel_id=1, source_target_pairs={{0,1},{1,0},{2,3},{3,2},{4,5},{5,4},{6,7},{7,6},{8,9},{9,8},{10,11... | collective-permute-start | bytes 2949128 | tf_op jit(solution)/shard_map/ppermute | solution.py:514
  117.7 0.1 collective-permute-start.17
  117.8 0.4 collective-permute-start.18
  118.2 0.1 collective-permute-start.19
  118.3 0.1 copy.12.gates_ref
  119.1 12.5 %weight_own.1 = (bf16[192,2560]{1,0:T(8,128)(2,1)}, bf16[192,2560]{1,0:T(8,128)(2,1)}, bf16[192,2560]{1,0:T(8,128)(2,1)}, bf16[192,2560]{1,0:T(8,128)(2,1)}) custom-call(s32[1]{0:T(128)} %bitcast.me_ref, bf16[520,640]{1,0:T(8,128)(2,1)} %copy-done.7, bf16[520,640]{1,0:T(8,128)(2,1)} %copy-done.10, bf16[520,640]{1,0:T(8,128)(2,1)} %copy-done.11, ...), custom_call_target="tpu_custom_call" | custom-call | flops 1000000 | bytes 1000000 | tf_op jit(solution)/shard_map/weight_own/pallas_call | solution.py:375
  131.6 0.0 collective-permute-done.16.rest_4_
  131.6 0.0 collective-permute-done.17.rest_5_
  131.6 0.0 collective-permute-done.18.rest_6_
  131.6 0.0 collective-permute-done.19.rest_7_
  131.6 0.0 copy-start
  131.6 1.2 copy-done
  132.8 1.2 copy-done.1
  134.0 1.2 copy-done.2
  135.2 1.2 copy-done.3
  136.4 4.0 %weight_add.1 = bf16[768,2560]{1,0:T(8,128)(2,1)} custom-call(s32[1]{0:T(128)S(6)} %copy.14.trained_ref, bf16[192,2560]{1,0:T(8,128)(2,1)S(1)} %copy-done, bf16[192,2560]{1,0:T(8,128)(2,1)S(1)} %copy-done.1, bf16[192,2560]{1,0:T(8,128)(2,1)S(1)} %copy-done.2, bf16[192,2560]{1,0:T(8,128)(2,1)S(1)} %copy-done.3, ...), custom_call_target="tpu_custom_call" | custom-call | flops 1000000 | bytes 1000000 | tf_op jit(solution)/shard_map/weight_add/pallas_call | solution.py:417
  140.4 0.1 copy.11
  140.5 0.0 all-to-all-done
  140.5 3.1 %unpack.1 = (bf16[6,128,768]{2,1,0:T(8,128)(2,1)}, bf16[6,128]{1,0:T(8,128)(2,1)}) custom-call(s32[128,6]{1,0:T(8,128)S(1)} %bitcast.15, bf16[128,6]{1,0:T(8,128)(2,1)S(1)} %copy.12.gates_ref, bf16[6,128,768]{2,1,0:T(8,128)(2,1)S(1)} %bitcast.17, bf16[1152,768]{1,0:T(8,128)(2,1)S(1)} %bitcast.14), custom_call_target="tpu_custom_call" | custom-call | flops 40000000000 | bytes 5308416 | tf_op jit(solution)/shard_map/unpack/pallas_call | solution.py:450
  (25 shorter events, 0.1 us)
Async XLA Ops:
  0.6 2.5 %copy-start.14 = (s32[128,6]{0,1:T(8,128)S(1)}, s32[128,6]{0,1:T(8,128)}, u32[]{:S(2)}) copy-start(s32[128,6]{0,1:T(8,128)} %param.8) | copy-start | bytes 9220
  0.6 34.9 %collective-permute-start.4 = (bf16[768,2560]{1,0:T(8,128)(2,1)}, bf16[768,2560]{1,0:T(8,128)(2,1)}, u32[]{:S(2)}, u32[]{:S(2)}) collective-permute-start(bf16[768,2560]{1,0:T(8,128)(2,1)} %bitcast.18), channel_id=1, source_target_pairs={{0,1},{1,0},{2,3},{3,2},{4,5},{5,4},{6,7},{7,6},{8,9},{9,8},{10,11... | collective-permute-start | bytes 11796488 | tf_op jit(solution)/shard_map/ppermute | solution.py:482
  3.2 6.1 %copy-start.7 = (bf16[520,640]{1,0:T(8,128)(2,1)}, bf16[520,640]{1,0:T(8,128)(2,1)S(1)}, u32[]{:S(2)}) copy-start(bf16[520,640]{1,0:T(8,128)(2,1)S(1)} %fusion.1.rest_0_) | copy-start | bytes 1996804
  3.2 16.6 %collective-permute-start = (bf16[520,640]{1,0:T(8,128)(2,1)S(1)}, bf16[520,640]{1,0:T(8,128)(2,1)S(1)}, u32[]{:S(2)}, u32[]{:S(2)}) collective-permute-start(bf16[520,640]{1,0:T(8,128)(2,1)S(1)} %fusion.1.rest_0_), channel_id=1, source_target_pairs={{0,4},{1,5},{4,8},{5,9},{8,12},{9,13},{12,14},{13,15},{14,10},{15,... | collective-permute-start | bytes 1996808 | tf_op jit(solution)/shard_map/ppermute | solution.py:472
  3.4 16.4 %collective-permute-start.1 = (bf16[520,640]{1,0:T(8,128)(2,1)S(1)}, bf16[520,640]{1,0:T(8,128)(2,1)S(1)}, u32[]{:S(2)}, u32[]{:S(2)}) collective-permute-start(bf16[520,640]{1,0:T(8,128)(2,1)S(1)} %fusion.1.rest_0_), channel_id=1, source_target_pairs={{0,2},{1,3},{4,0},{5,1},{8,4},{9,5},{12,8},{13,9},{14,12},{15,13},... | collective-permute-start | bytes 1996808 | tf_op jit(solution)/shard_map/ppermute | solution.py:472
  19.8 15.7 %copy-start.10 = (bf16[520,640]{1,0:T(8,128)(2,1)}, bf16[520,640]{1,0:T(8,128)(2,1)S(1)}, u32[]{:S(2)}) copy-start(bf16[520,640]{1,0:T(8,128)(2,1)S(1)} %collective-permute-done.rest_1_) | copy-start | bytes 1996804
  19.8 15.7 %copy-start.11 = (bf16[520,640]{1,0:T(8,128)(2,1)}, bf16[520,640]{1,0:T(8,128)(2,1)S(1)}, u32[]{:S(2)}) copy-start(bf16[520,640]{1,0:T(8,128)(2,1)S(1)} %collective-permute-done.1.rest_2_) | copy-start | bytes 1996804
  19.8 15.7 %collective-permute-start.2 = (bf16[520,640]{1,0:T(8,128)(2,1)S(1)}, bf16[520,640]{1,0:T(8,128)(2,1)S(1)}, u32[]{:S(2)}, u32[]{:S(2)}) collective-permute-start(bf16[520,640]{1,0:T(8,128)(2,1)S(1)} %collective-permute-done.rest_1_), channel_id=1, source_target_pairs={{0,4},{1,5},{4,8},{5,9},{8,12},{9,13},{12,14},{13,15},{14,10},{15,... | collective-permute-start | bytes 1996808 | tf_op jit(solution)/shard_map/ppermute | solution.py:472
  20.1 15.5 %collective-permute-start.3 = (bf16[520,640]{1,0:T(8,128)(2,1)S(1)}, bf16[520,640]{1,0:T(8,128)(2,1)}, u32[]{:S(2)}, u32[]{:S(2)}) collective-permute-start(bf16[520,640]{1,0:T(8,128)(2,1)S(1)} %collective-permute-done.1.rest_2_), channel_id=1, source_target_pairs={{0,2},{1,3},{4,0},{5,1},{8,4},{9,5},{12,8},{13,9},{14,12},{15,13},... | collective-permute-start | bytes 1996808 | tf_op jit(solution)/shard_map/ppermute | solution.py:472
  35.5 3.0 %copy-start.12 = (bf16[520,640]{1,0:T(8,128)(2,1)}, bf16[520,640]{1,0:T(8,128)(2,1)S(1)}, u32[]{:S(2)}) copy-start(bf16[520,640]{1,0:T(8,128)(2,1)S(1)} %collective-permute-done.2.rest_3_) | copy-start | bytes 1996804
  35.6 15.6 %collective-permute-start.6 = (bf16[520,640]{1,0:T(8,128)(2,1)}, bf16[520,640]{1,0:T(8,128)(2,1)S(1)}, u32[]{:S(2)}, u32[]{:S(2)}) collective-permute-start(bf16[520,640]{1,0:T(8,128)(2,1)} %collective-permute-done.3.rest_4_), channel_id=1, source_target_pairs={{0,2},{1,3},{4,0},{5,1},{8,4},{9,5},{12,8},{13,9},{14,12},{15,13},... | collective-permute-start | bytes 1996808 | tf_op jit(solution)/shard_map/ppermute | solution.py:472
  36.9 14.3 %collective-permute-start.5 = (bf16[520,640]{1,0:T(8,128)(2,1)S(1)}, bf16[520,640]{1,0:T(8,128)(2,1)S(1)}, u32[]{:S(2)}, u32[]{:S(2)}) collective-permute-start(bf16[520,640]{1,0:T(8,128)(2,1)S(1)} %collective-permute-done.2.rest_3_), channel_id=1, source_target_pairs={{0,4},{1,5},{4,8},{5,9},{8,12},{9,13},{12,14},{13,15},{14,10},{15,... | collective-permute-start | bytes 1996808 | tf_op jit(solution)/shard_map/ppermute | solution.py:472
  37.1 18.9 %collective-permute-start.7 = (bf16[144,768]{1,0:T(8,128)(2,1)}, bf16[144,768]{1,0:T(8,128)(2,1)}, u32[]{:S(2)}, u32[]{:S(2)}) collective-permute-start(bf16[144,768]{1,0:T(8,128)(2,1)} %get-tuple-element.64), channel_id=1, source_target_pairs={{0,4},{1,5},{4,8},{5,9},{8,12},{9,13},{12,14},{13,15},{14,10},{15,... | collective-permute-start | bytes 663560 | tf_op jit(solution)/shard_map/ppermute | solution.py:472
  37.9 18.1 %collective-permute-start.8 = (bf16[144,768]{1,0:T(8,128)(2,1)}, bf16[144,768]{1,0:T(8,128)(2,1)}, u32[]{:S(2)}, u32[]{:S(2)}) collective-permute-start(bf16[144,768]{1,0:T(8,128)(2,1)} %get-tuple-element.65), channel_id=1, source_target_pairs={{0,2},{1,3},{4,0},{5,1},{8,4},{9,5},{12,8},{13,9},{14,12},{15,13},... | collective-permute-start | bytes 663560 | tf_op jit(solution)/shard_map/ppermute | solution.py:472
  51.1 14.6 %copy-start.5 = (bf16[520,640]{1,0:T(8,128)(2,1)}, bf16[520,640]{1,0:T(8,128)(2,1)S(1)}, u32[]{:S(2)}) copy-start(bf16[520,640]{1,0:T(8,128)(2,1)S(1)} %collective-permute-done.6.rest_1_.rest_6_) | copy-start | bytes 1996804
  51.2 14.6 %copy-start.6 = (bf16[520,640]{1,0:T(8,128)(2,1)}, bf16[520,640]{1,0:T(8,128)(2,1)S(1)}, u32[]{:S(2)}) copy-start(bf16[520,640]{1,0:T(8,128)(2,1)S(1)} %collective-permute-done.5.rest_0_.rest_5_) | copy-start | bytes 1996804
  56.0 8.7 %collective-permute-start.10 = (bf16[264,640]{1,0:T(8,128)(2,1)S(1)}, bf16[264,640]{1,0:T(8,128)(2,1)S(1)}, u32[]{:S(2)}, u32[]{:S(2)}) collective-permute-start(bf16[264,640]{1,0:T(8,128)(2,1)S(1)} %slice.9), channel_id=1, source_target_pairs={{0,2},{1,3},{4,0},{5,1},{8,4},{9,5},{12,8},{13,9},{14,12},{15,13},... | collective-permute-start | bytes 1013768 | tf_op jit(solution)/shard_map/ppermute | solution.py:472
  57.2 6.2 %collective-permute-start.9 = (bf16[256,640]{1,0:T(8,128)(2,1)S(1)}, bf16[256,640]{1,0:T(8,128)(2,1)S(1)}, u32[]{:S(2)}, u32[]{:S(2)}) collective-permute-start(bf16[256,640]{1,0:T(8,128)(2,1)S(1)} %slice.8), channel_id=1, source_target_pairs={{0,4},{1,5},{4,8},{5,9},{8,12},{9,13},{12,14},{13,15},{14,10},{15,... | collective-permute-start | bytes 983048 | tf_op jit(solution)/shard_map/ppermute | solution.py:472
  57.4 17.2 %collective-permute-start.11 = (bf16[144,768]{1,0:T(8,128)(2,1)}, bf16[144,768]{1,0:T(8,128)(2,1)}, u32[]{:S(2)}, u32[]{:S(2)}) collective-permute-start(bf16[144,768]{1,0:T(8,128)(2,1)} %get-tuple-element.72), channel_id=1, source_target_pairs={{0,8},{1,9},{4,12},{5,13},{8,14},{9,15},{12,10},{13,11},{14,6},{15... | collective-permute-start | bytes 663560 | tf_op jit(solution)/shard_map/ppermute | solution.py:472
  58.0 16.7 %collective-permute-start.12 = (bf16[144,768]{1,0:T(8,128)(2,1)}, bf16[144,768]{1,0:T(8,128)(2,1)}, u32[]{:S(2)}, u32[]{:S(2)}) collective-permute-start(bf16[144,768]{1,0:T(8,128)(2,1)} %get-tuple-element.73), channel_id=1, source_target_pairs={{0,6},{1,7},{4,2},{5,3},{8,0},{9,1},{12,4},{13,5},{14,8},{15,9},{1... | collective-permute-start | bytes 663560 | tf_op jit(solution)/shard_map/ppermute | solution.py:472
  59.8 17.9 %collective-permute-start.13 = (bf16[144,768]{1,0:T(8,128)(2,1)}, bf16[144,768]{1,0:T(8,128)(2,1)}, u32[]{:S(2)}, u32[]{:S(2)}) collective-permute-start(bf16[144,768]{1,0:T(8,128)(2,1)} %get-tuple-element.74), channel_id=1, source_target_pairs={{0,12},{1,13},{4,14},{5,15},{8,10},{9,11},{12,6},{13,7},{14,2},{15... | collective-permute-start | bytes 663560 | tf_op jit(solution)/shard_map/ppermute | solution.py:472
  63.5 2.3 %copy-start.9 = (bf16[256,640]{1,0:T(8,128)(2,1)}, bf16[256,640]{1,0:T(8,128)(2,1)S(1)}, u32[]{:S(2)}) copy-start(bf16[256,640]{1,0:T(8,128)(2,1)S(1)} %collective-permute-done.9.rest_2_.rest_7_) | copy-start | bytes 983044
  63.5 26.4 %collective-permute-start.14 = (bf16[144,768]{1,0:T(8,128)(2,1)}, bf16[144,768]{1,0:T(8,128)(2,1)}, u32[]{:S(2)}, u32[]{:S(2)}) collective-permute-start(bf16[144,768]{1,0:T(8,128)(2,1)} %get-tuple-element.75), channel_id=1, source_target_pairs={{0,10},{1,11},{4,6},{5,7},{8,2},{9,3},{12,0},{13,1},{14,4},{15,5},... | collective-permute-start | bytes 663560 | tf_op jit(solution)/shard_map/ppermute | solution.py:472
  64.7 1.1 copy-start.8
  64.7 31.1 %collective-permute-start.15 = (bf16[144,768]{1,0:T(8,128)(2,1)}, bf16[144,768]{1,0:T(8,128)(2,1)}, u32[]{:S(2)}, u32[]{:S(2)}) collective-permute-start(bf16[144,768]{1,0:T(8,128)(2,1)} %get-tuple-element.76), channel_id=1, source_target_pairs={{0,14},{1,15},{4,10},{5,11},{8,6},{9,7},{12,2},{13,3},{14,0},{15,1... | collective-permute-start | bytes 663560 | tf_op jit(solution)/shard_map/ppermute | solution.py:472
  95.8 44.8 %all-to-all-start = ((bf16[8,144,768]{2,1,0:T(8,128)(2,1)}), bf16[8,144,768]{2,1,0:T(8,128)(2,1)S(1)}, u32[]{:S(2)}, u32[]{:S(2)}) async-start(bf16[8,144,768]{2,1,0:T(8,128)(2,1)} %upstream.3), calls=%async_computation | async-start | bytes 3538944 | tf_op jit(solution)/shard_map/all_to_all | solution.py:512
  100.3 18.0 %copy-start.15 = (bf16[128,6]{0,1:T(8,128)(2,1)S(1)}, bf16[128,6]{0,1:T(8,128)(2,1)}, u32[]{:S(2)}) copy-start(bf16[128,6]{0,1:T(8,128)(2,1)} %param.9) | copy-start | bytes 4612
  112.8 18.8 %collective-permute-start.16 = (bf16[192,2560]{1,0:T(8,128)(2,1)}, bf16[192,2560]{1,0:T(8,128)(2,1)}, u32[]{:S(2)}, u32[]{:S(2)}) collective-permute-start(bf16[192,2560]{1,0:T(8,128)(2,1)} %get-tuple-element.90), channel_id=1, source_target_pairs={{0,1},{1,0},{2,3},{3,2},{4,5},{5,4},{6,7},{7,6},{8,9},{9,8},{10,11... | collective-permute-start | bytes 2949128 | tf_op jit(solution)/shard_map/ppermute | solution.py:514
  117.7 13.9 %collective-permute-start.17 = (bf16[192,2560]{1,0:T(8,128)(2,1)}, bf16[192,2560]{1,0:T(8,128)(2,1)}, u32[]{:S(2)}, u32[]{:S(2)}) collective-permute-start(bf16[192,2560]{1,0:T(8,128)(2,1)} %get-tuple-element.91), channel_id=1, source_target_pairs={{0,1},{1,0},{2,3},{3,2},{4,5},{5,4},{6,7},{7,6},{8,9},{9,8},{10,11... | collective-permute-start | bytes 2949128 | tf_op jit(solution)/shard_map/ppermute | solution.py:514
  117.8 13.8 %collective-permute-start.18 = (bf16[192,2560]{1,0:T(8,128)(2,1)}, bf16[192,2560]{1,0:T(8,128)(2,1)}, u32[]{:S(2)}, u32[]{:S(2)}) collective-permute-start(bf16[192,2560]{1,0:T(8,128)(2,1)} %get-tuple-element.92), channel_id=1, source_target_pairs={{0,1},{1,0},{2,3},{3,2},{4,5},{5,4},{6,7},{7,6},{8,9},{9,8},{10,11... | collective-permute-start | bytes 2949128 | tf_op jit(solution)/shard_map/ppermute | solution.py:514
  118.2 13.4 %collective-permute-start.19 = (bf16[192,2560]{1,0:T(8,128)(2,1)}, bf16[192,2560]{1,0:T(8,128)(2,1)}, u32[]{:S(2)}, u32[]{:S(2)}) collective-permute-start(bf16[192,2560]{1,0:T(8,128)(2,1)} %get-tuple-element.93), channel_id=1, source_target_pairs={{0,1},{1,0},{2,3},{3,2},{4,5},{5,4},{6,7},{7,6},{8,9},{9,8},{10,11... | collective-permute-start | bytes 2949128 | tf_op jit(solution)/shard_map/ppermute | solution.py:514
  131.6 1.2 copy-start
  132.8 1.2 copy-start.1
  134.0 1.2 copy-start.2
  135.2 1.2 copy-start.3
  136.4 4.0 %copy-start.13 = (s32[6,128]{1,0:T(8,128)S(1)}, s32[6,128]{1,0:T(8,128)}, u32[]{:S(2)}) copy-start(s32[6,128]{1,0:T(8,128)} %get-tuple-element.94) | copy-start | bytes 9220
  136.4 4.1 %copy-start.4 = (bf16[128,6,768]{2,0,1:T(8,128)(2,1)S(1)}, bf16[128,6,768]{2,0,1:T(8,128)(2,1)}, u32[]{:S(2)}) copy-start(bf16[128,6,768]{2,0,1:T(8,128)(2,1)} %param.7) | copy-start | bytes 3538948

commit v7 on v6

--- a/solution.py
+++ b/solution.py
@@ -357,7 +357,7 @@
     for copy in grad_loads:
         copy.wait()
     width = grads.shape[1]
-    step = 512
+    step = 1280
 
     @pl.loop(0, width // step)
     def _(n):
@@ -436,11 +436,18 @@
             (place_ref[:, k : k + 1] == lane).astype(F32).astype(BF16)
         )
     sums[...] = jnp.zeros_like(sums)
-    up = jnp.dot(select[...], back_ref[...], preferred_element_type=F32)
+    step = 256
+    totals = [0.0] * top_count
+    for first in range(0, back_ref.shape[1], step):
+        units = slice(first, first + step)
+        up = jnp.dot(select[...], back_ref[:, units], preferred_element_type=F32)
+        for k in range(top_count):
+            mine = up[k * tokens : (k + 1) * tokens, :]
+            grad_ref[k, :, units] = (gates_ref[:, k : k + 1].astype(F32) * mine).astype(BF16)
+            products = hidden_ref[k, :, units].astype(F32) * mine
+            totals[k] = totals[k] + jnp.sum(products, axis=1, keepdims=True)
     for k in range(top_count):
-        mine = up[k * tokens : (k + 1) * tokens, :]
-        grad_ref[k] = (gates_ref[:, k : k + 1].astype(F32) * mine).astype(BF16)
-        sums[:, k : k + 1] = jnp.sum(hidden_ref[k].astype(F32) * mine, axis=1, keepdims=True)
+        sums[:, k : k + 1] = totals[k]
     gate_ref[...] = sums[...].T[:top_count, :].astype(BF16)
 
 
@@ -459,7 +466,7 @@
             pltpu.VMEM((top_count * tokens, rows), BF16),
             pltpu.VMEM((tokens, 128), F32),
         ],
-        compiler_params=pltpu.CompilerParams(vmem_limit_bytes=24 * 1024 * 1024),
+        compiler_params=pltpu.CompilerParams(vmem_limit_bytes=16 * 1024 * 1024),
         cost_estimate=pl.CostEstimate(
             flops=UNPACK_FLOPS, bytes_accessed=6 * rows * hidden_units, transcendentals=0
         ),
@@ -505,7 +512,7 @@
         (ahead[:cut], behind[cut:], hidden[1], hidden[2], up)
     )
     pieces += [send(ahead, 1), send(behind, -1)]
-    send_hidden(5, 6, 7, 3, 4)
+    send_hidden(7, 5, 6, 3, 4)
     up = upstream_of(OFFSETS[5:], pieces[5:], (up,))
     *hidden, up = barrier((*hidden, up))
     groups = [[ring_device(p, core) for p in range(RING)] for core in range(2)]

time: 145 us -> 145 us (level)
  no operation moved by 1% of the time
where the time goes in v7:
time: 145 us; the launch traced here: 143 us
  Pallas kernels  57 us (39%)
  waiting for transfers between devices  53.6 us (37%)
  starting transfers between devices  23.5 us (16%)
  local copies, waits for them, and re-layouts  6.89 us (5%)
  between operations  1.56 us (1%)
    ppermute x15, waiting for transfers between devices, send(): return lax.ppermute(value, 'expert', ring_shift(step))  53.6 us
    pallas_call x2, Pallas kernels, ring_weight_sum(): pl.pallas_call(functools.partial(ring_weight_kernel, capacity, other, len...  24 us
    pallas_call x2, Pallas kernels, ring_upstream(): pl.pallas_call(functools.partial(ring_upstream_kernel, capacity, offsets,...  21.4 us
    ppermute x15, starting transfers between devices, send(): return lax.ppermute(value, 'expert', ring_shift(step))  12.8 us
    ppermute x4, starting transfers between devices, ring_exchange(): came = [lax.ppermute(part, 'expert', SWAP) for part in theirs]  5.47 us
    unnamed x33, local copies, waits for them, and re-layouts  4.98 us
    all_to_all x1, starting transfers between devices, ring_exchange(): lax.all_to_all(up, 'expert', 0, 0, axis_index_groups=groups, tiled=True)  4.55 us
    pallas_call x1, Pallas kernels, ring_pack(): pl.pallas_call(functools.partial(ring_pack_kernel, capacity), out_shape=(...  4.54 us
  transfers between devices with their start and end apart: 21, of which 7 were waited for; matrix products, arithmetic and copies ran while one was open for 1% of the time, Pallas kernels for 38%

profile of v7, /device:TPU:13, one launch (start us, length us, event | category | flops | bytes accessed | tf_op | source)
XLA Modules:
  0.0 142.6 jit_solution(1055078997155577816)
XLA Ops:
  0.6 0.0 copy-start.14
  0.6 0.7 collective-permute-start.4
  1.4 1.7 %reshape.15 = bf16[2,64,4,640]{3,2,1,0:T(4,128)(2,1)S(1)} reshape(bf16[128,2560]{1,0:T(8,128)(2,1)} %param.6) | data formatting | bytes 1310720 | tf_op jit(solution)/shard_map/reshape | solution.py:485
  3.0 0.1 copy.10
  3.1 0.1 fusion.1.rest_0_
  3.2 0.2 collective-permute-start
  3.4 1.3 collective-permute-start.1
  4.7 4.5 %pack.1 = (bf16[144,768]{1,0:T(8,128)(2,1)}, bf16[144,768]{1,0:T(8,128)(2,1)}, bf16[144,768]{1,0:T(8,128)(2,1)}, bf16[144,768]{1,0:T(8,128)(2,1)}, bf16[144,768]...) custom-call(s32[1]{0:T(128)} %bitcast.me_ref, ...), custom_call_target="tpu_custom_call" | custom-call | flops 3000000000 | bytes 5000000 | tf_op jit(solution)/shard_map/pack/pallas_call | solution.py:210
  9.3 10.5 %collective-permute-done.rest_1_ = bf16[520,640]{1,0:T(8,128)(2,1)S(1)} collective-permute-done((bf16[520,640]{1,0:T(8,128)(2,1)S(1)}, bf16[520,640]{1,0:T(8,128)(2,1)S(1)}, u32[]{:S(2)}, u32[]{:S(2)}) %collective-permute-start) | collective-permute-done | bytes 665632 | tf_op jit(solution)/shard_map/ppermute | solution.py:479
  19.8 0.0 collective-permute-done.1.rest_2_
  19.8 0.2 collective-permute-start.2
  20.1 1.3 collective-permute-start.3
  21.4 14.2 %collective-permute-done.2.rest_3_ = bf16[520,640]{1,0:T(8,128)(2,1)S(1)} collective-permute-done((bf16[520,640]{1,0:T(8,128)(2,1)S(1)}, bf16[520,640]{1,0:T(8,128)(2,1)S(1)}, u32[]{:S(2)}, u32[]{:S(2)}) %collective-permute-start.2) | collective-permute-done | bytes 665632 | tf_op jit(solution)/shard_map/ppermute | solution.py:479
  35.5 0.0 collective-permute-done.3.rest_4_
  35.5 0.0 collective-permute-done.4.other_ref
  35.6 1.4 collective-permute-start.6
  36.9 0.2 collective-permute-start.5
  37.1 0.8 collective-permute-start.7
  37.9 0.7 collective-permute-start.8
  38.6 0.0 copy-done.12
  38.6 12.6 %upstream.2.rest_4_ = bf16[8,144,768]{2,1,0:T(8,128)(2,1)} custom-call(s32[1]{0:T(128)} %bitcast.me_ref, bf16[768,2560]{1,0:T(8,128)(2,1)} %bitcast.19, bf16[768,2560]{1,0:T(8,128)(2,1)} %collective-permute-done.4.other_ref, bf16[520,640]{1,0:T(8,128)(2,1)} %copy-done.7, bf16[520,640]{1,0:T(8,128)(2,1)} %copy-done.10, bf16[520,640]{1,0:T(8,128)(2,1)} %copy-done.11, ...), custom_call_target="tpu_custom_call" | custom-call | flops 5033164800 | bytes 11141120 | tf_op jit(solution)/shard_map/upstream/pallas_call | solution.py:311
  51.1 0.0 collective-permute-done.6.rest_1_.rest_6_
  51.2 0.0 collective-permute-done.5.rest_0_.rest_5_
  51.2 4.7 %collective-permute-done.7.rest_10_ = bf16[144,768]{1,0:T(8,128)(2,1)} collective-permute-done((bf16[144,768]{1,0:T(8,128)(2,1)}, bf16[144,768]{1,0:T(8,128)(2,1)}, u32[]{:S(2)}, u32[]{:S(2)}) %collective-permute-start.7) | collective-permute-done | bytes 221216 | tf_op jit(solution)/shard_map/ppermute | solution.py:479
  56.0 0.0 collective-permute-done.8.rest_11_
  56.0 1.3 collective-permute-start.10
  57.2 0.2 collective-permute-start.9
  57.4 0.5 collective-permute-start.11
  58.0 1.8 %collective-permute-start.12 = (bf16[144,768]{1,0:T(8,128)(2,1)}, bf16[144,768]{1,0:T(8,128)(2,1)}, u32[]{:S(2)}, u32[]{:S(2)}) collective-permute-start(bf16[144,768]{1,0:T(8,128)(2,1)} %get-tuple-element.73), channel_id=1, source_target_pairs={{0,6},{1,7},{4,2},{5,3},{8,0},{9,1},{12,4},{13,5},{14,8},{15,9},{1... | collective-permute-start | bytes 663560 | tf_op jit(solution)/shard_map/ppermute | solution.py:479
  59.8 0.6 collective-permute-start.13
  60.4 3.0 %collective-permute-done.9.rest_2_.rest_7_ = bf16[256,640]{1,0:T(8,128)(2,1)S(1)} collective-permute-done((bf16[256,640]{1,0:T(8,128)(2,1)S(1)}, bf16[256,640]{1,0:T(8,128)(2,1)S(1)}, u32[]{:S(2)}, u32[]{:S(2)}) %collective-permute-start.9) | collective-permute-done | bytes 327712 | tf_op jit(solution)/shard_map/ppermute | solution.py:479
  63.5 1.2 collective-permute-start.14
  64.7 0.0 collective-permute-done.10.rest_3_.rest_8_
  64.7 1.1 collective-permute-start.15
  65.7 0.0 copy-done.5
  65.8 8.9 %upstream.3 = bf16[8,144,768]{2,1,0:T(8,128)(2,1)} custom-call(s32[1]{0:T(128)} %bitcast.me_ref, bf16[768,2560]{1,0:T(8,128)(2,1)} %bitcast.20, bf16[768,2560]{1,0:T(8,128)(2,1)} %collective-permute-done.4.other_ref, bf16[520,640]{1,0:T(8,128)(2,1)} %copy-done.6, bf16[520,640]{1,0:T(8,128)(2,1)} %copy-done.5, ...), custom_call_target="tpu_custom_call", output_to_operand_aliasing={{}: (7, {})} | custom-call | flops 3019898880 | bytes 9830400 | tf_op jit(solution)/shard_map/upstream/pallas_call | solution.py:311
  74.6 0.0 collective-permute-done.11.rest_12_
  74.6 0.0 collective-permute-done.12.rest_13_
  74.7 3.0 %collective-permute-done.13.rest_14_ = bf16[144,768]{1,0:T(8,128)(2,1)} collective-permute-done((bf16[144,768]{1,0:T(8,128)(2,1)}, bf16[144,768]{1,0:T(8,128)(2,1)}, u32[]{:S(2)}, u32[]{:S(2)}) %collective-permute-start.13) | collective-permute-done | bytes 221216 | tf_op jit(solution)/shard_map/ppermute | solution.py:479
  77.7 12.1 %collective-permute-done.14.rest_15_ = bf16[144,768]{1,0:T(8,128)(2,1)} collective-permute-done((bf16[144,768]{1,0:T(8,128)(2,1)}, bf16[144,768]{1,0:T(8,128)(2,1)}, u32[]{:S(2)}, u32[]{:S(2)}) %collective-permute-start.14) | collective-permute-done | bytes 221216 | tf_op jit(solution)/shard_map/ppermute | solution.py:479
  89.8 5.9 %collective-permute-done.15.rest_16_ = bf16[144,768]{1,0:T(8,128)(2,1)} collective-permute-done((bf16[144,768]{1,0:T(8,128)(2,1)}, bf16[144,768]{1,0:T(8,128)(2,1)}, u32[]{:S(2)}, u32[]{:S(2)}) %collective-permute-start.15) | collective-permute-done | bytes 221216 | tf_op jit(solution)/shard_map/ppermute | solution.py:479
  95.8 4.5 %all-to-all-start = ((bf16[8,144,768]{2,1,0:T(8,128)(2,1)}), bf16[8,144,768]{2,1,0:T(8,128)(2,1)S(1)}, u32[]{:S(2)}, u32[]{:S(2)}) async-start(bf16[8,144,768]{2,1,0:T(8,128)(2,1)} %upstream.3), calls=%async_computation | async-start | bytes 3538944 | tf_op jit(solution)/shard_map/all_to_all | solution.py:519
  100.3 12.0 %weight_other.1 = (bf16[192,2560]{1,0:T(8,128)(2,1)}, bf16[192,2560]{1,0:T(8,128)(2,1)}, bf16[192,2560]{1,0:T(8,128)(2,1)}, bf16[192,2560]{1,0:T(8,128)(2,1)}) custom-call(s32[1]{0:T(128)} %bitcast.me_ref, bf16[520,640]{1,0:T(8,128)(2,1)} %copy-done.7, bf16[520,640]{1,0:T(8,128)(2,1)} %copy-done.10, bf16[520,640]{1,0:T(8,128)(2,1)} %copy-done.11, ...), custom_call_target="tpu_custom_call" | custom-call | flops 1000000 | bytes 1000000 | tf_op jit(solution)/shard_map/weight_other/pallas_call | solution.py:375
  112.3 4.9 %collective-permute-start.16 = (bf16[192,2560]{1,0:T(8,128)(2,1)}, bf16[192,2560]{1,0:T(8,128)(2,1)}, u32[]{:S(2)}, u32[]{:S(2)}) collective-permute-start(bf16[192,2560]{1,0:T(8,128)(2,1)} %get-tuple-element.90), channel_id=1, source_target_pairs={{0,1},{1,0},{2,3},{3,2},{4,5},{5,4},{6,7},{7,6},{8,9},{9,8},{10,11... | collective-permute-start | bytes 2949128 | tf_op jit(solution)/shard_map/ppermute | solution.py:521
  117.2 0.1 collective-permute-start.17
  117.3 0.4 collective-permute-start.18
  117.7 0.1 collective-permute-start.19
  117.8 0.0 copy-done.15
  117.8 0.1 copy.12.gates_ref
  118.6 12.0 %weight_own.1 = (bf16[192,2560]{1,0:T(8,128)(2,1)}, bf16[192,2560]{1,0:T(8,128)(2,1)}, bf16[192,2560]{1,0:T(8,128)(2,1)}, bf16[192,2560]{1,0:T(8,128)(2,1)}) custom-call(s32[1]{0:T(128)} %bitcast.me_ref, bf16[520,640]{1,0:T(8,128)(2,1)} %copy-done.7, bf16[520,640]{1,0:T(8,128)(2,1)} %copy-done.10, bf16[520,640]{1,0:T(8,128)(2,1)} %copy-done.11, ...), custom_call_target="tpu_custom_call" | custom-call | flops 1000000 | bytes 1000000 | tf_op jit(solution)/shard_map/weight_own/pallas_call | solution.py:375
  130.6 0.0 collective-permute-done.16.rest_4_
  130.6 0.0 collective-permute-done.17.rest_5_
  130.6 0.0 collective-permute-done.18.rest_6_
  130.6 0.0 collective-permute-done.19.rest_7_
  130.6 0.0 copy-start
  130.6 1.2 copy-done
  131.8 1.2 copy-done.1
  133.0 1.2 copy-done.2
  134.2 1.2 copy-done.3
  135.4 4.0 %weight_add.1 = bf16[768,2560]{1,0:T(8,128)(2,1)} custom-call(s32[1]{0:T(128)S(6)} %copy.14.trained_ref, bf16[192,2560]{1,0:T(8,128)(2,1)S(1)} %copy-done, bf16[192,2560]{1,0:T(8,128)(2,1)S(1)} %copy-done.1, bf16[192,2560]{1,0:T(8,128)(2,1)S(1)} %copy-done.2, bf16[192,2560]{1,0:T(8,128)(2,1)S(1)} %copy-done.3, ...), custom_call_target="tpu_custom_call" | custom-call | flops 1000000 | bytes 1000000 | tf_op jit(solution)/shard_map/weight_add/pallas_call | solution.py:417
  139.4 0.0 copy-done.13
  139.4 0.1 copy.11
  139.5 0.0 all-to-all-done
  139.5 3.1 %unpack.1 = (bf16[6,128,768]{2,1,0:T(8,128)(2,1)}, bf16[6,128]{1,0:T(8,128)(2,1)}) custom-call(s32[128,6]{1,0:T(8,128)S(1)} %bitcast.15, bf16[128,6]{1,0:T(8,128)(2,1)S(1)} %copy.12.gates_ref, bf16[6,128,768]{2,1,0:T(8,128)(2,1)S(1)} %bitcast.17, bf16[1152,768]{1,0:T(8,128)(2,1)S(1)} %bitcast.14), custom_call_target="tpu_custom_call" | custom-call | flops 40000000000 | bytes 5308416 | tf_op jit(solution)/shard_map/unpack/pallas_call | solution.py:457
  (25 shorter events, 0.1 us)
Async XLA Ops:
  0.6 2.5 %copy-start.14 = (s32[128,6]{0,1:T(8,128)S(1)}, s32[128,6]{0,1:T(8,128)}, u32[]{:S(2)}) copy-start(s32[128,6]{0,1:T(8,128)} %param.8) | copy-start | bytes 9220
  0.6 34.9 %collective-permute-start.4 = (bf16[768,2560]{1,0:T(8,128)(2,1)}, bf16[768,2560]{1,0:T(8,128)(2,1)}, u32[]{:S(2)}, u32[]{:S(2)}) collective-permute-start(bf16[768,2560]{1,0:T(8,128)(2,1)} %bitcast.18), channel_id=1, source_target_pairs={{0,1},{1,0},{2,3},{3,2},{4,5},{5,4},{6,7},{7,6},{8,9},{9,8},{10,11... | collective-permute-start | bytes 11796488 | tf_op jit(solution)/shard_map/ppermute | solution.py:489
  3.2 6.1 %copy-start.7 = (bf16[520,640]{1,0:T(8,128)(2,1)}, bf16[520,640]{1,0:T(8,128)(2,1)S(1)}, u32[]{:S(2)}) copy-start(bf16[520,640]{1,0:T(8,128)(2,1)S(1)} %fusion.1.rest_0_) | copy-start | bytes 1996804
  3.2 16.6 %collective-permute-start = (bf16[520,640]{1,0:T(8,128)(2,1)S(1)}, bf16[520,640]{1,0:T(8,128)(2,1)S(1)}, u32[]{:S(2)}, u32[]{:S(2)}) collective-permute-start(bf16[520,640]{1,0:T(8,128)(2,1)S(1)} %fusion.1.rest_0_), channel_id=1, source_target_pairs={{0,4},{1,5},{4,8},{5,9},{8,12},{9,13},{12,14},{13,15},{14,10},{15,... | collective-permute-start | bytes 1996808 | tf_op jit(solution)/shard_map/ppermute | solution.py:479
  3.4 16.4 %collective-permute-start.1 = (bf16[520,640]{1,0:T(8,128)(2,1)S(1)}, bf16[520,640]{1,0:T(8,128)(2,1)S(1)}, u32[]{:S(2)}, u32[]{:S(2)}) collective-permute-start(bf16[520,640]{1,0:T(8,128)(2,1)S(1)} %fusion.1.rest_0_), channel_id=1, source_target_pairs={{0,2},{1,3},{4,0},{5,1},{8,4},{9,5},{12,8},{13,9},{14,12},{15,13},... | collective-permute-start | bytes 1996808 | tf_op jit(solution)/shard_map/ppermute | solution.py:479
  19.8 15.7 %copy-start.10 = (bf16[520,640]{1,0:T(8,128)(2,1)}, bf16[520,640]{1,0:T(8,128)(2,1)S(1)}, u32[]{:S(2)}) copy-start(bf16[520,640]{1,0:T(8,128)(2,1)S(1)} %collective-permute-done.rest_1_) | copy-start | bytes 1996804
  19.8 15.7 %copy-start.11 = (bf16[520,640]{1,0:T(8,128)(2,1)}, bf16[520,640]{1,0:T(8,128)(2,1)S(1)}, u32[]{:S(2)}) copy-start(bf16[520,640]{1,0:T(8,128)(2,1)S(1)} %collective-permute-done.1.rest_2_) | copy-start | bytes 1996804
  19.8 15.7 %collective-permute-start.2 = (bf16[520,640]{1,0:T(8,128)(2,1)S(1)}, bf16[520,640]{1,0:T(8,128)(2,1)S(1)}, u32[]{:S(2)}, u32[]{:S(2)}) collective-permute-start(bf16[520,640]{1,0:T(8,128)(2,1)S(1)} %collective-permute-done.rest_1_), channel_id=1, source_target_pairs={{0,4},{1,5},{4,8},{5,9},{8,12},{9,13},{12,14},{13,15},{14,10},{15,... | collective-permute-start | bytes 1996808 | tf_op jit(solution)/shard_map/ppermute | solution.py:479
  20.1 15.5 %collective-permute-start.3 = (bf16[520,640]{1,0:T(8,128)(2,1)S(1)}, bf16[520,640]{1,0:T(8,128)(2,1)}, u32[]{:S(2)}, u32[]{:S(2)}) collective-permute-start(bf16[520,640]{1,0:T(8,128)(2,1)S(1)} %collective-permute-done.1.rest_2_), channel_id=1, source_target_pairs={{0,2},{1,3},{4,0},{5,1},{8,4},{9,5},{12,8},{13,9},{14,12},{15,13},... | collective-permute-start | bytes 1996808 | tf_op jit(solution)/shard_map/ppermute | solution.py:479
  35.5 3.0 %copy-start.12 = (bf16[520,640]{1,0:T(8,128)(2,1)}, bf16[520,640]{1,0:T(8,128)(2,1)S(1)}, u32[]{:S(2)}) copy-start(bf16[520,640]{1,0:T(8,128)(2,1)S(1)} %collective-permute-done.2.rest_3_) | copy-start | bytes 1996804
  35.6 15.6 %collective-permute-start.6 = (bf16[520,640]{1,0:T(8,128)(2,1)}, bf16[520,640]{1,0:T(8,128)(2,1)S(1)}, u32[]{:S(2)}, u32[]{:S(2)}) collective-permute-start(bf16[520,640]{1,0:T(8,128)(2,1)} %collective-permute-done.3.rest_4_), channel_id=1, source_target_pairs={{0,2},{1,3},{4,0},{5,1},{8,4},{9,5},{12,8},{13,9},{14,12},{15,13},... | collective-permute-start | bytes 1996808 | tf_op jit(solution)/shard_map/ppermute | solution.py:479
  36.9 14.3 %collective-permute-start.5 = (bf16[520,640]{1,0:T(8,128)(2,1)S(1)}, bf16[520,640]{1,0:T(8,128)(2,1)S(1)}, u32[]{:S(2)}, u32[]{:S(2)}) collective-permute-start(bf16[520,640]{1,0:T(8,128)(2,1)S(1)} %collective-permute-done.2.rest_3_), channel_id=1, source_target_pairs={{0,4},{1,5},{4,8},{5,9},{8,12},{9,13},{12,14},{13,15},{14,10},{15,... | collective-permute-start | bytes 1996808 | tf_op jit(solution)/shard_map/ppermute | solution.py:479
  37.1 18.9 %collective-permute-start.7 = (bf16[144,768]{1,0:T(8,128)(2,1)}, bf16[144,768]{1,0:T(8,128)(2,1)}, u32[]{:S(2)}, u32[]{:S(2)}) collective-permute-start(bf16[144,768]{1,0:T(8,128)(2,1)} %get-tuple-element.64), channel_id=1, source_target_pairs={{0,4},{1,5},{4,8},{5,9},{8,12},{9,13},{12,14},{13,15},{14,10},{15,... | collective-permute-start | bytes 663560 | tf_op jit(solution)/shard_map/ppermute | solution.py:479
  37.9 18.1 %collective-permute-start.8 = (bf16[144,768]{1,0:T(8,128)(2,1)}, bf16[144,768]{1,0:T(8,128)(2,1)}, u32[]{:S(2)}, u32[]{:S(2)}) collective-permute-start(bf16[144,768]{1,0:T(8,128)(2,1)} %get-tuple-element.65), channel_id=1, source_target_pairs={{0,2},{1,3},{4,0},{5,1},{8,4},{9,5},{12,8},{13,9},{14,12},{15,13},... | collective-permute-start | bytes 663560 | tf_op jit(solution)/shard_map/ppermute | solution.py:479
  51.1 14.6 %copy-start.5 = (bf16[520,640]{1,0:T(8,128)(2,1)}, bf16[520,640]{1,0:T(8,128)(2,1)S(1)}, u32[]{:S(2)}) copy-start(bf16[520,640]{1,0:T(8,128)(2,1)S(1)} %collective-permute-done.6.rest_1_.rest_6_) | copy-start | bytes 1996804
  51.2 14.6 %copy-start.6 = (bf16[520,640]{1,0:T(8,128)(2,1)}, bf16[520,640]{1,0:T(8,128)(2,1)S(1)}, u32[]{:S(2)}) copy-start(bf16[520,640]{1,0:T(8,128)(2,1)S(1)} %collective-permute-done.5.rest_0_.rest_5_) | copy-start | bytes 1996804
  56.0 8.7 %collective-permute-start.10 = (bf16[264,640]{1,0:T(8,128)(2,1)S(1)}, bf16[264,640]{1,0:T(8,128)(2,1)S(1)}, u32[]{:S(2)}, u32[]{:S(2)}) collective-permute-start(bf16[264,640]{1,0:T(8,128)(2,1)S(1)} %slice.9), channel_id=1, source_target_pairs={{0,2},{1,3},{4,0},{5,1},{8,4},{9,5},{12,8},{13,9},{14,12},{15,13},... | collective-permute-start | bytes 1013768 | tf_op jit(solution)/shard_map/ppermute | solution.py:479
  57.2 6.2 %collective-permute-start.9 = (bf16[256,640]{1,0:T(8,128)(2,1)S(1)}, bf16[256,640]{1,0:T(8,128)(2,1)S(1)}, u32[]{:S(2)}, u32[]{:S(2)}) collective-permute-start(bf16[256,640]{1,0:T(8,128)(2,1)S(1)} %slice.8), channel_id=1, source_target_pairs={{0,4},{1,5},{4,8},{5,9},{8,12},{9,13},{12,14},{13,15},{14,10},{15,... | collective-permute-start | bytes 983048 | tf_op jit(solution)/shard_map/ppermute | solution.py:479
  57.4 17.2 %collective-permute-start.11 = (bf16[144,768]{1,0:T(8,128)(2,1)}, bf16[144,768]{1,0:T(8,128)(2,1)}, u32[]{:S(2)}, u32[]{:S(2)}) collective-permute-start(bf16[144,768]{1,0:T(8,128)(2,1)} %get-tuple-element.72), channel_id=1, source_target_pairs={{0,8},{1,9},{4,12},{5,13},{8,14},{9,15},{12,10},{13,11},{14,6},{15... | collective-permute-start | bytes 663560 | tf_op jit(solution)/shard_map/ppermute | solution.py:479
  58.0 16.7 %collective-permute-start.12 = (bf16[144,768]{1,0:T(8,128)(2,1)}, bf16[144,768]{1,0:T(8,128)(2,1)}, u32[]{:S(2)}, u32[]{:S(2)}) collective-permute-start(bf16[144,768]{1,0:T(8,128)(2,1)} %get-tuple-element.73), channel_id=1, source_target_pairs={{0,6},{1,7},{4,2},{5,3},{8,0},{9,1},{12,4},{13,5},{14,8},{15,9},{1... | collective-permute-start | bytes 663560 | tf_op jit(solution)/shard_map/ppermute | solution.py:479
  59.8 17.9 %collective-permute-start.13 = (bf16[144,768]{1,0:T(8,128)(2,1)}, bf16[144,768]{1,0:T(8,128)(2,1)}, u32[]{:S(2)}, u32[]{:S(2)}) collective-permute-start(bf16[144,768]{1,0:T(8,128)(2,1)} %get-tuple-element.74), channel_id=1, source_target_pairs={{0,12},{1,13},{4,14},{5,15},{8,10},{9,11},{12,6},{13,7},{14,2},{15... | collective-permute-start | bytes 663560 | tf_op jit(solution)/shard_map/ppermute | solution.py:479
  63.5 2.3 %copy-start.9 = (bf16[256,640]{1,0:T(8,128)(2,1)}, bf16[256,640]{1,0:T(8,128)(2,1)S(1)}, u32[]{:S(2)}) copy-start(bf16[256,640]{1,0:T(8,128)(2,1)S(1)} %collective-permute-done.9.rest_2_.rest_7_) | copy-start | bytes 983044
  63.5 26.4 %collective-permute-start.14 = (bf16[144,768]{1,0:T(8,128)(2,1)}, bf16[144,768]{1,0:T(8,128)(2,1)}, u32[]{:S(2)}, u32[]{:S(2)}) collective-permute-start(bf16[144,768]{1,0:T(8,128)(2,1)} %get-tuple-element.75), channel_id=1, source_target_pairs={{0,10},{1,11},{4,6},{5,7},{8,2},{9,3},{12,0},{13,1},{14,4},{15,5},... | collective-permute-start | bytes 663560 | tf_op jit(solution)/shard_map/ppermute | solution.py:479
  64.7 1.1 copy-start.8
  64.7 31.1 %collective-permute-start.15 = (bf16[144,768]{1,0:T(8,128)(2,1)}, bf16[144,768]{1,0:T(8,128)(2,1)}, u32[]{:S(2)}, u32[]{:S(2)}) collective-permute-start(bf16[144,768]{1,0:T(8,128)(2,1)} %get-tuple-element.76), channel_id=1, source_target_pairs={{0,14},{1,15},{4,10},{5,11},{8,6},{9,7},{12,2},{13,3},{14,0},{15,1... | collective-permute-start | bytes 663560 | tf_op jit(solution)/shard_map/ppermute | solution.py:479
  95.8 43.8 %all-to-all-start = ((bf16[8,144,768]{2,1,0:T(8,128)(2,1)}), bf16[8,144,768]{2,1,0:T(8,128)(2,1)S(1)}, u32[]{:S(2)}, u32[]{:S(2)}) async-start(bf16[8,144,768]{2,1,0:T(8,128)(2,1)} %upstream.3), calls=%async_computation | async-start | bytes 3538944 | tf_op jit(solution)/shard_map/all_to_all | solution.py:519
  100.3 17.5 %copy-start.15 = (bf16[128,6]{0,1:T(8,128)(2,1)S(1)}, bf16[128,6]{0,1:T(8,128)(2,1)}, u32[]{:S(2)}) copy-start(bf16[128,6]{0,1:T(8,128)(2,1)} %param.9) | copy-start | bytes 4612
  112.3 18.3 %collective-permute-start.16 = (bf16[192,2560]{1,0:T(8,128)(2,1)}, bf16[192,2560]{1,0:T(8,128)(2,1)}, u32[]{:S(2)}, u32[]{:S(2)}) collective-permute-start(bf16[192,2560]{1,0:T(8,128)(2,1)} %get-tuple-element.90), channel_id=1, source_target_pairs={{0,1},{1,0},{2,3},{3,2},{4,5},{5,4},{6,7},{7,6},{8,9},{9,8},{10,11... | collective-permute-start | bytes 2949128 | tf_op jit(solution)/shard_map/ppermute | solution.py:521
  117.2 13.4 %collective-permute-start.17 = (bf16[192,2560]{1,0:T(8,128)(2,1)}, bf16[192,2560]{1,0:T(8,128)(2,1)}, u32[]{:S(2)}, u32[]{:S(2)}) collective-permute-start(bf16[192,2560]{1,0:T(8,128)(2,1)} %get-tuple-element.91), channel_id=1, source_target_pairs={{0,1},{1,0},{2,3},{3,2},{4,5},{5,4},{6,7},{7,6},{8,9},{9,8},{10,11... | collective-permute-start | bytes 2949128 | tf_op jit(solution)/shard_map/ppermute | solution.py:521
  117.3 13.3 %collective-permute-start.18 = (bf16[192,2560]{1,0:T(8,128)(2,1)}, bf16[192,2560]{1,0:T(8,128)(2,1)}, u32[]{:S(2)}, u32[]{:S(2)}) collective-permute-start(bf16[192,2560]{1,0:T(8,128)(2,1)} %get-tuple-element.92), channel_id=1, source_target_pairs={{0,1},{1,0},{2,3},{3,2},{4,5},{5,4},{6,7},{7,6},{8,9},{9,8},{10,11... | collective-permute-start | bytes 2949128 | tf_op jit(solution)/shard_map/ppermute | solution.py:521
  117.7 12.9 %collective-permute-start.19 = (bf16[192,2560]{1,0:T(8,128)(2,1)}, bf16[192,2560]{1,0:T(8,128)(2,1)}, u32[]{:S(2)}, u32[]{:S(2)}) collective-permute-start(bf16[192,2560]{1,0:T(8,128)(2,1)} %get-tuple-element.93), channel_id=1, source_target_pairs={{0,1},{1,0},{2,3},{3,2},{4,5},{5,4},{6,7},{7,6},{8,9},{9,8},{10,11... | collective-permute-start | bytes 2949128 | tf_op jit(solution)/shard_map/ppermute | solution.py:521
  130.6 1.2 copy-start
  131.8 1.2 copy-start.1
  133.0 1.2 copy-start.2
  134.2 1.2 copy-start.3
  135.4 4.0 %copy-start.13 = (s32[6,128]{1,0:T(8,128)S(1)}, s32[6,128]{1,0:T(8,128)}, u32[]{:S(2)}) copy-start(s32[6,128]{1,0:T(8,128)} %get-tuple-element.94) | copy-start | bytes 9220
  135.4 4.1 %copy-start.4 = (bf16[128,6,768]{2,0,1:T(8,128)(2,1)S(1)}, bf16[128,6,768]{2,0,1:T(8,128)(2,1)}, u32[]{:S(2)}) copy-start(bf16[128,6,768]{2,0,1:T(8,128)(2,1)} %param.7) | copy-start | bytes 3538948
